TPU v7x, 32 devices: a whole 2x2x4 slice. The times are simulated.
32 devices in a mesh: dp: 16 (over z, x, core), mp: 2 (over y).
Axes of the slice: x: 2, y: 2, z: 4, core: 2. Of those that a mesh axis runs over, the one named last changes fastest.
Arguments:
- attn_out: bfloat16 [3072, 1536], P('dp', 'mp'), may hold values from -6 to 6
- residual: bfloat16 [3072, 1536], P('dp', 'mp')
- out_proj: bfloat16 [1536, 1536], P(None, 'mp'), may hold values from -0.15625 to 0.15625
- gain_attn: float32 [1536], P('mp'), may hold values from 0.25 to 1.75
- routes: int32 [3072, 8], P('dp'), may hold values from 0 to 47, all different within a row; in each aligned block of 192 rows (0 to 191, 192 to 383, ...) at most 40 rows name the same one
- gate_weights: float32 [3072, 8], P('dp'), may hold values from 0.05 to 0.5
- gate_up: bfloat16 [48, 1536, 2, 512], P('dp', 'mp')
- down_proj: bfloat16 [48, 512, 1536], P('dp', None, 'mp')
- gain_moe: float32 [1536], P('mp'), may hold values from 0.25 to 1.75
- kv_proj: bfloat16 [1536, 1024], P(None, 'mp'), may hold values from -0.15625 to 0.15625
- prompt_lens: int32 [16], replicated, may hold values from 1 to 760, 3040 in all
- decode_pos: int32 [32], replicated, may hold values from 0 to 1023
- page_table: int32 [48, 8], replicated, may hold values from 0 to 383, as said below
- kv_cache: bfloat16 [384, 128, 1024], P('dp', None, 'mp'), may hold values from -6 to 6
Outputs:
- layer_out: bfloat16 [3072, 1536], P('dp', 'mp')
- cache_out: bfloat16 [384, 128, 1024], P('dp', None, 'mp')
Inputs may be any that keep to these rules, and one draw needn't show every extreme that they name: In each aligned block of 192 rows (the rows of one index of dp), no slot is named by more than 40 routes, a bound that some block reaches. Slot s is held by dp index s // 3. `page_table`: all entries are distinct; page n lies on dp index n // 24. `prompt_lens`: they sum to the prefill rows of all dp indices.
All inputs are finite; a program needn't handle non-finite values.
Results may differ from a plain program's by a relative error of at most 0.0095.
Values may be sent and summed in bfloat16 or wider, within the bound.
No kernel may reach another device: no remote copies, remote signals or barrier semaphores. Data moves between devices by JAX's collectives and lax.ppermute only.
A program may use at most 128 MiB of HBM per device.

v0:
```python
import jax
import jax.numpy as jnp
from jax import lax
from jax.sharding import PartitionSpec as P

D = 1536
TOP = 8
KVH = 8
HD = 64
PAGE = 128
PAGES_SEQ = 8
DEC_DEV = 2
ROWS_DEV = 192
PRE_DEV = 190


NORM_EPS = 1e-05
ROPE_BASE = 10000.0


def row_places(row_ids, prompt_lens, decode_pos, page_table):
    prompts = prompt_lens.shape[0]
    decodes = decode_pos.shape[0]
    device = row_ids // ROWS_DEV
    within = row_ids % ROWS_DEV
    prefill = within < PRE_DEV
    stream = device * PRE_DEV + within
    seq_ends = jnp.cumsum(prompt_lens)
    seq_pre = jnp.sum((seq_ends[None, :] <= stream[:, None]).astype(jnp.int32), axis=1)
    seq_pre = jnp.minimum(seq_pre, prompts - 1)
    seq_begin = jnp.sum(
        jnp.where(
            jnp.arange(prompts, dtype=jnp.int32)[None, :] == seq_pre[:, None],
            (seq_ends - prompt_lens)[None, :],
            0,
        ),
        axis=1,
    )
    decode_ids = device * DEC_DEV + within - PRE_DEV
    decode_at = jnp.sum(
        jnp.where(
            jnp.arange(decodes, dtype=jnp.int32)[None, :] == decode_ids[:, None],
            decode_pos[None, :],
            0,
        ),
        axis=1,
    )
    sequence = jnp.where(prefill, seq_pre, prompts + decode_ids)
    position = jnp.where(prefill, stream - seq_begin, decode_at)
    page_num = page_table.reshape(-1)[sequence * PAGES_SEQ + position // PAGE]
    return (position, page_num * PAGE + position % PAGE)


def rotate_keys(values, position, key_mask):
    half_dim = HD // 2
    inverse = jnp.exp(
        -(jnp.arange(half_dim).astype(jnp.float32) * (2.0 / HD)) * jnp.log(jnp.float32(ROPE_BASE))
    )
    angles = position[:, None] * inverse[None, :]
    cosine_table = jnp.concatenate([jnp.cos(angles), jnp.cos(angles)], axis=1)
    sine_table = jnp.concatenate([jnp.sin(angles), jnp.sin(angles)], axis=1)
    first_half = values[:, :, :half_dim]
    second_half = values[:, :, half_dim:]
    turned = jnp.concatenate([-second_half, first_half], axis=2)
    rotated = values * cosine_table[:, None, :] + turned * sine_table[:, None, :]
    return jnp.where(key_mask[None, :, None], rotated, values)


def fold_with(weight, block_in):
    return jnp.dot(block_in, weight, preferred_element_type=jnp.float32)


def on_device(
    attn_out,
    residual,
    out_proj,
    gain_attn,
    routes,
    gate_weights,
    gate_up,
    down_proj,
    gain_moe,
    kv_proj,
    prompt_lens,
    decode_pos,
    page_table,
    kv_cache,
):
    rows_here = attn_out.shape[0]
    dev_count = lax.axis_size("dp")
    my_dev = lax.axis_index("dp")
    my_col = lax.axis_index("mp")
    projected = fold_with(out_proj, lax.all_gather(attn_out, "mp", axis=1, tiled=True))
    hidden_res = lax.optimization_barrier(
        (residual.astype(jnp.float32) + projected).astype(jnp.bfloat16)
    )
    res_f = hidden_res.astype(jnp.float32)
    squares = lax.psum(jnp.sum(res_f * res_f, axis=1), "mp")
    normed = (res_f * lax.rsqrt(squares / D + NORM_EPS)[:, None] * gain_attn[None, :]).astype(
        jnp.bfloat16
    )
    slots_here = gate_up.shape[0]
    slot_total = slots_here * dev_count
    capacity = (5 * rows_here * TOP + 4 * slot_total - 1) // (4 * slot_total)
    width_here = normed.shape[1]
    flat_routes = routes.reshape(-1)
    onehot = (flat_routes[:, None] == jnp.arange(slot_total, dtype=jnp.int32)[None, :]).astype(
        jnp.int32
    )
    earlier = jnp.sum((jnp.cumsum(onehot, axis=0) - onehot) * onehot, axis=1)
    target = flat_routes * capacity + earlier
    outgoing = (
        jnp.zeros((slot_total * capacity, width_here), jnp.bfloat16)
        .at[target]
        .set(jnp.repeat(normed, TOP, axis=0))
    )
    arrived = lax.all_to_all(
        outgoing.reshape(dev_count, slots_here * capacity, width_here),
        "dp",
        split_axis=0,
        concat_axis=0,
        tiled=True,
    )
    expert_in = (
        arrived.reshape(dev_count, slots_here, capacity, width_here)
        .transpose(1, 0, 2, 3)
        .reshape(slots_here, dev_count * capacity, width_here)
    )
    partial_value = jnp.einsum(
        "srd,sdgf->srgf", expert_in, gate_up, preferred_element_type=jnp.float32
    ).astype(jnp.bfloat16)
    summed = lax.psum(partial_value, "mp").astype(jnp.float32)
    activation = (jax.nn.silu(summed[:, :, 0]) * summed[:, :, 1]).astype(jnp.bfloat16)
    expert_out = jnp.einsum(
        "srf,sfd->srd", activation, down_proj, preferred_element_type=jnp.float32
    ).astype(jnp.bfloat16)
    outbound = (
        expert_out.reshape(slots_here, dev_count, capacity, width_here)
        .transpose(1, 0, 2, 3)
        .reshape(dev_count, slots_here * capacity, width_here)
    )
    returned = lax.all_to_all(outbound, "dp", split_axis=0, concat_axis=0, tiled=True).reshape(
        slot_total * capacity, width_here
    )
    picked = returned[target].astype(jnp.float32)
    mixture = jnp.sum(
        (gate_weights.reshape(-1, 1) * picked).reshape(rows_here, TOP, width_here), axis=1
    )
    layer_out = lax.optimization_barrier((res_f + mixture).astype(jnp.bfloat16))
    out_f = layer_out.astype(jnp.float32)
    out_squares = lax.psum(jnp.sum(out_f * out_f, axis=1), "mp")
    normed_kv = (out_f * lax.rsqrt(out_squares / D + NORM_EPS)[:, None] * gain_moe[None, :]).astype(
        jnp.bfloat16
    )
    kv_local = fold_with(kv_proj, lax.all_gather(normed_kv, "mp", axis=1, tiled=True))
    heads_here = kv_proj.shape[1] // HD
    head_ids = my_col * heads_here + jnp.arange(heads_here, dtype=jnp.int32)
    row_ids = my_dev * rows_here + jnp.arange(rows_here, dtype=jnp.int32)
    position, linear = row_places(row_ids, prompt_lens, decode_pos, page_table)
    rotated = rotate_keys(
        kv_local.reshape(rows_here, heads_here, HD), position.astype(jnp.float32), head_ids < KVH
    )
    rotated = rotated.reshape(rows_here, kv_proj.shape[1]).astype(jnp.bfloat16)
    per_dev = kv_cache.shape[0] * kv_cache.shape[1]
    flat_cache = kv_cache.reshape(per_dev, kv_cache.shape[2])
    new_slots = lax.all_gather(linear, "dp", axis=0, tiled=True)
    is_mine = new_slots // per_dev == my_dev
    local_slot = jnp.where(is_mine, new_slots % per_dev, per_dev)
    written = flat_cache.at[local_slot].set(
        lax.all_gather(rotated, "dp", axis=0, tiled=True), mode="drop"
    )
    return (layer_out, written.reshape(kv_cache.shape))


def solution(mesh):
    placed = (
        P("dp", "mp"),
        P("dp", "mp"),
        P(None, "mp"),
        P("mp"),
        P("dp", None),
        P("dp", None),
        P("dp", "mp", None, None),
        P("dp", None, "mp"),
        P("mp"),
        P(None, "mp"),
        P(),
        P(),
        P(),
        P("dp", None, "mp"),
    )
    return jax.shard_map(
        on_device,
        mesh=mesh,
        in_specs=placed,
        out_specs=(P("dp", "mp"), P("dp", None, "mp")),
        check_vma=False,
    )
```

profile of v0, /device:TPU:0, one launch (start us, length us, event | category | flops | bytes accessed | tf_op | source)
XLA Modules:
  0.0 432.8 jit_solution(3425271000680538237)
XLA Ops:
  7.2 4.0 copy.62
  11.8 13.6 %reduce-window.18 = s32[48,12,128]{2,1,0:T(8,128)S(1)} reduce-window(s32[48,12,128]{2,1,0:T(8,128)S(1)} %fusion.21, s32[]{:T(128)} %constant.92.clone.1), window={size=1x1x128 pad=0_0x0_0x127_0}, to_apply=%region_0.0 | reduce-window | flops 9363456 | bytes 589828 | tf_op jit(solution)/shard_map/reduce-window
  25.6 0.2 copy.39
  26.2 10.9 %all_gather.12 = bf16[192,1536]{1,0:T(8,128)(2,1)S(1)} all-gather(bf16[192,768]{1,0:T(8,128)(2,1)} %param.14), channel_id=1, replica_groups=mesh['dp'=16,'mp'=2] {'mp'}, dimensions={1}, use_global_device_ids=true | all-gather | bytes 884736 | tf_op jit(solution)/shard_map/all_gather | solution.py:93
  37.1 2.3 fusion.12
  39.5 4.9 %psum.21 = f32[192]{0:T(256)S(1)} all-reduce(f32[192]{0:T(256)S(1)} %fusion.17), channel_id=1, replica_groups=mesh['dp'=16,'mp'=2] {'mp'}, use_global_device_ids=true, to_apply=%region_4.5 | all-reduce | flops 192 | bytes 1536 | tf_op jit(solution)/shard_map/psum | solution.py:98
  44.8 9.4 %scatter_custom_fusion = bf16[1920,768]{1,0:T(8,128)(2,1)} fusion(s32[1536]{0:T(1024)S(1)} %fusion.28, bf16[]{:T(256)} %constant.90.clone.1, bf16[192,768]{1,0:T(8,128)(2,1)S(1)} %fusion.19), kind=kCustom, calls=%fused_computation.13 | custom fusion | bytes 3244034 | tf_op jit(solution)/shard_map/scatter | solution.py:115
  54.2 72.3 %all_to_all.10 = bf16[16,120,768]{2,1,0:T(8,128)(2,1)S(1)} all-to-all(bf16[16,120,768]{2,1,0:T(8,128)(2,1)} %bitcast.73), channel_id=1, replica_groups=mesh['dp'=16,'mp'=2] {'dp'}, dimensions={0} | all-to-all | bytes 5898240 | tf_op jit(solution)/shard_map/all_to_all | solution.py:117
  126.5 0.2 copy.41
  126.7 7.1 %fusion.5 = bf16[3,640,2,512]{3,1,2,0:T(8,128)(2,1)} fusion(bf16[3,640,768,1]{2,1,3,0:T(8,128)(2,1)S(1)} %bitcast.75, bf16[3,768,2,512]{3,2,1,0:T(2,128)(2,1)} %param.20), kind=kOutput, calls=%fused_computation.12 | convolution fusion | flops 3021864960 | bytes 11599872 | tf_op jit(solution)/shard_map/srd,sdgf->srgf/dot_general | solution.py:129
  133.8 102.9 %all-reduce.3.cloned.1.call-done = bf16[3,640,2,512]{3,1,2,0:T(8,128)(2,1)} async-done(((bf16[3,640,2,512]{3,1,2,0:T(8,128)(2,1)}), bf16[3,640,2,512]{3,1,2,0:T(8,128)(2,1)}) %all-reduce.3.cloned.1.call-update) | async-done | bytes 3932176 | tf_op jit(solution)/shard_map/psum | solution.py:132
  236.7 3.2 convert_element_type.74
  239.9 1.9 convolution_convert_fusion
  241.8 1.8 copy.44
  243.7 5.8 %all-to-all-start.1 = ((bf16[16,120,768]{2,1,0:T(8,128)(2,1)}), bf16[16,120,768]{2,1,0:T(8,128)(2,1)}, u32[]{:S(2)}, u32[]{:S(2)}) async-start(bf16[16,120,768]{2,1,0:T(8,128)(2,1)} %bitcast.72), calls=%async_computation.1 | async-start | bytes 5898240 | tf_op jit(solution)/shard_map/all_to_all | solution.py:142
  250.1 0.6 dynamic-slice
  251.7 1.6 gather_fusion.1
  253.3 0.3 fusion.37
  253.6 0.2 multiply_cosine_fusion
  253.9 0.9 copy.47
  255.0 50.3 %all-to-all-done.1 = bf16[16,120,768]{2,1,0:T(8,128)(2,1)} async-done(((bf16[16,120,768]{2,1,0:T(8,128)(2,1)}), bf16[16,120,768]{2,1,0:T(8,128)(2,1)}, u32[]{:S(2)}, u32[]{:S(2)}) %all-to-all-start.1) | async-done | bytes 2949152 | tf_op jit(solution)/shard_map/all_to_all | solution.py:142
  305.3 8.9 %gather_fusion = bf16[1536,768]{1,0:T(8,128)(2,1)} fusion(bf16[1920,768]{1,0:T(8,128)(2,1)} %bitcast.14, s32[2048]{0:T(1024)S(1)} %pad_clamp_fusion), kind=kCustom, calls=%fused_computation | custom fusion | bytes 4724736 | tf_op jit(solution)/shard_map/gather | solution.py:145
  314.3 3.2 fusion
  317.7 5.0 %psum.23 = f32[192]{0:T(256)S(1)} all-reduce(f32[192]{0:T(256)S(1)} %fusion.14), channel_id=1, replica_groups=mesh['dp'=16,'mp'=2] {'mp'}, use_global_device_ids=true, to_apply=%region_13.14 | all-reduce | flops 192 | bytes 1536 | tf_op jit(solution)/shard_map/psum | solution.py:151
  322.8 9.7 %all_gather.14 = bf16[192,1536]{1,0:T(8,128)(2,1)S(1)} all-gather(bf16[192,768]{1,0:T(8,128)(2,1)S(1)} %fusion.16), channel_id=1, replica_groups=mesh['dp'=16,'mp'=2] {'mp'}, dimensions={1}, use_global_device_ids=true | all-gather | bytes 884736 | tf_op jit(solution)/shard_map/all_gather | solution.py:155
  332.5 1.9 fusion.38
  334.4 1.0 copy.48
  335.3 1.1 slice_negate_fusion
  336.5 0.9 copy.49
  337.4 1.9 select_convert_fusion
  339.3 68.3 %all-reduce = s32[3072]{0:T(1024)S(1)} all-reduce(s32[3072]{0:T(1024)S(1)} %get-tuple-element.5), channel_id=1, replica_groups=mesh['dp'=16,'mp'=2] {'dp'}, use_global_device_ids=true, to_apply=%add | all-reduce | flops 3072 | bytes 24576
  407.7 18.3 %scatter_fusion = bf16[3072,512]{1,0:T(8,128)(2,1)} fusion(bf16[3072,512]{1,0:T(8,128)(2,1)} %bitcast.70, s32[3072]{0:T(1024)S(1)} %compare_select_fusion.1, bf16[3072,512]{1,0:T(8,128)(2,1)} %all-gather.2.cloned.1.call-done), kind=kCustom, calls=%fused_computation.3 | custom fusion | bytes 9449472 | tf_op jit(solution)/shard_map/scatter | solution.py:169
  (72 shorter events, 3.1 us)
Async XLA Ops:
  7.2 232.8 %copy-start = (bf16[3,512,768]{2,1,0:T(8,128)(2,1)S(1)}, bf16[3,512,768]{2,1,0:T(8,128)(2,1)}, u32[]{:S(2)}) copy-start(bf16[3,512,768]{2,1,0:T(8,128)(2,1)} %param.21) | copy-start | bytes 7077892
  7.2 4.1 copy-start.3
  7.2 229.5 %all-reduce.3.cloned.1.call-start = ((), (), s32[]{:S(2)}) async-start(), calls=%async_computation.2 | async-start | bytes 7864320 | tf_op jit(solution)/shard_map/psum | solution.py:132
  11.2 25.8 %copy-start.2 = (bf16[192,768]{1,0:T(8,128)(2,1)S(1)}, bf16[192,768]{1,0:T(8,128)(2,1)}, u32[]{:S(2)}) copy-start(bf16[192,768]{1,0:T(8,128)(2,1)} %param.15) | copy-start | bytes 884740
  26.0 18.7 %copy-start.5 = (f32[768]{0:T(1024)S(1)}, f32[768]{0:T(1024)}, u32[]{:S(2)}) copy-start(f32[768]{0:T(1024)} %param.17) | copy-start | bytes 9220
  243.6 5.9 %copy-start.4 = (f32[192,8]{0,1:T(8,128)S(1)}, f32[192,8]{0,1:T(8,128)}, u32[]{:S(2)}) copy-start(f32[192,8]{0,1:T(8,128)} %param.19) | copy-start | bytes 18436
  243.6 6.0 %copy-start.8 = (s32[16]{0:T(128)S(1)}, s32[16]{0:T(128)}, u32[]{:S(2)}) copy-start(s32[16]{0:T(128)} %param.24) | copy-start | bytes 196
  243.6 6.3 %copy-start.7 = (s32[48,8]{0,1:T(8,128)S(1)}, s32[48,8]{0,1:T(8,128)}, u32[]{:S(2)}) copy-start(s32[48,8]{0,1:T(8,128)} %param.26) | copy-start | bytes 4612
  243.6 6.5 %copy-start.10 = (u32[32]{0:T(128)S(1)}, u32[32]{0:T(128)}, u32[]{:S(2)}) copy-start(u32[32]{0:T(128)} %constant.121) | copy-start | bytes 388
  243.6 7.8 %copy-start.9 = (s32[32]{0:T(128)S(1)}, s32[32]{0:T(128)}, u32[]{:S(2)}) copy-start(s32[32]{0:T(128)} %param.25) | copy-start | bytes 388
  243.7 61.7 %all-to-all-start.1 = ((bf16[16,120,768]{2,1,0:T(8,128)(2,1)}), bf16[16,120,768]{2,1,0:T(8,128)(2,1)}, u32[]{:S(2)}, u32[]{:S(2)}) async-start(bf16[16,120,768]{2,1,0:T(8,128)(2,1)} %bitcast.72), calls=%async_computation.1 | async-start | bytes 5898240 | tf_op jit(solution)/shard_map/all_to_all | solution.py:142
  249.5 158.2 %all-gather.2.cloned.1.call-start = ((), (), s32[]{:S(2)}) async-start(), calls=%async_computation.3 | async-start | bytes 3342336 | tf_op jit(solution)/shard_map/all_gather | solution.py:170
  314.2 8.4 %copy-start.6 = (f32[768]{0:T(1024)S(1)}, f32[768]{0:T(1024)}, u32[]{:S(2)}) copy-start(f32[768]{0:T(1024)} %param.22) | copy-start | bytes 9220
  317.5 18.9 %copy-start.1 = (bf16[192,768]{1,0:T(8,128)(2,1)}, bf16[192,768]{1,0:T(8,128)(2,1)S(1)}, u32[]{:S(2)}) copy-start(bf16[192,768]{1,0:T(8,128)(2,1)S(1)} %fusion.20) | copy-start | bytes 884740
Sparse Core Ops, SparseCore 0:
  133.9 102.7 all-reduce.2
  339.5 53.7 all-gather.1
where the time goes:
time: 433 us
  blocking collectives  171 us (39%)
  waiting for transfers between devices  153 us (35%)
  local copies, waits for them, and re-layouts  49.3 us (11%)
  other arithmetic  25.1 us (6%)
  between operations  15.1 us (3%)
  matrix products  13.1 us (3%)
  starting transfers between devices  5.88 us (1%)
    psum x1, waiting for transfers between devices, on_device(): summed = lax.psum(partial_value, 'mp').astype(jnp.float32)  103 us
    all_to_all x1, blocking collectives, on_device(): lax.all_to_all(outgoing.reshape(dev_count, slots_here * capacity, width_h...  72.3 us
    unnamed x1, blocking collectives  68.3 us
    all_to_all x1, waiting for transfers between devices, on_device(): lax.all_to_all(outbound, 'dp', split_axis=0, concat_axis=0, tiled=True)  50.3 us
    scatter x1, local copies, waits for them, and re-layouts, on_device(): flat_cache.at[local_slot]  18.3 us
    another operation x5, other arithmetic  14 us
    all_gather x1, blocking collectives, on_device(): lax.all_gather(attn_out, 'mp', axis=1, tiled=True)  10.9 us
    all_gather x1, blocking collectives, on_device(): lax.all_gather(normed_kv, 'mp', axis=1, tiled=True)  9.68 us
  transfers between devices with their start and end apart: 3, of which 2 were waited for; matrix products, arithmetic and copies ran while one was open for 1% of the time, Pallas kernels for 0%

commit v1 on v0

--- a/solution.py
+++ b/solution.py
@@ -1,6 +1,9 @@
+import functools
 import jax
 import jax.numpy as jnp
 from jax import lax
+from jax.experimental import pallas as pl
+from jax.experimental.pallas import tpu as pltpu
 from jax.sharding import PartitionSpec as P
 
 D = 1536
@@ -172,7 +175,375 @@
     return (layer_out, written.reshape(kv_cache.shape))
 
 
+NZ = 4
+NX = 2
+NC = 2
+BF = jnp.bfloat16
+F32 = jnp.float32
+Z_ORDER = (0, 1, 3, 2)
+
+
+def at(z, x, c):
+    return (z * NX + x) * NC + c
+
+
+def moves(dz, dx, dc):
+    return [
+        (at(z, x, c), at((z + dz) % NZ, x ^ dx, c ^ dc))
+        for z in range(NZ)
+        for x in range(NX)
+        for c in range(NC)
+    ]
+
+
+def z_move(value, dz):
+    return lax.ppermute(value, "dp", moves(dz, 0, 0))
+
+
+def x_move(value):
+    return lax.ppermute(value, "dp", moves(0, 1, 0))
+
+
+def core_move(value):
+    return lax.ppermute(value, "dp", moves(0, 0, 1))
+
+
+def y_move(value):
+    return lax.ppermute(value, "mp", [(0, 1), (1, 0)])
+
+
+def gate_up_kernel(col_ref, a0, a1, b0, b1, pick_ref, w_ref, send_ref, keep_ref, rows):
+    cap = pick_ref.shape[2]
+    for i, block in enumerate((a0, a1, b0, b1)):
+        rows[i * cap : (i + 1) * cap, :] = jnp.dot(
+            pick_ref[0, i], block[...], preferred_element_type=F32
+        )
+    part = jnp.dot(rows[...].astype(BF), w_ref[0], preferred_element_type=F32)
+    first, second = part[: 2 * cap], part[2 * cap :]
+    keeps_first = col_ref[0] == 0
+    send_ref[0] = jnp.where(keeps_first, second, first).astype(BF)
+    keep_ref[0] = jnp.where(keeps_first, first, second)
+
+
+def gate_up(col, blocks, pick, weight):
+    slots, _, cap, rows = pick.shape
+    width, hidden2 = weight.shape[1], weight.shape[2]
+    whole = pl.BlockSpec((rows, width), lambda s, c: (0, 0))
+    out = pl.BlockSpec((1, 2 * cap, hidden2), lambda s, c: (s, 0, 0))
+    return pl.pallas_call(
+        gate_up_kernel,
+        out_shape=(
+            jax.ShapeDtypeStruct((slots, 2 * cap, hidden2), BF),
+            jax.ShapeDtypeStruct((slots, 2 * cap, hidden2), F32),
+        ),
+        grid_spec=pltpu.PrefetchScalarGridSpec(
+            num_scalar_prefetch=1,
+            grid=(slots,),
+            in_specs=[whole] * 4
+            + [
+                pl.BlockSpec((1, 4, cap, rows), lambda s, c: (s, 0, 0, 0)),
+                pl.BlockSpec((1, width, hidden2), lambda s, c: (s, 0, 0)),
+            ],
+            out_specs=(out, out),
+            scratch_shapes=[pltpu.VMEM((4 * cap, width), F32)],
+        ),
+        cost_estimate=pl.CostEstimate(
+            flops=2 * slots * 4 * cap * width * hidden2, bytes_accessed=8 << 20, transcendentals=0
+        ),
+        name="gate_up",
+    )(col, *blocks, pick, weight)
+
+
+def act_kernel(keep_ref, got_ref, gate_ref, act_ref):
+    total = keep_ref[...] + got_ref[...].astype(F32)
+    half = total.shape[2] // 2
+    act_ref[...] = (jax.nn.silu(total[:, :, :half]) * total[:, :, half:] * gate_ref[...]).astype(BF)
+
+
+def activate(keep, got, gate):
+    slots, rows, hidden2 = keep.shape
+    return pl.pallas_call(
+        act_kernel,
+        out_shape=jax.ShapeDtypeStruct((slots, rows, hidden2 // 2), BF),
+        cost_estimate=pl.CostEstimate(
+            flops=10 * keep.size, bytes_accessed=2 << 20, transcendentals=keep.size
+        ),
+        name="activate",
+    )(keep, got, gate)
+
+
+def down_kernel(col_ref, mine_ref, got_ref, spread_ref, w_ref, a0, a1, b0, b1, rows):
+    s = pl.program_id(0)
+    cap = mine_ref.shape[1] // 2
+    keeps_first = col_ref[0] == 0
+    mine, got = mine_ref[0], got_ref[0]
+    first = jnp.where(keeps_first, mine, got)
+    second = jnp.where(keeps_first, got, mine)
+    for half, act in enumerate((first, second)):
+        done = jnp.dot(act, w_ref[0], preferred_element_type=F32)
+        for i in range(2):
+            rows[2 * half + i, pl.ds(pl.multiple_of(s * cap, 8), cap), :] = done[
+                i * cap : (i + 1) * cap
+            ]
+
+    @pl.when(s == pl.num_programs(0) - 1)
+    def _():
+        for i, out in enumerate((a0, a1, b0, b1)):
+            out[...] = jnp.dot(
+                spread_ref[i], rows[i].astype(BF), preferred_element_type=F32
+            ).astype(BF)
+
+
+def down(col, mine, got, spread, weight):
+    slots, half_rows, hidden = mine.shape
+    cap = half_rows // 2
+    width = weight.shape[2]
+    tokens = spread.shape[1]
+    act_spec = pl.BlockSpec((1, half_rows, hidden), lambda s, c: (s, 0, 0))
+    out = pl.BlockSpec((tokens, width), lambda s, c: (0, 0))
+    return pl.pallas_call(
+        down_kernel,
+        out_shape=[jax.ShapeDtypeStruct((tokens, width), BF)] * 4,
+        grid_spec=pltpu.PrefetchScalarGridSpec(
+            num_scalar_prefetch=1,
+            grid=(slots,),
+            in_specs=[
+                act_spec,
+                act_spec,
+                pl.BlockSpec((4, tokens, slots * cap), lambda s, c: (0, 0, 0)),
+                pl.BlockSpec((1, hidden, width), lambda s, c: (s, 0, 0)),
+            ],
+            out_specs=[out] * 4,
+            scratch_shapes=[pltpu.VMEM((4, slots * cap, width), F32)],
+        ),
+        cost_estimate=pl.CostEstimate(
+            flops=4 * slots * half_rows * width * hidden, bytes_accessed=4 << 20, transcendentals=0
+        ),
+        name="down",
+    )(col, mine, got, spread, weight)
+
+
+def page_kernel(place_ref, page_ref, *refs):
+    count = len(refs) - 3
+    cache_ref, out_ref, everything = refs[count], refs[count + 1], refs[count + 2]
+
+    @pl.when(pl.program_id(0) == 0)
+    def _():
+        for i in range(count):
+            everything[place_ref[i]] = refs[i][...]
+
+    pages, length, _ = cache_ref.shape
+    tokens = everything.shape[1]
+    i = lax.broadcasted_iota(jnp.int32, (length, 2 * tokens), 0)
+    m = lax.broadcasted_iota(jnp.int32, (length, 2 * tokens), 1)
+    row = lax.broadcasted_iota(jnp.int32, (length, 1), 0)
+    for k in range(pages):
+        page = pl.program_id(0) * pages + k
+        base, offset = page_ref[0, page], page_ref[1, page]
+        low, high, skip = page_ref[2, page], page_ref[3, page], page_ref[4, page]
+
+        @pl.when(high > low)
+        def _():
+            source = i + offset + jnp.where(i + offset >= PRE_DEV, skip, 0)
+            select = (m == source).astype(F32).astype(BF)
+            taken = jnp.dot(
+                select[:, :tokens], everything[base], preferred_element_type=F32
+            ) + jnp.dot(
+                select[:, tokens:],
+                everything[jnp.minimum(base + 1, count - 1)],
+                preferred_element_type=F32,
+            )
+            hit = (row >= low) & (row < high)
+            out_ref[k] = jnp.where(hit, taken, cache_ref[k].astype(F32)).astype(BF)
+
+        @pl.when(high <= low)
+        def _():
+            out_ref[k] = cache_ref[k]
+
+
+def write_pages(place, page_data, blocks, cache):
+    pages, length, width = cache.shape
+    step = 4 if pages % 4 == 0 else 1
+    tokens = blocks[0].shape[0]
+    whole = pl.BlockSpec((tokens, width), lambda s, a, b: (0, 0))
+    page_spec = pl.BlockSpec((step, length, width), lambda s, a, b: (s, 0, 0))
+    return pl.pallas_call(
+        page_kernel,
+        out_shape=jax.ShapeDtypeStruct(cache.shape, cache.dtype),
+        grid_spec=pltpu.PrefetchScalarGridSpec(
+            num_scalar_prefetch=2,
+            grid=(pages // step,),
+            in_specs=[whole] * len(blocks) + [page_spec],
+            out_specs=page_spec,
+            scratch_shapes=[pltpu.VMEM((len(blocks), tokens, width), cache.dtype)],
+        ),
+        name="write_pages",
+    )(place, page_data, *blocks, cache)
+
+
+def page_sources(my_dev, pages_here, prompt_lens, decode_pos, page_table):
+    prompts = prompt_lens.shape[0]
+    ends = jnp.cumsum(prompt_lens)
+    ordinal = jnp.arange(PAGES_SEQ, dtype=jnp.int32)[None, :]
+    start = (ends - prompt_lens)[:, None] + ordinal * PAGE
+    high_p = jnp.clip(prompt_lens[:, None] - ordinal * PAGE, 0, PAGE)
+    base_p = start // PRE_DEV
+    offset_p = start % PRE_DEV
+    c = jnp.arange(decode_pos.shape[0], dtype=jnp.int32)[:, None]
+    at_row = (decode_pos % PAGE)[:, None] + 0 * ordinal
+    hit = (decode_pos // PAGE)[:, None] == ordinal
+    base_d = c // DEC_DEV + 0 * ordinal
+    offset_d = PRE_DEV + c % DEC_DEV - at_row
+    high_d = jnp.where(hit, at_row + 1, at_row)
+    both = lambda p, d: jnp.concatenate([p, d], axis=0).reshape(-1)
+    entries = jnp.stack(
+        [
+            both(base_p, base_d),
+            both(offset_p, offset_d),
+            both(0 * high_p, at_row),
+            both(high_p, high_d),
+            both(0 * high_p + DEC_DEV, 0 * high_d),
+        ]
+    )
+    entries = entries.at[0].set(jnp.where(entries[3] > entries[2], entries[0], 0))
+    mine = my_dev * pages_here + jnp.arange(pages_here, dtype=jnp.int32)
+    match = page_table.reshape(-1)[None, :] == mine[:, None]
+    return jnp.sum(jnp.where(match[None], entries[:, None, :], 0), axis=2).astype(jnp.int32)
+
+
+def routing(meta, slot_ids, cap):
+    names, gates = meta[:, :TOP], meta[:, TOP:]
+    rows = meta.shape[2]
+    same = names[:, None] == slot_ids.astype(F32)[None, :, None, None]
+    chosen = jnp.max(same.astype(F32), axis=2)
+    gate = jnp.sum(jnp.where(same, gates[:, None], 0.0), axis=2)
+    r = jnp.arange(rows, dtype=jnp.int32)
+    before = (r[:, None] < r[None, :]).astype(BF)
+    position = jnp.einsum("bst,tu->bsu", chosen.astype(BF), before, preferred_element_type=F32)
+    position = jnp.where(chosen > 0, position, -1.0)
+    places = jnp.arange(cap, dtype=jnp.int32).astype(F32)
+    taken = position[:, :, None, :] == places[None, None, :, None]
+    pick = taken.astype(BF).transpose(1, 0, 2, 3)
+    slots = slot_ids.shape[0]
+    wide = jnp.repeat(position.transpose(0, 2, 1), cap, axis=2)
+    spread = (wide == jnp.tile(places, slots)[None, None, :]).astype(BF)
+    row_gate = jnp.sum(jnp.where(taken, gate[:, :, None, :], 0.0), axis=3)
+    return pick, spread, row_gate.transpose(1, 0, 2)
+
+
+def on_device_16x2(
+    attn_out,
+    residual,
+    out_proj,
+    gain_attn,
+    routes,
+    gate_weights,
+    gate_up_w,
+    down_proj,
+    gain_moe,
+    kv_proj,
+    prompt_lens,
+    decode_pos,
+    page_table,
+    kv_cache,
+):
+    rows_here, width = attn_out.shape
+    my_dev = lax.axis_index("dp")
+    my_col = lax.axis_index("mp")
+    col = my_col.reshape(1)
+    slots_here = gate_up_w.shape[0]
+    slot_total = slots_here * NZ * NX * NC
+    cap = (5 * rows_here * TOP + 4 * slot_total - 1) // (4 * slot_total)
+    weight = gate_up_w.reshape(slots_here, width, -1)
+
+    attn_other = y_move(attn_out)
+    meta = jnp.concatenate([routes.astype(F32).T, gate_weights.T], axis=0)
+    meta_x = x_move(meta)
+    pair = jnp.stack([meta, meta_x])
+    quad = jnp.concatenate([pair, core_move(pair)])
+    metas = {0: quad}
+    for dz in (1, 3, 2):
+        metas[dz] = z_move(quad, dz)
+
+    own_first = lambda w: (
+        lax.dynamic_slice_in_dim(w, my_col * width, width, 0),
+        lax.dynamic_slice_in_dim(w, (1 - my_col) * width, width, 0),
+    )
+    proj_own, proj_other = own_first(out_proj)
+    dot = functools.partial(jnp.dot, preferred_element_type=F32)
+    hidden = (
+        residual.astype(F32) + dot(attn_out, proj_own) + dot(attn_other, proj_other)
+    ).astype(BF)
+    hidden = lax.optimization_barrier(hidden)
+    res_f = hidden.astype(F32)
+    squares = jnp.sum(res_f * res_f, axis=1)
+    squares = squares + y_move(squares)
+    normed = (res_f * lax.rsqrt(squares / D + NORM_EPS)[:, None] * gain_attn[None, :]).astype(BF)
+
+    slot_ids = my_dev * slots_here + jnp.arange(slots_here, dtype=jnp.int32)
+    routed = {dz: routing(metas[dz], slot_ids, cap) for dz in range(NZ)}
+
+    column = {dz: z_move(normed, dz) if dz else normed for dz in Z_ORDER}
+    blocks = {}
+    for dz in Z_ORDER:
+        a0 = column[dz]
+        a1 = x_move(a0)
+        blocks[dz] = (a0, a1, core_move(a0), core_move(a1))
+
+    mixture = res_f
+    for dz in Z_ORDER:
+        pick, spread, row_gate = routed[dz]
+        send, keep = gate_up(col, blocks[dz], pick, weight)
+        got = y_move(send)
+        gate = jnp.where(my_col == 0, row_gate[:, :2], row_gate[:, 2:])
+        act = activate(keep, got, gate.reshape(slots_here, 2 * cap, 1))
+        act_got = y_move(act)
+        a0, a1, b0, b1 = down(col, act, act_got, spread, down_proj)
+        a1 = (a1.astype(F32) + core_move(b1).astype(F32)).astype(BF)
+        from_x = x_move(a1).astype(F32)
+        a0 = a0.astype(F32) + core_move(b0).astype(F32) + from_x
+        mixture = mixture + (z_move(a0.astype(BF), NZ - dz).astype(F32) if dz else a0)
+    layer_out = lax.optimization_barrier(mixture.astype(BF))
+
+    out_other = y_move(layer_out)
+    gain_other = y_move(gain_moe)
+    own_f, other_f = layer_out.astype(F32), out_other.astype(F32)
+    out_squares = jnp.sum(own_f * own_f, axis=1) + jnp.sum(other_f * other_f, axis=1)
+    scale = lax.rsqrt(out_squares / D + NORM_EPS)[:, None]
+    v_own = (own_f * scale * gain_moe[None, :]).astype(BF)
+    v_other = (other_f * scale * gain_other[None, :]).astype(BF)
+
+    columns = kv_proj.shape[1]
+    halves = kv_proj.reshape(-1, columns // HD, 2, HD // 2)
+    turned = jnp.stack([-halves[:, :, 1], halves[:, :, 0]], axis=2).reshape(kv_proj.shape)
+    kv_own, kv_other = own_first(jnp.concatenate([kv_proj, turned], axis=1))
+    both = dot(v_own, kv_own) + dot(v_other, kv_other)
+    row_ids = my_dev * rows_here + jnp.arange(rows_here, dtype=jnp.int32)
+    position, _ = row_places(row_ids, prompt_lens, decode_pos, page_table)
+    lane = jnp.arange(columns, dtype=jnp.int32)
+    inverse = jnp.exp(-((lane % (HD // 2)).astype(F32) * (2.0 / HD)) * jnp.log(F32(ROPE_BASE)))
+    angles = position.astype(F32)[:, None] * inverse[None, :]
+    is_key = (my_col * columns + lane < KVH * HD)[None, :]
+    cosine = jnp.where(is_key, jnp.cos(angles), 1.0)
+    sine = jnp.where(is_key, jnp.sin(angles), 0.0)
+    rotated = (both[:, :columns] * cosine + both[:, columns:] * sine).astype(BF)
+
+    z, x, c = my_dev // (NX * NC), my_dev // NC % NX, my_dev % NC
+    kv_blocks, places = [], []
+    kv_column = {dz: z_move(rotated, dz) if dz else rotated for dz in Z_ORDER}
+    for dz in Z_ORDER:
+        a0 = kv_column[dz]
+        a1 = x_move(a0)
+        kv_blocks += [a0, a1, core_move(a0), core_move(a1)]
+        source_z = (z + NZ - dz) % NZ
+        places += [at(source_z, x, c), at(source_z, 1 - x, c), at(source_z, x, 1 - c), at(source_z, 1 - x, 1 - c)]
+    page_data = page_sources(my_dev, kv_cache.shape[0], prompt_lens, decode_pos, page_table)
+    written = write_pages(jnp.stack(places).astype(jnp.int32), page_data, kv_blocks, kv_cache)
+    return (layer_out, written)
+
+
 def solution(mesh):
+    body = on_device_16x2 if (mesh.shape["dp"], mesh.shape["mp"]) == (NZ * NX * NC, 2) else on_device
     placed = (
         P("dp", "mp"),
         P("dp", "mp"),
@@ -190,7 +561,7 @@
         P("dp", None, "mp"),
     )
     return jax.shard_map(
-        on_device,
+        body,
         mesh=mesh,
         in_specs=placed,
         out_specs=(P("dp", "mp"), P("dp", None, "mp")),

time: 433 us -> 273 us (0.63)
  the two profiles are of different devices: /device:TPU:0 before, /device:TPU:19 now
where the time goes in v1:
time: 273 us; the launch traced here: 271 us
  waiting for transfers between devices  77.9 us (29%)
  starting transfers between devices  63.6 us (23%)
  Pallas kernels  58.4 us (21%)
  local copies, waits for them, and re-layouts  33.2 us (12%)
  other arithmetic  29.6 us (11%)
  matrix products  7.03 us (3%)
    ppermute x12, waiting for transfers between devices, z_move(): return lax.ppermute(value, 'dp', moves(dz, 0, 0))  50.6 us
    ppermute x25, starting transfers between devices, core_move(): return lax.ppermute(value, 'dp', moves(0, 0, 1))  34.2 us
    pallas_call x4, Pallas kernels, gate_up(): pl.pallas_call(gate_up_kernel, out_shape=(jax.ShapeDtypeStruct((slots, 2...  22.1 us
    pallas_call x4, Pallas kernels, down(): pl.pallas_call(down_kernel, out_shape=[jax.ShapeDtypeStruct((tokens, widt...  19.2 us
    ppermute x12, waiting for transfers between devices, y_move(): return lax.ppermute(value, 'mp', [(0, 1), (1, 0)])  16.2 us
    ppermute x12, starting transfers between devices, z_move(): return lax.ppermute(value, 'dp', moves(dz, 0, 0))  11.3 us
    ppermute x13, waiting for transfers between devices, x_move(): return lax.ppermute(value, 'dp', moves(0, 1, 0))  11 us
    ppermute x13, starting transfers between devices, x_move(): return lax.ppermute(value, 'dp', moves(0, 1, 0))  10.3 us
  transfers between devices with their start and end apart: 62, of which 18 were waited for; matrix products, arithmetic and copies ran while one was open for 24% of the time, Pallas kernels for 18%

profile of v1, /device:TPU:19, one launch (start us, length us, event | category | flops | bytes accessed | tf_op | source)
XLA Modules:
  0.0 271.1 jit_solution(17338447161447152312)
XLA Ops:
  6.5 2.6 copy.140
  9.1 2.4 slice_negate_fusion
  16.1 8.7 %reshape.311.w_ref = bf16[3,768,1024]{2,1,0:T(8,128)(2,1)} reshape(bf16[3,768,2,512]{3,2,1,0:T(2,128)(2,1)} %param.22) | data formatting | bytes 9437184 | tf_op jit(solution)/shard_map/reshape | solution.py:457
  25.0 2.4 collective-permute-start.27
  29.9 4.3 %collective-permute-done.16 = f32[4,16,192]{2,1,0:T(8,128)S(1)} collective-permute-done((f32[4,16,192]{2,1,0:T(8,128)S(1)}, f32[4,16,192]{2,1,0:T(8,128)S(1)}, u32[]{:S(2)}, u32[]{:S(2)}) %collective-permute-start.16) | collective-permute-done | bytes 49184 | tf_op jit(solution)/shard_map/ppermute | solution.py:200
  43.2 3.1 %collective-permute-start.3 = (bf16[192,768]{1,0:T(8,128)(2,1)S(1)}, bf16[192,768]{1,0:T(8,128)(2,1)S(1)}, u32[]{:S(2)}, u32[]{:S(2)}) collective-permute-start(bf16[192,768]{1,0:T(8,128)(2,1)S(1)} %fusion.22.a0), channel_id=1, source_target_pairs={{0,2},{2,0},{4,6},{6,4},{8,10},{10,8},{12,14},{14,12},{16,18},{18,... | collective-permute-start | bytes 884744 | tf_op jit(solution)/shard_map/ppermute | solution.py:208
  46.3 6.8 %collective-permute-done.34.a0 = bf16[192,768]{1,0:T(8,128)(2,1)} collective-permute-done((bf16[192,768]{1,0:T(8,128)(2,1)S(1)}, bf16[192,768]{1,0:T(8,128)(2,1)}, u32[]{:S(2)}, u32[]{:S(2)}) %collective-permute-start.34) | collective-permute-done | bytes 294944 | tf_op jit(solution)/shard_map/ppermute | solution.py:200
  56.5 8.2 %collective-permute-done.23.a0 = bf16[192,768]{1,0:T(8,128)(2,1)} collective-permute-done((bf16[192,768]{1,0:T(8,128)(2,1)S(1)}, bf16[192,768]{1,0:T(8,128)(2,1)}, u32[]{:S(2)}, u32[]{:S(2)}) %collective-permute-start.23) | collective-permute-done | bytes 294944 | tf_op jit(solution)/shard_map/ppermute | solution.py:200
  69.7 5.5 %gate_up.4 = (bf16[3,80,1024]{2,1,0:T(8,128)(2,1)}, f32[3,80,1024]{2,1,0:T(8,128)}) custom-call(s32[1]{0:T(128)} %bitcast.2.col_ref, bf16[192,768]{1,0:T(8,128)(2,1)} %copy-done.5, bf16[192,768]{1,0:T(8,128)(2,1)} %copy-done.9, bf16[192,768]{1,0:T(8,128)(2,1)} %copy-done.10, bf16[192,768]{1,0:T(8,128)(2,1)} %copy-done.11, ...), custom_call_target="tpu_custom_call" | custom-call | flops 754974720 | bytes 8388608 | tf_op jit(solution)/shard_map/gate_up/pallas_call | solution.py:233
  78.7 2.7 collective-permute-start.14
  81.4 5.5 %gate_up.7 = (bf16[3,80,1024]{2,1,0:T(8,128)(2,1)}, f32[3,80,1024]{2,1,0:T(8,128)}) custom-call(s32[1]{0:T(128)} %bitcast.2.col_ref, bf16[192,768]{1,0:T(8,128)(2,1)} %collective-permute-done.34.a0, bf16[192,768]{1,0:T(8,128)(2,1)} %collective-permute-done.35.a1, bf16[192,768]{1,0:T(8,128)(2,1)} %collective-permute-done.36.b0, ...), custom_call_target="tpu_custom_call" | custom-call | flops 754974720 | bytes 8388608 | tf_op jit(solution)/shard_map/gate_up/pallas_call | solution.py:233
  87.3 5.5 %gate_up.6 = (bf16[3,80,1024]{2,1,0:T(8,128)(2,1)}, f32[3,80,1024]{2,1,0:T(8,128)}) custom-call(s32[1]{0:T(128)} %bitcast.2.col_ref, bf16[192,768]{1,0:T(8,128)(2,1)} %collective-permute-done.23.a0, bf16[192,768]{1,0:T(8,128)(2,1)} %collective-permute-done.24.a1, bf16[192,768]{1,0:T(8,128)(2,1)} %collective-permute-done.25.b0, ...), custom_call_target="tpu_custom_call" | custom-call | flops 754974720 | bytes 8388608 | tf_op jit(solution)/shard_map/gate_up/pallas_call | solution.py:233
  107.6 5.5 %gate_up.5 = (bf16[3,80,1024]{2,1,0:T(8,128)(2,1)}, f32[3,80,1024]{2,1,0:T(8,128)}) custom-call(s32[1]{0:T(128)} %bitcast.2.col_ref, bf16[192,768]{1,0:T(8,128)(2,1)} %collective-permute-done.12.a0, bf16[192,768]{1,0:T(8,128)(2,1)} %collective-permute-done.13.a1, bf16[192,768]{1,0:T(8,128)(2,1)} %collective-permute-done.14.b0, ...), custom_call_target="tpu_custom_call" | custom-call | flops 754974720 | bytes 8388608 | tf_op jit(solution)/shard_map/gate_up/pallas_call | solution.py:233
  116.8 2.4 compare_convert_fusion.7
  121.8 8.7 %collective-permute-done.8.got_ref = bf16[3,80,512]{2,1,0:T(8,128)(2,1)} collective-permute-done((bf16[3,80,512]{2,1,0:T(8,128)(2,1)}, bf16[3,80,512]{2,1,0:T(8,128)(2,1)}, u32[]{:S(2)}, u32[]{:S(2)}) %collective-permute-start.8) | collective-permute-done | bytes 245792 | tf_op jit(solution)/shard_map/ppermute | solution.py:212
  130.5 4.8 %down.4 = (bf16[192,768]{1,0:T(8,128)(2,1)}, bf16[192,768]{1,0:T(8,128)(2,1)}, bf16[192,768]{1,0:T(8,128)(2,1)}, bf16[192,768]{1,0:T(8,128)(2,1)}) custom-call(s32[1]{0:T(128)} %bitcast.2.col_ref, bf16[3,80,512]{2,1,0:T(8,128)(2,1)} %activate.4.mine_ref, bf16[3,80,512]{2,1,0:T(8,128)(2,1)} %collective-permute-done.8.got_ref, ...), custom_call_target="tpu_custom_call" | custom-call | flops 377487360 | bytes 4194304 | tf_op jit(solution)/shard_map/down/pallas_call | solution.py:304
  135.3 3.4 %collective-permute-start.10 = (bf16[192,768]{1,0:T(8,128)(2,1)}, bf16[192,768]{1,0:T(8,128)(2,1)}, u32[]{:S(2)}, u32[]{:S(2)}) collective-permute-start(bf16[192,768]{1,0:T(8,128)(2,1)} %get-tuple-element.43), channel_id=1, source_target_pairs={{0,2},{2,0},{4,6},{6,4},{8,10},{10,8},{12,14},{14,12},{16,18},{18,... | collective-permute-start | bytes 884744 | tf_op jit(solution)/shard_map/ppermute | solution.py:208
  145.6 4.8 %down.7 = (bf16[192,768]{1,0:T(8,128)(2,1)}, bf16[192,768]{1,0:T(8,128)(2,1)}, bf16[192,768]{1,0:T(8,128)(2,1)}, bf16[192,768]{1,0:T(8,128)(2,1)}) custom-call(s32[1]{0:T(128)} %bitcast.2.col_ref, bf16[3,80,512]{2,1,0:T(8,128)(2,1)} %activate.7.mine_ref, bf16[3,80,512]{2,1,0:T(8,128)(2,1)} %collective-permute-done.40.got_ref, ...), custom_call_target="tpu_custom_call" | custom-call | flops 377487360 | bytes 4194304 | tf_op jit(solution)/shard_map/down/pallas_call | solution.py:304
  151.0 4.8 %down.6 = (bf16[192,768]{1,0:T(8,128)(2,1)}, bf16[192,768]{1,0:T(8,128)(2,1)}, bf16[192,768]{1,0:T(8,128)(2,1)}, bf16[192,768]{1,0:T(8,128)(2,1)}) custom-call(s32[1]{0:T(128)} %bitcast.2.col_ref, bf16[3,80,512]{2,1,0:T(8,128)(2,1)} %activate.6.mine_ref, bf16[3,80,512]{2,1,0:T(8,128)(2,1)} %collective-permute-done.29.got_ref, ...), custom_call_target="tpu_custom_call" | custom-call | flops 377487360 | bytes 4194304 | tf_op jit(solution)/shard_map/down/pallas_call | solution.py:304
  158.1 4.8 %down.5 = (bf16[192,768]{1,0:T(8,128)(2,1)}, bf16[192,768]{1,0:T(8,128)(2,1)}, bf16[192,768]{1,0:T(8,128)(2,1)}, bf16[192,768]{1,0:T(8,128)(2,1)}) custom-call(s32[1]{0:T(128)} %bitcast.2.col_ref, bf16[3,80,512]{2,1,0:T(8,128)(2,1)} %activate.5.mine_ref, bf16[3,80,512]{2,1,0:T(8,128)(2,1)} %collective-permute-done.18.got_ref, ...), custom_call_target="tpu_custom_call" | custom-call | flops 377487360 | bytes 4194304 | tf_op jit(solution)/shard_map/down/pallas_call | solution.py:304
  168.2 4.9 %collective-permute-done.43 = bf16[192,768]{1,0:T(8,128)(2,1)S(1)} collective-permute-done((bf16[192,768]{1,0:T(8,128)(2,1)S(1)}, bf16[192,768]{1,0:T(8,128)(2,1)S(1)}, u32[]{:S(2)}, u32[]{:S(2)}) %collective-permute-start.43) | collective-permute-done | bytes 294944 | tf_op jit(solution)/shard_map/ppermute | solution.py:204
  176.4 3.1 %collective-permute-done.32 = bf16[192,768]{1,0:T(8,128)(2,1)S(1)} collective-permute-done((bf16[192,768]{1,0:T(8,128)(2,1)S(1)}, bf16[192,768]{1,0:T(8,128)(2,1)S(1)}, u32[]{:S(2)}, u32[]{:S(2)}) %collective-permute-start.32) | collective-permute-done | bytes 294944 | tf_op jit(solution)/shard_map/ppermute | solution.py:204
  181.2 3.5 %collective-permute-start.33 = (bf16[192,768]{1,0:T(8,128)(2,1)}, bf16[192,768]{1,0:T(8,128)(2,1)}, u32[]{:S(2)}, u32[]{:S(2)}) collective-permute-start(bf16[192,768]{1,0:T(8,128)(2,1)} %add_convert_fusion.2), channel_id=1, source_target_pairs={{0,8},{2,10},{4,12},{6,14},{8,16},{10,18},{12,20},{14,22},{16,24},... | collective-permute-start | bytes 884744 | tf_op jit(solution)/shard_map/ppermute | solution.py:200
  186.7 2.3 collective-permute-start.22
  189.6 2.5 pad_maximum_fusion
  192.5 3.7 %collective-permute-done.44 = bf16[192,768]{1,0:T(8,128)(2,1)} collective-permute-done((bf16[192,768]{1,0:T(8,128)(2,1)}, bf16[192,768]{1,0:T(8,128)(2,1)}, u32[]{:S(2)}, u32[]{:S(2)}) %collective-permute-start.44) | collective-permute-done | bytes 294944 | tf_op jit(solution)/shard_map/ppermute | solution.py:200
  196.2 12.3 %collective-permute-done.33 = bf16[192,768]{1,0:T(8,128)(2,1)} collective-permute-done((bf16[192,768]{1,0:T(8,128)(2,1)}, bf16[192,768]{1,0:T(8,128)(2,1)}, u32[]{:S(2)}, u32[]{:S(2)}) %collective-permute-start.33) | collective-permute-done | bytes 294944 | tf_op jit(solution)/shard_map/ppermute | solution.py:200
  212.7 5.6 %collective-permute-done.45 = bf16[192,768]{1,0:T(8,128)(2,1)S(1)} collective-permute-done((bf16[192,768]{1,0:T(8,128)(2,1)S(1)}, bf16[192,768]{1,0:T(8,128)(2,1)S(1)}, u32[]{:S(2)}, u32[]{:S(2)}) %collective-permute-start.45) | collective-permute-done | bytes 294944 | tf_op jit(solution)/shard_map/ppermute | solution.py:212
  228.3 12.7 %collective-permute-done.50.refs_4_ = bf16[192,512]{1,0:T(8,128)(2,1)S(1)} collective-permute-done((bf16[192,512]{1,0:T(8,128)(2,1)S(1)}, bf16[192,512]{1,0:T(8,128)(2,1)S(1)}, u32[]{:S(2)}, u32[]{:S(2)}) %collective-permute-start.50) | collective-permute-done | bytes 196640 | tf_op jit(solution)/shard_map/ppermute | solution.py:200
  246.3 4.0 %collective-permute-start.60 = (bf16[192,512]{1,0:T(8,128)(2,1)S(1)}, bf16[192,512]{1,0:T(8,128)(2,1)}, u32[]{:S(2)}, u32[]{:S(2)}) collective-permute-start(bf16[192,512]{1,0:T(8,128)(2,1)S(1)} %collective-permute-done.58.refs_12_), channel_id=1, source_target_pairs={{0,2},{2,0},{4,6},{6,4},{8,10},{10,8},{12,14},{14,12},{16,18},{18,... | collective-permute-start | bytes 589832 | tf_op jit(solution)/shard_map/ppermute | solution.py:208
  250.5 4.0 %collective-permute-start.57 = (bf16[192,512]{1,0:T(8,128)(2,1)}, bf16[192,512]{1,0:T(8,128)(2,1)}, u32[]{:S(2)}, u32[]{:S(2)}) collective-permute-start(bf16[192,512]{1,0:T(8,128)(2,1)} %collective-permute-done.55.refs_9_), channel_id=1, source_target_pairs={{0,2},{2,0},{4,6},{6,4},{8,10},{10,8},{12,14},{14,12},{16,18},{18,... | collective-permute-start | bytes 589832 | tf_op jit(solution)/shard_map/ppermute | solution.py:208
  262.8 8.3 %write_pages.1 = bf16[24,128,512]{2,1,0:T(8,128)(2,1)} custom-call(s32[16]{0:T(128)} %stack.86.place_ref, s32[5,24]{1,0:T(8,128)} %select_reduce_fusion.4.page_ref, bf16[192,512]{1,0:T(8,128)(2,1)} %copy-done.6, bf16[192,512]{1,0:T(8,128)(2,1)} %copy-done.16, bf16[192,512]{1,0:T(8,128)(2,1)} %copy-done.17, bf16[192,512]{1,0:T(8,128)(2,1)} %copy-done.22, ...), custom_call_target="tpu_custom_call" | custom-call | tf_op jit(solution)/shard_map/write_pages/pallas_call | solution.py:370
  (288 shorter events, 106.1 us)
Async XLA Ops:
  0.6 34.2 %collective-permute-start = (bf16[192,768]{1,0:T(8,128)(2,1)}, bf16[192,768]{1,0:T(8,128)(2,1)}, u32[]{:S(2)}, u32[]{:S(2)}) collective-permute-start(bf16[192,768]{1,0:T(8,128)(2,1)} %param.16), channel_id=1, source_target_pairs={{0,1},{1,0},{2,3},{3,2},{4,5},{5,4},{6,7},{7,6},{8,9},{9,8},{10,11... | collective-permute-start | bytes 884744 | tf_op jit(solution)/shard_map/ppermute | solution.py:212
  39.1 15.3 %collective-permute-start.2 = (bf16[192,768]{1,0:T(8,128)(2,1)S(1)}, bf16[192,768]{1,0:T(8,128)(2,1)S(1)}, u32[]{:S(2)}, u32[]{:S(2)}) collective-permute-start(bf16[192,768]{1,0:T(8,128)(2,1)S(1)} %fusion.22.a0), channel_id=1, source_target_pairs={{0,4},{2,6},{4,0},{6,2},{8,12},{10,14},{12,8},{14,10},{16,20},{18,... | collective-permute-start | bytes 884744 | tf_op jit(solution)/shard_map/ppermute | solution.py:204
  40.6 24.1 %collective-permute-start.23 = (bf16[192,768]{1,0:T(8,128)(2,1)S(1)}, bf16[192,768]{1,0:T(8,128)(2,1)}, u32[]{:S(2)}, u32[]{:S(2)}) collective-permute-start(bf16[192,768]{1,0:T(8,128)(2,1)S(1)} %fusion.22.a0), channel_id=1, source_target_pairs={{0,24},{2,26},{4,28},{6,30},{8,0},{10,2},{12,4},{14,6},{16,8},{18,... | collective-permute-start | bytes 884744 | tf_op jit(solution)/shard_map/ppermute | solution.py:200
  41.6 23.8 %collective-permute-start.12 = (bf16[192,768]{1,0:T(8,128)(2,1)S(1)}, bf16[192,768]{1,0:T(8,128)(2,1)}, u32[]{:S(2)}, u32[]{:S(2)}) collective-permute-start(bf16[192,768]{1,0:T(8,128)(2,1)S(1)} %fusion.22.a0), channel_id=1, source_target_pairs={{0,8},{2,10},{4,12},{6,14},{8,16},{10,18},{12,20},{14,22},{16,24},... | collective-permute-start | bytes 884744 | tf_op jit(solution)/shard_map/ppermute | solution.py:200
  43.2 23.3 %collective-permute-start.3 = (bf16[192,768]{1,0:T(8,128)(2,1)S(1)}, bf16[192,768]{1,0:T(8,128)(2,1)S(1)}, u32[]{:S(2)}, u32[]{:S(2)}) collective-permute-start(bf16[192,768]{1,0:T(8,128)(2,1)S(1)} %fusion.22.a0), channel_id=1, source_target_pairs={{0,2},{2,0},{4,6},{6,4},{8,10},{10,8},{12,14},{14,12},{16,18},{18,... | collective-permute-start | bytes 884744 | tf_op jit(solution)/shard_map/ppermute | solution.py:208
  53.1 15.6 %collective-permute-start.35 = (bf16[192,768]{1,0:T(8,128)(2,1)}, bf16[192,768]{1,0:T(8,128)(2,1)}, u32[]{:S(2)}, u32[]{:S(2)}) collective-permute-start(bf16[192,768]{1,0:T(8,128)(2,1)} %collective-permute-done.34.a0), channel_id=1, source_target_pairs={{0,4},{2,6},{4,0},{6,2},{8,12},{10,14},{12,8},{14,10},{16,20},{18,... | collective-permute-start | bytes 884744 | tf_op jit(solution)/shard_map/ppermute | solution.py:204
  54.4 14.6 %collective-permute-start.4 = (bf16[192,768]{1,0:T(8,128)(2,1)S(1)}, bf16[192,768]{1,0:T(8,128)(2,1)S(1)}, u32[]{:S(2)}, u32[]{:S(2)}) collective-permute-start(bf16[192,768]{1,0:T(8,128)(2,1)S(1)} %collective-permute-done.2.a1), channel_id=1, source_target_pairs={{0,2},{2,0},{4,6},{6,4},{8,10},{10,8},{12,14},{14,12},{16,18},{18,... | collective-permute-start | bytes 884744 | tf_op jit(solution)/shard_map/ppermute | solution.py:208
  66.6 20.4 %collective-permute-start.25 = (bf16[192,768]{1,0:T(8,128)(2,1)}, bf16[192,768]{1,0:T(8,128)(2,1)}, u32[]{:S(2)}, u32[]{:S(2)}) collective-permute-start(bf16[192,768]{1,0:T(8,128)(2,1)} %collective-permute-done.23.a0), channel_id=1, source_target_pairs={{0,2},{2,0},{4,6},{6,4},{8,10},{10,8},{12,14},{14,12},{16,18},{18,... | collective-permute-start | bytes 884744 | tf_op jit(solution)/shard_map/ppermute | solution.py:208
  75.3 38.2 %collective-permute-start.7 = (bf16[3,80,1024]{2,1,0:T(8,128)(2,1)}, bf16[3,80,1024]{2,1,0:T(8,128)(2,1)}, u32[]{:S(2)}, u32[]{:S(2)}) collective-permute-start(bf16[3,80,1024]{2,1,0:T(8,128)(2,1)} %get-tuple-element.39), channel_id=1, source_target_pairs={{0,1},{1,0},{2,3},{3,2},{4,5},{5,4},{6,7},{7,6},{8,9},{9,8},{10,11... | collective-permute-start | bytes 1474568 | tf_op jit(solution)/shard_map/ppermute | solution.py:212
  78.7 29.0 %collective-permute-start.14 = (bf16[192,768]{1,0:T(8,128)(2,1)}, bf16[192,768]{1,0:T(8,128)(2,1)}, u32[]{:S(2)}, u32[]{:S(2)}) collective-permute-start(bf16[192,768]{1,0:T(8,128)(2,1)} %collective-permute-done.12.a0), channel_id=1, source_target_pairs={{0,2},{2,0},{4,6},{6,4},{8,10},{10,8},{12,14},{14,12},{16,18},{18,... | collective-permute-start | bytes 884744 | tf_op jit(solution)/shard_map/ppermute | solution.py:208
  81.4 26.3 %collective-permute-start.15 = (bf16[192,768]{1,0:T(8,128)(2,1)}, bf16[192,768]{1,0:T(8,128)(2,1)}, u32[]{:S(2)}, u32[]{:S(2)}) collective-permute-start(bf16[192,768]{1,0:T(8,128)(2,1)} %collective-permute-done.13.a1), channel_id=1, source_target_pairs={{0,2},{2,0},{4,6},{6,4},{8,10},{10,8},{12,14},{14,12},{16,18},{18,... | collective-permute-start | bytes 884744 | tf_op jit(solution)/shard_map/ppermute | solution.py:208
  86.9 32.3 %collective-permute-start.39 = (bf16[3,80,1024]{2,1,0:T(8,128)(2,1)}, bf16[3,80,1024]{2,1,0:T(8,128)(2,1)}, u32[]{:S(2)}, u32[]{:S(2)}) collective-permute-start(bf16[3,80,1024]{2,1,0:T(8,128)(2,1)} %get-tuple-element.57), channel_id=1, source_target_pairs={{0,1},{1,0},{2,3},{3,2},{4,5},{5,4},{6,7},{7,6},{8,9},{9,8},{10,11... | collective-permute-start | bytes 1474568 | tf_op jit(solution)/shard_map/ppermute | solution.py:212
  92.9 45.8 %collective-permute-start.28 = (bf16[3,80,1024]{2,1,0:T(8,128)(2,1)}, bf16[3,80,1024]{2,1,0:T(8,128)(2,1)}, u32[]{:S(2)}, u32[]{:S(2)}) collective-permute-start(bf16[3,80,1024]{2,1,0:T(8,128)(2,1)} %get-tuple-element.51), channel_id=1, source_target_pairs={{0,1},{1,0},{2,3},{3,2},{4,5},{5,4},{6,7},{7,6},{8,9},{9,8},{10,11... | collective-permute-start | bytes 1474568 | tf_op jit(solution)/shard_map/ppermute | solution.py:212
  113.2 29.2 %collective-permute-start.17 = (bf16[3,80,1024]{2,1,0:T(8,128)(2,1)}, bf16[3,80,1024]{2,1,0:T(8,128)(2,1)}, u32[]{:S(2)}, u32[]{:S(2)}) collective-permute-start(bf16[3,80,1024]{2,1,0:T(8,128)(2,1)} %get-tuple-element.45), channel_id=1, source_target_pairs={{0,1},{1,0},{2,3},{3,2},{4,5},{5,4},{6,7},{7,6},{8,9},{9,8},{10,11... | collective-permute-start | bytes 1474568 | tf_op jit(solution)/shard_map/ppermute | solution.py:212
  115.7 14.8 %collective-permute-start.8 = (bf16[3,80,512]{2,1,0:T(8,128)(2,1)}, bf16[3,80,512]{2,1,0:T(8,128)(2,1)}, u32[]{:S(2)}, u32[]{:S(2)}) collective-permute-start(bf16[3,80,512]{2,1,0:T(8,128)(2,1)} %activate.4.mine_ref), channel_id=1, source_target_pairs={{0,1},{1,0},{2,3},{3,2},{4,5},{5,4},{6,7},{7,6},{8,9},{9,8},{10,11... | collective-permute-start | bytes 737288 | tf_op jit(solution)/shard_map/ppermute | solution.py:212
  121.5 24.2 %collective-permute-start.40 = (bf16[3,80,512]{2,1,0:T(8,128)(2,1)}, bf16[3,80,512]{2,1,0:T(8,128)(2,1)}, u32[]{:S(2)}, u32[]{:S(2)}) collective-permute-start(bf16[3,80,512]{2,1,0:T(8,128)(2,1)} %activate.7.mine_ref), channel_id=1, source_target_pairs={{0,1},{1,0},{2,3},{3,2},{4,5},{5,4},{6,7},{7,6},{8,9},{9,8},{10,11... | collective-permute-start | bytes 737288 | tf_op jit(solution)/shard_map/ppermute | solution.py:212
  135.3 20.5 %collective-permute-start.10 = (bf16[192,768]{1,0:T(8,128)(2,1)}, bf16[192,768]{1,0:T(8,128)(2,1)}, u32[]{:S(2)}, u32[]{:S(2)}) collective-permute-start(bf16[192,768]{1,0:T(8,128)(2,1)} %get-tuple-element.43), channel_id=1, source_target_pairs={{0,2},{2,0},{4,6},{6,4},{8,10},{10,8},{12,14},{14,12},{16,18},{18,... | collective-permute-start | bytes 884744 | tf_op jit(solution)/shard_map/ppermute | solution.py:208
  142.0 50.0 %collective-permute-start.9 = (bf16[192,768]{1,0:T(8,128)(2,1)}, bf16[192,768]{1,0:T(8,128)(2,1)}, u32[]{:S(2)}, u32[]{:S(2)}) collective-permute-start(bf16[192,768]{1,0:T(8,128)(2,1)} %get-tuple-element.41), channel_id=1, source_target_pairs={{0,2},{2,0},{4,6},{6,4},{8,10},{10,8},{12,14},{14,12},{16,18},{18,... | collective-permute-start | bytes 884744 | tf_op jit(solution)/shard_map/ppermute | solution.py:208
  150.9 16.5 %collective-permute-start.41 = (bf16[192,768]{1,0:T(8,128)(2,1)}, bf16[192,768]{1,0:T(8,128)(2,1)}, u32[]{:S(2)}, u32[]{:S(2)}) collective-permute-start(bf16[192,768]{1,0:T(8,128)(2,1)} %get-tuple-element.59), channel_id=1, source_target_pairs={{0,2},{2,0},{4,6},{6,4},{8,10},{10,8},{12,14},{14,12},{16,18},{18,... | collective-permute-start | bytes 884744 | tf_op jit(solution)/shard_map/ppermute | solution.py:208
  158.1 18.0 %collective-permute-start.30 = (bf16[192,768]{1,0:T(8,128)(2,1)}, bf16[192,768]{1,0:T(8,128)(2,1)}, u32[]{:S(2)}, u32[]{:S(2)}) collective-permute-start(bf16[192,768]{1,0:T(8,128)(2,1)} %get-tuple-element.53), channel_id=1, source_target_pairs={{0,2},{2,0},{4,6},{6,4},{8,10},{10,8},{12,14},{14,12},{16,18},{18,... | collective-permute-start | bytes 884744 | tf_op jit(solution)/shard_map/ppermute | solution.py:208
  176.1 16.4 %collective-permute-start.11 = (bf16[192,768]{1,0:T(8,128)(2,1)}, bf16[192,768]{1,0:T(8,128)(2,1)}, u32[]{:S(2)}, u32[]{:S(2)}) collective-permute-start(bf16[192,768]{1,0:T(8,128)(2,1)} %add_convert_fusion.6), channel_id=1, source_target_pairs={{0,4},{2,6},{4,0},{6,2},{8,12},{10,14},{12,8},{14,10},{16,20},{18,... | collective-permute-start | bytes 884744 | tf_op jit(solution)/shard_map/ppermute | solution.py:204
  179.4 16.8 %collective-permute-start.44 = (bf16[192,768]{1,0:T(8,128)(2,1)}, bf16[192,768]{1,0:T(8,128)(2,1)}, u32[]{:S(2)}, u32[]{:S(2)}) collective-permute-start(bf16[192,768]{1,0:T(8,128)(2,1)} %add_convert_fusion), channel_id=1, source_target_pairs={{0,16},{2,18},{4,20},{6,22},{8,24},{10,26},{12,28},{14,30},{16,0},... | collective-permute-start | bytes 884744 | tf_op jit(solution)/shard_map/ppermute | solution.py:200
  181.2 27.3 %collective-permute-start.33 = (bf16[192,768]{1,0:T(8,128)(2,1)}, bf16[192,768]{1,0:T(8,128)(2,1)}, u32[]{:S(2)}, u32[]{:S(2)}) collective-permute-start(bf16[192,768]{1,0:T(8,128)(2,1)} %add_convert_fusion.2), channel_id=1, source_target_pairs={{0,8},{2,10},{4,12},{6,14},{8,16},{10,18},{12,20},{14,22},{16,24},... | collective-permute-start | bytes 884744 | tf_op jit(solution)/shard_map/ppermute | solution.py:200
  186.7 21.9 %collective-permute-start.22 = (bf16[192,768]{1,0:T(8,128)(2,1)}, bf16[192,768]{1,0:T(8,128)(2,1)}, u32[]{:S(2)}, u32[]{:S(2)}) collective-permute-start(bf16[192,768]{1,0:T(8,128)(2,1)} %add_convert_fusion.4), channel_id=1, source_target_pairs={{0,24},{2,26},{4,28},{6,30},{8,0},{10,2},{12,4},{14,6},{16,8},{18,... | collective-permute-start | bytes 884744 | tf_op jit(solution)/shard_map/ppermute | solution.py:200
  192.1 28.7 %collective-permute-start.46 = (f32[768]{0:T(1024)S(1)}, f32[768]{0:T(1024)S(1)}, u32[]{:S(2)}, u32[]{:S(2)}) collective-permute-start(f32[768]{0:T(1024)S(1)} %copy-done.34), channel_id=1, source_target_pairs={{0,1},{1,0},{2,3},{3,2},{4,5},{5,4},{6,7},{7,6},{8,9},{9,8},{10,11... | collective-permute-start | bytes 9224 | tf_op jit(solution)/shard_map/ppermute | solution.py:212
  223.3 18.0 %collective-permute-start.47 = (bf16[192,512]{1,0:T(8,128)(2,1)S(1)}, bf16[192,512]{1,0:T(8,128)(2,1)S(1)}, u32[]{:S(2)}, u32[]{:S(2)}) collective-permute-start(bf16[192,512]{1,0:T(8,128)(2,1)S(1)} %fusion.30.refs_0_), channel_id=1, source_target_pairs={{0,4},{2,6},{4,0},{6,2},{8,12},{10,14},{12,8},{14,10},{16,20},{18,... | collective-permute-start | bytes 589832 | tf_op jit(solution)/shard_map/ppermute | solution.py:204
  224.5 18.4 %collective-permute-start.48 = (bf16[192,512]{1,0:T(8,128)(2,1)S(1)}, bf16[192,512]{1,0:T(8,128)(2,1)S(1)}, u32[]{:S(2)}, u32[]{:S(2)}) collective-permute-start(bf16[192,512]{1,0:T(8,128)(2,1)S(1)} %fusion.30.refs_0_), channel_id=1, source_target_pairs={{0,2},{2,0},{4,6},{6,4},{8,10},{10,8},{12,14},{14,12},{16,18},{18,... | collective-permute-start | bytes 589832 | tf_op jit(solution)/shard_map/ppermute | solution.py:208
  226.2 14.9 %collective-permute-start.50 = (bf16[192,512]{1,0:T(8,128)(2,1)S(1)}, bf16[192,512]{1,0:T(8,128)(2,1)S(1)}, u32[]{:S(2)}, u32[]{:S(2)}) collective-permute-start(bf16[192,512]{1,0:T(8,128)(2,1)S(1)} %fusion.30.refs_0_), channel_id=1, source_target_pairs={{0,8},{2,10},{4,12},{6,14},{8,16},{10,18},{12,20},{14,22},{16,24},... | collective-permute-start | bytes 589832 | tf_op jit(solution)/shard_map/ppermute | solution.py:200
  226.2 16.9 %collective-permute-start.54 = (bf16[192,512]{1,0:T(8,128)(2,1)S(1)}, bf16[192,512]{1,0:T(8,128)(2,1)S(1)}, u32[]{:S(2)}, u32[]{:S(2)}) collective-permute-start(bf16[192,512]{1,0:T(8,128)(2,1)S(1)} %fusion.30.refs_0_), channel_id=1, source_target_pairs={{0,24},{2,26},{4,28},{6,30},{8,0},{10,2},{12,4},{14,6},{16,8},{18,... | collective-permute-start | bytes 589832 | tf_op jit(solution)/shard_map/ppermute | solution.py:200
  227.6 16.6 %collective-permute-start.58 = (bf16[192,512]{1,0:T(8,128)(2,1)S(1)}, bf16[192,512]{1,0:T(8,128)(2,1)S(1)}, u32[]{:S(2)}, u32[]{:S(2)}) collective-permute-start(bf16[192,512]{1,0:T(8,128)(2,1)S(1)} %fusion.30.refs_0_), channel_id=1, source_target_pairs={{0,16},{2,18},{4,20},{6,22},{8,24},{10,26},{12,28},{14,30},{16,0},... | collective-permute-start | bytes 589832 | tf_op jit(solution)/shard_map/ppermute | solution.py:200
  245.1 17.6 %collective-permute-start.56 = (bf16[192,512]{1,0:T(8,128)(2,1)S(1)}, bf16[192,512]{1,0:T(8,128)(2,1)}, u32[]{:S(2)}, u32[]{:S(2)}) collective-permute-start(bf16[192,512]{1,0:T(8,128)(2,1)S(1)} %collective-permute-done.54.refs_8_), channel_id=1, source_target_pairs={{0,2},{2,0},{4,6},{6,4},{8,10},{10,8},{12,14},{14,12},{16,18},{18,... | collective-permute-start | bytes 589832 | tf_op jit(solution)/shard_map/ppermute | solution.py:208
  246.3 16.4 %collective-permute-start.60 = (bf16[192,512]{1,0:T(8,128)(2,1)S(1)}, bf16[192,512]{1,0:T(8,128)(2,1)}, u32[]{:S(2)}, u32[]{:S(2)}) collective-permute-start(bf16[192,512]{1,0:T(8,128)(2,1)S(1)} %collective-permute-done.58.refs_12_), channel_id=1, source_target_pairs={{0,2},{2,0},{4,6},{6,4},{8,10},{10,8},{12,14},{14,12},{16,18},{18,... | collective-permute-start | bytes 589832 | tf_op jit(solution)/shard_map/ppermute | solution.py:208
  (66 other events, 737.4 us)

commit v2 on v0

--- a/solution.py
+++ b/solution.py
@@ -1,6 +1,9 @@
+import functools
 import jax
 import jax.numpy as jnp
 from jax import lax
+from jax.experimental import pallas as pl
+from jax.experimental.pallas import tpu as pltpu
 from jax.sharding import PartitionSpec as P
 
 D = 1536
@@ -172,7 +175,580 @@
     return (layer_out, written.reshape(kv_cache.shape))
 
 
+NZ = 4
+NX = 2
+NC = 2
+BF = jnp.bfloat16
+F32 = jnp.float32
+GATE_LANES = 256
+LIGHT = pl.CostEstimate(flops=1, bytes_accessed=1, transcendentals=0)
+ROOM = pltpu.CompilerParams(vmem_limit_bytes=16 << 20)
+
+
+def at(z, x, c):
+    return (z * NX + x) * NC + c
+
+
+def moves(dz, dx, dc):
+    return [
+        (at(z, x, c), at((z + dz) % NZ, x ^ dx, c ^ dc))
+        for z in range(NZ)
+        for x in range(NX)
+        for c in range(NC)
+    ]
+
+
+def z_move(value, dz):
+    return lax.ppermute(value, "dp", moves(dz, 0, 0))
+
+
+def x_move(value):
+    return lax.ppermute(value, "dp", moves(0, 1, 0))
+
+
+def core_move(value):
+    return lax.ppermute(value, "dp", moves(0, 0, 1))
+
+
+def y_move(value):
+    return lax.ppermute(value, "mp", [(0, 1), (1, 0)])
+
+
+def after(value, *earlier):
+    return lax.optimization_barrier((value,) + earlier)[0]
+
+
+def picked(info, slots, cap):
+    place = lax.broadcasted_iota(jnp.int32, (cap, info.shape[1]), 0).astype(F32)
+    return jnp.concatenate([(info[q : q + 1] == place).astype(F32) for q in range(slots)], axis=0)
+
+
+def gate_up_kernel(count, mine_ref, w_ref, *refs):
+    *sources, send_ref, keep_ref, info_ref, rows = refs
+    slots, total, _ = rows.shape
+    cap = total // count
+    s = pl.program_id(0)
+
+    @pl.when(s == 0)
+    def _():
+        blocks = [b for r in sources for b in ([r] if len(r.shape) == 2 else [r.at[0], r.at[1]])]
+        tokens = info_ref.shape[2]
+        r = lax.broadcasted_iota(jnp.int32, (tokens, tokens), 0)
+        before = (r < lax.broadcasted_iota(jnp.int32, (tokens, tokens), 1)).astype(F32).astype(BF)
+        for i, block in enumerate(blocks):
+            meta = block[tokens:, :].astype(F32)
+            names = meta[:TOP, :tokens]
+            gates = sum(meta[TOP:, k * GATE_LANES : k * GATE_LANES + tokens] for k in range(3))
+            chosen, gate = [], []
+            for q in range(slots):
+                same = names == (mine_ref[1] + q).astype(F32)
+                chosen.append(jnp.max(same.astype(F32), axis=0, keepdims=True))
+                gate.append(jnp.sum(jnp.where(same, gates, 0.0), axis=0, keepdims=True))
+            unused = jnp.zeros((info_ref.shape[1] - slots, tokens), F32)
+            chosen = jnp.concatenate(chosen + [unused], axis=0)
+            place = jnp.dot(chosen.astype(BF), before, preferred_element_type=F32)
+            place = jnp.where(chosen > 0, place, -1.0)
+            rest = jnp.zeros((info_ref.shape[1] - 2 * slots, tokens), F32)
+            info_ref[i] = jnp.concatenate([place[:slots]] + gate + [rest], axis=0)
+            pick = picked(place, slots, cap).astype(BF)
+            taken = jnp.dot(pick, block[:tokens, :], preferred_element_type=F32)
+            for q in range(slots):
+                rows[q, i * cap : (i + 1) * cap] = taken[q * cap : (q + 1) * cap]
+
+    x = rows[s].astype(BF)
+    half, hidden = total // 2, w_ref.shape[3]
+    keeps_first = mine_ref[0] == 0
+    for k in range(2):
+        part = jnp.dot(x, w_ref[k, 0], preferred_element_type=F32)
+        first, second = part[:half], part[half:]
+        send_ref[0, :, k * hidden : (k + 1) * hidden] = jnp.where(
+            keeps_first, second, first
+        ).astype(BF)
+        keep_ref[0, :, k * hidden : (k + 1) * hidden] = jnp.where(keeps_first, first, second)
+
+
+def gate_up(mine, blocks, weight, cap):
+    _, slots, width, hidden = weight.shape
+    n = sum(b.ndim - 1 for b in blocks)
+    tokens = blocks[0].shape[-2] - 2 * TOP
+    half = n * cap // 2
+    info = (n, -(-2 * slots // 8) * 8, tokens)
+    out = pl.BlockSpec((1, half, 2 * hidden), lambda s, c: (s, 0, 0))
+    return pl.pallas_call(
+        functools.partial(gate_up_kernel, n),
+        out_shape=(
+            jax.ShapeDtypeStruct((slots, half, 2 * hidden), BF),
+            jax.ShapeDtypeStruct((slots, half, 2 * hidden), F32),
+            jax.ShapeDtypeStruct(info, F32),
+        ),
+        grid_spec=pltpu.PrefetchScalarGridSpec(
+            num_scalar_prefetch=1,
+            grid=(slots,),
+            in_specs=[pl.BlockSpec((2, 1, width, hidden), lambda s, c: (0, s, 0, 0))]
+            + [pl.BlockSpec(b.shape, lambda s, c, d=b.ndim: (0,) * d) for b in blocks],
+            out_specs=(out, out, pl.BlockSpec(info, lambda s, c: (0, 0, 0))),
+            scratch_shapes=[pltpu.VMEM((slots, n * cap, width), F32)],
+        ),
+        cost_estimate=LIGHT,
+        compiler_params=ROOM,
+        name="gate_up",
+    )(mine, weight, *blocks)
+
+
+def act_kernel(col_ref, info_ref, keep_ref, got_ref, act_ref):
+    s = pl.program_id(0)
+    slots = pl.num_programs(0)
+    n = info_ref.shape[0] // 2
+    cap = keep_ref.shape[1] // n
+    place = lax.broadcasted_iota(jnp.int32, (cap, info_ref.shape[2]), 0).astype(F32)
+    gates = []
+    for i in range(n):
+        block = col_ref[0] * n + i
+        position = info_ref[block, pl.ds(s, 1), :]
+        gate = info_ref[block, pl.ds(slots + s, 1), :]
+        gates.append(jnp.sum(jnp.where(position == place, gate, 0.0), axis=1, keepdims=True))
+    gate = jnp.concatenate(gates, axis=0) if n > 1 else gates[0]
+    total = keep_ref[0] + got_ref[0].astype(F32)
+    half = total.shape[1] // 2
+    act_ref[0] = (jax.nn.silu(total[:, :half]) * total[:, half:] * gate).astype(BF)
+
+
+def activate(col, info, keep, got):
+    slots, rows, hidden2 = keep.shape
+    spec = lambda w: pl.BlockSpec((1, rows, w), lambda s, c: (s, 0, 0))
+    return pl.pallas_call(
+        act_kernel,
+        out_shape=jax.ShapeDtypeStruct((slots, rows, hidden2 // 2), BF),
+        grid_spec=pltpu.PrefetchScalarGridSpec(
+            num_scalar_prefetch=1,
+            grid=(slots,),
+            in_specs=[
+                pl.BlockSpec(info.shape, lambda s, c: (0, 0, 0)),
+                spec(hidden2),
+                spec(hidden2),
+            ],
+            out_specs=spec(hidden2 // 2),
+        ),
+        cost_estimate=LIGHT,
+        compiler_params=ROOM,
+        name="activate",
+    )(col, info, keep, got)
+
+
+def down_kernel(col_ref, info_ref, mine_ref, got_ref, w_ref, *refs):
+    *outs, rows = refs
+    s = pl.program_id(0)
+    n = len(outs) // 2
+    slots = pl.num_programs(0)
+    total = rows.shape[1]
+    count = info_ref.shape[0]
+    cap = mine_ref.shape[1] // n
+    keeps_first = col_ref[0] == 0
+    mine, got = mine_ref[0], got_ref[0]
+    for half, act in enumerate(
+        (jnp.where(keeps_first, mine, got), jnp.where(keeps_first, got, mine))
+    ):
+        done = jnp.dot(act, w_ref[0], preferred_element_type=F32)
+        for i in range(n):
+            rows[half * n + i, pl.ds(pl.multiple_of(s * cap, 8), cap), :] = done[
+                i * cap : (i + 1) * cap
+            ]
+
+    @pl.when(s == slots - 1)
+    def _():
+        for i in range(count):
+            pick = picked(info_ref[i], total // cap, cap)
+            summed = jnp.dot(pick.T.astype(BF), rows[i].astype(BF), preferred_element_type=F32)
+            outs[i][...] = summed.astype(BF)
+
+
+def down(col, info, mine, got, weight):
+    slots, half_rows, hidden = mine.shape
+    n = info.shape[0] // 2
+    cap = half_rows // n
+    tokens, width = info.shape[2], weight.shape[2]
+    act_spec = pl.BlockSpec((1, half_rows, hidden), lambda s, c: (s, 0, 0))
+    out = pl.BlockSpec((tokens, width), lambda s, c: (0, 0))
+    return pl.pallas_call(
+        down_kernel,
+        out_shape=[jax.ShapeDtypeStruct((tokens, width), BF)] * (2 * n),
+        grid_spec=pltpu.PrefetchScalarGridSpec(
+            num_scalar_prefetch=1,
+            grid=(slots,),
+            in_specs=[
+                pl.BlockSpec(info.shape, lambda s, c: (0, 0, 0)),
+                act_spec,
+                act_spec,
+                pl.BlockSpec((1, hidden, width), lambda s, c: (s, 0, 0)),
+            ],
+            out_specs=[out] * (2 * n),
+            scratch_shapes=[pltpu.VMEM((2 * n, slots * cap, width), F32)],
+        ),
+        cost_estimate=LIGHT,
+        compiler_params=ROOM,
+        name="down",
+    )(col, info, mine, got, weight)
+
+
+def add_kernel(stacked, mine_ref, *refs):
+    n = (len(refs) - 1) // 2 if stacked else len(refs) // 3
+    for i in range(n):
+        total = (refs[i][...].astype(F32) + refs[n + i][...].astype(F32)).astype(BF)
+        if stacked:
+            refs[-1][i] = total
+        else:
+            refs[2 * n + i][...] = total
+
+
+def add(mine, left, right, stacked):
+    n, shape = len(left), left[0].shape
+    out = jax.ShapeDtypeStruct(((n,) if stacked else ()) + shape, BF)
+    return pl.pallas_call(
+        functools.partial(add_kernel, stacked),
+        out_shape=out if stacked else [out] * n,
+        in_specs=[pl.BlockSpec(memory_space=pltpu.SMEM)]
+        + [pl.BlockSpec(memory_space=pltpu.VMEM)] * (2 * n),
+        cost_estimate=LIGHT,
+        compiler_params=ROOM,
+        name="add",
+    )(mine, *left, *right)
+
+
+def stack_kernel(a_ref, b_ref, out_ref):
+    out_ref[0] = a_ref[...]
+    out_ref[1] = b_ref[...]
+
+
+def stack(a, b):
+    return pl.pallas_call(
+        stack_kernel,
+        out_shape=jax.ShapeDtypeStruct((2,) + a.shape, a.dtype),
+        cost_estimate=LIGHT,
+        compiler_params=ROOM,
+        name="stack",
+    )(a, b)
+
+
+def copy_kernel(cache_ref, out_ref):
+    out_ref[...] = cache_ref[...]
+
+
+def copy_cache(cache):
+    pages, length, width = cache.shape
+    step = 4 if pages % 4 == 0 else 1
+    spec = pl.BlockSpec((step, length, width), lambda s: (s, 0, 0))
+    return pl.pallas_call(
+        copy_kernel,
+        out_shape=jax.ShapeDtypeStruct(cache.shape, cache.dtype),
+        grid=(pages // step,),
+        in_specs=[spec],
+        out_specs=spec,
+        cost_estimate=LIGHT,
+        compiler_params=ROOM,
+        name="copy_cache",
+    )(cache)
+
+
+def page_list_kernel(dev_ref, lens_ref, pos_ref, table_ref, out_ref):
+    prompts, pages_here = lens_ref.shape[0], dev_ref[1]
+    dev = dev_ref[0]
+
+    def put(found, page, base, offset, low, high, skip):
+        local = page - dev * pages_here
+        here = (local >= 0) & (local < pages_here)
+
+        @pl.when(here)
+        def _():
+            for k, value in enumerate((local, base, offset, low, high, skip)):
+                out_ref[k, found] = value
+
+        return found + here.astype(jnp.int32)
+
+    def prompt(q, carry):
+        begin, found = carry
+        length = lens_ref[q]
+
+        def page(k, found):
+            start = begin + k * PAGE
+            high = jnp.minimum(length - k * PAGE, PAGE)
+            base = lax.div(start, PRE_DEV)
+            return put(
+                found, table_ref[q, k], base, start - base * PRE_DEV, 0, high, jnp.int32(DEC_DEV)
+            )
+
+        return begin + length, lax.fori_loop(0, lax.div(length + PAGE - 1, PAGE), page, found)
+
+    def decode(c, found):
+        k = lax.div(pos_ref[c], PAGE)
+        low = pos_ref[c] - k * PAGE
+        base = lax.div(c, DEC_DEV)
+        offset = PRE_DEV + c - base * DEC_DEV - low
+        return put(found, table_ref[prompts + c, k], base, offset, low, low + 1, jnp.int32(0))
+
+    _, found = lax.fori_loop(0, prompts, prompt, (jnp.int32(0), jnp.int32(0)))
+    out_ref[6, 0] = lax.fori_loop(0, pos_ref.shape[0], decode, found)
+
+
+def page_list(my_dev, pages_here, prompt_lens, decode_pos, page_table):
+    smem = pl.BlockSpec(memory_space=pltpu.SMEM)
+    return pl.pallas_call(
+        page_list_kernel,
+        out_shape=jax.ShapeDtypeStruct((8, pages_here), jnp.int32),
+        in_specs=[smem] * 4,
+        out_specs=smem,
+        cost_estimate=LIGHT,
+        compiler_params=ROOM,
+        name="page_list",
+    )(jnp.stack([my_dev, jnp.int32(pages_here)]), prompt_lens, decode_pos, page_table)
+
+
+def page_kernel(place_ref, page_ref, *refs):
+    count = len(refs) - 7
+    cache_ref, out_ref, everything, held, kv_sem, in_sem, out_sem = refs[count:]
+    tokens = everything.shape[1]
+    length = held.shape[1]
+    pages = page_ref[6, 0]
+    block_copies = [
+        pltpu.make_async_copy(refs[i], everything.at[place_ref[i]], kv_sem.at[i])
+        for i in range(count)
+    ]
+    page_in = lambda k: pltpu.make_async_copy(
+        cache_ref.at[page_ref[0, k]], held.at[k], in_sem.at[k]
+    )
+    page_out = lambda k: pltpu.make_async_copy(
+        held.at[k], out_ref.at[page_ref[0, k]], out_sem.at[k]
+    )
+    lax.fori_loop(0, pages, lambda k, x: (page_in(k).start(), x)[1], 0)
+    for copy in block_copies:
+        copy.start()
+    i = lax.broadcasted_iota(jnp.int32, (length, 2 * tokens), 0)
+    m = lax.broadcasted_iota(jnp.int32, (length, 2 * tokens), 1)
+    row = lax.broadcasted_iota(jnp.int32, (length, 1), 0)
+    for copy in block_copies:
+        copy.wait()
+
+    def step(k, carry):
+        base, offset = page_ref[1, k], page_ref[2, k]
+        low, high, skip = page_ref[3, k], page_ref[4, k], page_ref[5, k]
+        source = i + offset + jnp.where(i + offset >= PRE_DEV, skip, 0)
+        select = (m == source).astype(F32).astype(BF)
+        after_base = jnp.minimum(base + 1, count - 1)
+        taken = jnp.dot(
+            select[:, :tokens], everything[base], preferred_element_type=F32
+        ) + jnp.dot(select[:, tokens:], everything[after_base], preferred_element_type=F32)
+        hit = (row >= low) & (row < high)
+        page_in(k).wait()
+        held[k] = jnp.where(hit, taken, held[k].astype(F32)).astype(BF)
+        page_out(k).start()
+        return carry
+
+    lax.fori_loop(0, pages, step, 0)
+    lax.fori_loop(0, pages, lambda k, x: (page_out(k).wait(), x)[1], 0)
+
+
+def write_pages(place, page_data, blocks, cache):
+    pages, length, width = cache.shape
+    tokens = blocks[0].shape[0]
+    in_hbm = pl.BlockSpec(memory_space=pltpu.HBM)
+    return pl.pallas_call(
+        page_kernel,
+        out_shape=jax.ShapeDtypeStruct(cache.shape, cache.dtype),
+        grid_spec=pltpu.PrefetchScalarGridSpec(
+            num_scalar_prefetch=2,
+            grid=(),
+            in_specs=[pl.BlockSpec(memory_space=pl.ANY)] * len(blocks) + [in_hbm],
+            out_specs=in_hbm,
+            scratch_shapes=[
+                pltpu.VMEM((len(blocks), tokens, width), cache.dtype),
+                pltpu.VMEM(cache.shape, cache.dtype),
+                pltpu.SemaphoreType.DMA((len(blocks),)),
+                pltpu.SemaphoreType.DMA((pages,)),
+                pltpu.SemaphoreType.DMA((pages,)),
+            ],
+        ),
+        input_output_aliases={2 + len(blocks): 0},
+        cost_estimate=LIGHT,
+        compiler_params=ROOM,
+        name="write_pages",
+    )(place, page_data, *blocks, cache)
+
+
+def on_device_16x2(
+    attn_out,
+    residual,
+    out_proj,
+    gain_attn,
+    routes,
+    gate_weights,
+    gate_up_w,
+    down_proj,
+    gain_moe,
+    kv_proj,
+    prompt_lens,
+    decode_pos,
+    page_table,
+    kv_cache,
+):
+    rows_here, width = attn_out.shape
+    my_dev = lax.axis_index("dp")
+    my_col = lax.axis_index("mp")
+    slots_here = gate_up_w.shape[0]
+    slot_total = slots_here * NZ * NX * NC
+    cap = (5 * rows_here * TOP + 4 * slot_total - 1) // (4 * slot_total)
+    dot = functools.partial(jnp.dot, preferred_element_type=F32)
+    own_first = lambda w: (
+        lax.dynamic_slice_in_dim(w, my_col * width, width, 0),
+        lax.dynamic_slice_in_dim(w, (1 - my_col) * width, width, 0),
+    )
+
+    attn_other = y_move(attn_out)
+    weight = gate_up_w.transpose(2, 0, 1, 3)
+    proj_own, proj_other = own_first(out_proj)
+    first_half = residual.astype(F32) + dot(attn_out, proj_own)
+    gates = gate_weights.T
+    high = lax.reduce_precision(gates, 8, 7)
+    middle = lax.reduce_precision(gates - high, 8, 7)
+    padded = lambda a, lanes: jnp.pad(a, ((0, 0), (0, lanes - rows_here)))
+    last = width - 2 * GATE_LANES
+    names = jnp.pad(padded(routes.astype(F32).T, GATE_LANES), ((0, 0), (0, width - GATE_LANES)))
+    gates = jnp.concatenate(
+        [padded(high, GATE_LANES), padded(middle, GATE_LANES), padded(gates - high - middle, last)],
+        axis=1,
+    )
+    meta = jnp.concatenate([names, gates], axis=0).astype(BF)
+    weight, first_half, meta = lax.optimization_barrier((weight, first_half, meta))
+    hidden = (first_half + dot(attn_other, proj_other)).astype(BF)
+    hidden = lax.optimization_barrier(hidden)
+    res_f = hidden.astype(F32)
+    squares = jnp.sum(res_f * res_f, axis=1)
+    squares = squares + y_move(squares)
+    scale = lax.rsqrt(squares / D + NORM_EPS)[:, None]
+    normed = (res_f * scale * gain_attn[None, :]).astype(BF)
+    own = jnp.concatenate([normed, meta], axis=0)
+
+    mine = jnp.stack([my_col, my_dev * slots_here]).astype(jnp.int32)
+    infos, keeps, moving, acts, parts, sums = {}, {}, {}, {}, {}, {}
+
+    def up_step(g, blocks, *earlier):
+        send, keeps[g], infos[g] = gate_up(after(mine, *earlier), blocks, weight, cap)
+        moving[g] = y_move(send)
+        return keeps[g]
+
+    def act_step(g, *earlier):
+        acts[g] = activate(after(mine, *earlier), infos[g], keeps[g], moving[g])
+        moving[g] = y_move(acts[g])
+        return acts[g]
+
+    def down_step(g, *earlier):
+        outs = down(after(mine, *earlier), infos[g], acts[g], moving[g], down_proj)
+        n = len(outs) // 2
+        parts[g] = (outs[:n], [core_move(b) for b in outs[n:]])
+        return outs[0]
+
+    def sum_step(g, stacked, *earlier):
+        sums[g] = add(after(mine, *earlier), *parts[g], stacked)
+        return sums[g] if stacked else sums[g][-1]
+
+    own_c = core_move(own)
+    x0 = x_move(own)
+    z1 = z_move(own, 1)
+    z3 = z_move(own, 3)
+    t = up_step(0, [own, own_c])
+
+    columns = kv_proj.shape[1]
+    proj = after(kv_proj, t)
+    halves = proj.reshape(-1, columns // HD, 2, HD // 2)
+    turned = jnp.stack([-halves[:, :, 1], halves[:, :, 0]], axis=2).reshape(kv_proj.shape)
+    kv_own, kv_other = own_first(jnp.concatenate([proj, turned], axis=1))
+    kv_own, kv_other = lax.optimization_barrier((kv_own, kv_other))
+
+    t = act_step(0, t, kv_own, kv_other)
+    x0_c = core_move(x0)
+    t = up_step(1, [x0, x0_c], t)
+    x13 = x_move(stack(after(z1, t), z3))
+    z1_c, z3_c = core_move(z1), core_move(z3)
+    z2 = z_move(z1, 1)
+    t = up_step(2, [z1, z3, z1_c, z3_c], t)
+    t = down_step(0, t)
+    t = act_step(1, t)
+
+    lens, positions, cache = lax.optimization_barrier((prompt_lens, decode_pos, kv_cache, t))[:3]
+    pages = page_list(my_dev, kv_cache.shape[0], lens, positions, page_table)
+    row_ids = my_dev * rows_here + jnp.arange(rows_here, dtype=jnp.int32)
+    position, _ = row_places(row_ids, lens, positions, page_table)
+    lane = jnp.arange(columns, dtype=jnp.int32)
+    inverse = jnp.exp(-((lane % (HD // 2)).astype(F32) * (2.0 / HD)) * jnp.log(F32(ROPE_BASE)))
+    angles = position.astype(F32)[:, None] * inverse[None, :]
+    is_key = (my_col * columns + lane < KVH * HD)[None, :]
+    cosine = jnp.where(is_key, jnp.cos(angles), 1.0)
+    sine = jnp.where(is_key, jnp.sin(angles), 0.0)
+    cache = copy_cache(cache)
+    z, x, c = my_dev // (NX * NC), my_dev // NC % NX, my_dev % NC
+    places = jnp.stack(
+        [
+            at((z + NZ - dz) % NZ, x ^ dx, c ^ dc)
+            for dz in range(NZ)
+            for dx in range(NX)
+            for dc in range(NC)
+        ]
+    ).astype(jnp.int32)
+    pages, cosine, sine, cache, places = lax.optimization_barrier(
+        (pages, cosine, sine, cache, places)
+    )
+
+    t = sum_step(0, False, t, cosine)
+    z2_c = core_move(z2)
+    x2 = x_move(z2)
+    t = down_step(1, t, z2)
+    x1_c, x3_c = core_move(x13[0]), core_move(x13[1])
+    t = up_step(3, [x13, x1_c, x3_c], t)
+    t = sum_step(1, False, t)
+    back_x0 = x_move(sums[1][0])
+    t = act_step(2, t)
+    x2_c = core_move(x2)
+    t = up_step(4, [z2, x2, z2_c, x2_c], t)
+    t = down_step(2, t)
+    t = act_step(3, t)
+    t = sum_step(2, False, t, back_x0)
+    t = down_step(3, t)
+    t = act_step(4, t)
+    t = sum_step(3, True, t)
+    back_x13 = x_move(sums[3])
+    t = down_step(4, t)
+    sum_step(4, False, t)
+    back_x2 = x_move(sums[4][1])
+    whole = lambda a, b: a.astype(F32) + b.astype(F32)
+    back_1 = z_move(whole(sums[2][0], back_x13[0]).astype(BF), 3)
+    back_3 = z_move(whole(sums[2][1], back_x13[1]).astype(BF), 1)
+    back_2 = z_move(whole(sums[4][0], back_x2).astype(BF), 2)
+    mixture = whole(sums[0][0], back_x0) + whole(back_1, back_3) + back_2.astype(F32)
+    layer_out = lax.optimization_barrier((res_f + mixture).astype(BF))
+
+    out_other = y_move(layer_out)
+    gain_other = y_move(gain_moe)
+    own_f, other_f = layer_out.astype(F32), out_other.astype(F32)
+    out_squares = jnp.sum(own_f * own_f, axis=1) + jnp.sum(other_f * other_f, axis=1)
+    scale = lax.rsqrt(out_squares / D + NORM_EPS)[:, None]
+    v_own = (own_f * scale * gain_moe[None, :]).astype(BF)
+    v_other = (other_f * scale * gain_other[None, :]).astype(BF)
+    both = dot(v_own, kv_own) + dot(v_other, kv_other)
+    rotated = (both[:, :columns] * cosine + both[:, columns:] * sine).astype(BF)
+
+    kv = {(0, 0, 0): rotated}
+    kv[1, 0, 0] = z_move(rotated, 1)
+    kv[3, 0, 0] = z_move(rotated, 3)
+    kv[2, 0, 0] = z_move(kv[1, 0, 0], 1)
+    for dz in (0, 1, 3, 2):
+        kv[dz, 1, 0] = x_move(kv[dz, 0, 0])
+        for dx in range(NX):
+            kv[dz, dx, 1] = core_move(kv[dz, dx, 0])
+    kv_blocks = [kv[dz, dx, dc] for dz in range(NZ) for dx in range(NX) for dc in range(NC)]
+    written = write_pages(places, pages, kv_blocks, cache)
+    return (layer_out, written)
+
+
 def solution(mesh):
+    body = on_device_16x2 if (mesh.shape["dp"], mesh.shape["mp"]) == (NZ * NX * NC, 2) else on_device
     placed = (
         P("dp", "mp"),
         P("dp", "mp"),
@@ -190,7 +766,7 @@
         P("dp", None, "mp"),
     )
     return jax.shard_map(
-        on_device,
+        body,
         mesh=mesh,
         in_specs=placed,
         out_specs=(P("dp", "mp"), P("dp", None, "mp")),

time: 433 us -> 221 us (0.51)
  blocking collectives: 171 us -> 0 us
  waiting for transfers between devices: 153 us -> 76.8 us
  Pallas kernels: 0 us -> 60.3 us
  starting transfers between devices: 5.88 us -> 44.6 us
  local copies, waits for them, and re-layouts: 49.3 us -> 21.8 us
  other arithmetic: 25.1 us -> 11.2 us
  between operations: 15.1 us -> 1.47 us
  matrix products: 13.1 us -> 3.15 us
    psum x1 -> x0, waiting for transfers between devices: 103 us -> none  [on_device(): summed = lax.psum(partial_value, 'mp').astype(jnp.float32)]
    ppermute x0 -> x57, waiting for transfers between devices: none -> 76.8 us  [the longest x14 36.5 us: y_move(): return lax.ppermute(value, 'mp', [(0, 1), (1, 0)])]
    all_to_all x1 -> x0, blocking collectives: 72.3 us -> none  [on_device(): lax.all_to_all(outgoing.reshape(dev_count, slots_here * capacity, width_h...]
    unnamed x1 -> x0, blocking collectives: 68.3 us -> none
    pallas_call x0 -> x24, Pallas kernels: none -> 60.3 us  [the longest x5 19.5 us: gate_up(): pl.pallas_call(functools.partial(gate_up_kernel, n), out_shape=(jax.Shape...]
    all_to_all x1 -> x0, waiting for transfers between devices: 50.3 us -> none  [on_device(): lax.all_to_all(outbound, 'dp', split_axis=0, concat_axis=0, tiled=True)]
    ppermute x0 -> x57, starting transfers between devices: none -> 44.6 us  [the longest x14 17.2 us: y_move(): return lax.ppermute(value, 'mp', [(0, 1), (1, 0)])]
    scatter x2 -> x0, local copies, waits for them, and re-layouts: 27.7 us -> none  [the longest x1 18.3 us: on_device(): flat_cache.at[local_slot]]
  transfers between devices with their start and end apart: 3 -> 57, of which waited for: 2 -> 19; matrix products, arithmetic and copies ran while one was open for 1% -> 9% of each run, Pallas kernels for 0% -> 24%
where the time goes in v2:
time: 221 us; the launch traced here: 219 us
  waiting for transfers between devices  76.8 us (35%)
  Pallas kernels  60.3 us (27%)
  starting transfers between devices  44.6 us (20%)
  local copies, waits for them, and re-layouts  21.8 us (10%)
  other arithmetic  11.2 us (5%)
  matrix products  3.15 us (1%)
    ppermute x14, waiting for transfers between devices, y_move(): return lax.ppermute(value, 'mp', [(0, 1), (1, 0)])  36.5 us
    ppermute x9, waiting for transfers between devices, z_move(): return lax.ppermute(value, 'dp', moves(dz, 0, 0))  28.9 us
    pallas_call x5, Pallas kernels, gate_up(): pl.pallas_call(functools.partial(gate_up_kernel, n), out_shape=(jax.Shape...  19.5 us
    unnamed x70, local copies, waits for them, and re-layouts  19 us
    ppermute x14, starting transfers between devices, y_move(): return lax.ppermute(value, 'mp', [(0, 1), (1, 0)])  17.2 us
    pallas_call x5, Pallas kernels, down(): pl.pallas_call(down_kernel, out_shape=[jax.ShapeDtypeStruct((tokens, widt...  14 us
    ppermute x9, starting transfers between devices, z_move(): return lax.ppermute(value, 'dp', moves(dz, 0, 0))  11.6 us
    ppermute x10, starting transfers between devices, x_move(): return lax.ppermute(value, 'dp', moves(0, 1, 0))  10.9 us
  transfers between devices with their start and end apart: 57, of which 19 were waited for; matrix products, arithmetic and copies ran while one was open for 9% of the time, Pallas kernels for 24%

profile of v2, /device:TPU:0, one launch (start us, length us, event | category | flops | bytes accessed | tf_op | source)
XLA Modules:
  0.0 219.4 jit_solution(13968923371151852705)
XLA Ops:
  0.6 3.1 %collective-permute-start = (bf16[192,768]{1,0:T(8,128)(2,1)}, bf16[192,768]{1,0:T(8,128)(2,1)}, u32[]{:S(2)}, u32[]{:S(2)}) collective-permute-start(bf16[192,768]{1,0:T(8,128)(2,1)} %param.14), channel_id=1, source_target_pairs={{0,1},{1,0},{2,3},{3,2},{4,5},{5,4},{6,7},{7,6},{8,9},{9,8},{10,11... | collective-permute-start | bytes 884744 | tf_op jit(solution)/shard_map/ppermute | solution.py:214
  5.7 5.4 %copy.31 = bf16[3,768,2,512]{3,1,0,2:T(8,128)(2,1)} copy(bf16[3,768,2,512]{3,2,1,0:T(2,128)(2,1)} %param.20) | data formatting | bytes 9437184 | tf_op args[6]
  14.4 2.4 %collective-permute-done.1 = f32[192]{0:T(256)S(1)} collective-permute-done((f32[192]{0:T(256)S(1)}, f32[192]{0:T(256)S(1)}, u32[]{:S(2)}, u32[]{:S(2)}) %collective-permute-start.1) | collective-permute-done | bytes 800 | tf_op jit(solution)/shard_map/ppermute | solution.py:214
  22.4 2.3 %copy-done.1 = bf16[3,768,2,512]{3,1,0,2:T(8,128)(2,1)S(1)} copy-done((bf16[3,768,2,512]{3,1,0,2:T(8,128)(2,1)S(1)}, bf16[3,768,2,512]{3,1,0,2:T(8,128)(2,1)}, u32[]{:S(2)}) %copy-start.1) | copy-done | bytes 4718616
  24.8 3.4 %gate_up.5 = (bf16[3,40,1024]{2,1,0:T(8,128)(2,1)}, f32[3,40,1024]{2,1,0:T(8,128)S(1)}, f32[2,8,192]{2,1,0:T(8,128)S(1)}) custom-call(s32[2]{0:T(128)S(1)} %pad_add_fusion.mine_ref.col_ref, bf16[2,3,768,512]{3,2,1,0:T(8,128)(2,1)S(1)} %bitcast.62, bf16[208,768]{1,0:T(8,128)(2,1)S(1)} %pad_maximum_fusion.1.refs_0_, ...), custom_call_target="tpu_custom_call" | custom-call | flops 1 | bytes 1 | tf_op jit(solution)/shard_map/gate_up/pallas_call | solution.py:277
  28.9 2.6 %copy.27 = bf16[1536,512]{0,1:T(8,128)(2,1)} copy(bf16[1536,512]{1,0:T(8,128)(2,1)} %param.23) | data formatting | bytes 3145728 | tf_op jit(solution)/shard_map/optimization_barrier | solution.py:218
  40.1 2.3 %copy-done.2 = bf16[3,768,2,512]{3,1,0,2:T(8,128)(2,1)S(1)} copy-done((bf16[3,768,2,512]{3,1,0,2:T(8,128)(2,1)S(1)}, bf16[3,768,2,512]{3,1,0,2:T(8,128)(2,1)}, u32[]{:S(2)}) %copy-start.2) | copy-done | bytes 4718616
  42.5 4.2 %gate_up.6 = (bf16[3,40,1024]{2,1,0:T(8,128)(2,1)}, f32[3,40,1024]{2,1,0:T(8,128)S(1)}, f32[2,8,192]{2,1,0:T(8,128)S(1)}) custom-call(s32[2]{0:T(128)S(1)} %pad_add_fusion.mine_ref.col_ref, bf16[2,3,768,512]{3,2,1,0:T(8,128)(2,1)S(1)} %bitcast.63, bf16[208,768]{1,0:T(8,128)(2,1)} %collective-permute-done.4.refs_0_, ...), custom_call_target="tpu_custom_call" | custom-call | flops 1 | bytes 1 | tf_op jit(solution)/shard_map/gate_up/pallas_call | solution.py:277
  53.9 2.3 %copy-done.3 = bf16[3,768,2,512]{3,1,0,2:T(8,128)(2,1)S(1)} copy-done((bf16[3,768,2,512]{3,1,0,2:T(8,128)(2,1)S(1)}, bf16[3,768,2,512]{3,1,0,2:T(8,128)(2,1)}, u32[]{:S(2)}) %copy-start.3) | copy-done | bytes 4718616
  57.2 4.8 %gate_up.7 = (bf16[3,80,1024]{2,1,0:T(8,128)(2,1)}, f32[3,80,1024]{2,1,0:T(8,128)S(1)}, f32[4,8,192]{2,1,0:T(8,128)S(1)}) custom-call(s32[2]{0:T(128)S(1)} %pad_add_fusion.mine_ref.col_ref, bf16[2,3,768,512]{3,2,1,0:T(8,128)(2,1)S(1)} %bitcast.64, bf16[208,768]{1,0:T(8,128)(2,1)S(1)} %collective-permute-done.6.refs_0_.a_ref, ...), custom_call_target="tpu_custom_call" | custom-call | flops 1 | bytes 1 | tf_op jit(solution)/shard_map/gate_up/pallas_call | solution.py:277
  64.8 3.9 %down.5 = (bf16[192,768]{1,0:T(8,128)(2,1)S(1)}, bf16[192,768]{1,0:T(8,128)(2,1)}) custom-call(s32[2]{0:T(128)S(1)} %pad_add_fusion.mine_ref.col_ref, f32[2,8,192]{2,1,0:T(8,128)S(1)} %get-tuple-element.79.info_ref, bf16[3,40,512]{2,1,0:T(8,128)(2,1)S(1)} %activate.5.mine_ref, bf16[3,40,512]{2,1,0:T(8,128)(2,1)} %collective-permute-done.10.got_ref, ...), custom_call_target="tpu_custom_call" | custom-call | flops 1 | bytes 1 | tf_op jit(solution)/shard_map/down/pallas_call | solution.py:372
  68.8 2.5 %activate.6.mine_ref = bf16[3,40,512]{2,1,0:T(8,128)(2,1)S(1)} custom-call(s32[2]{0:T(128)S(1)} %pad_add_fusion.mine_ref.col_ref, f32[2,8,192]{2,1,0:T(8,128)S(1)} %get-tuple-element.88.info_ref, f32[3,40,1024]{2,1,0:T(8,128)S(1)} %copy-done.10, bf16[3,40,1024]{2,1,0:T(8,128)(2,1)} %collective-permute-done.11.got_ref), custom_call_target="tpu_custom_call" | custom-call | flops 1 | bytes 1 | tf_op jit(solution)/shard_map/activate/pallas_call | solution.py:319
  78.1 2.7 %copy_cache.1.refs_16_ = bf16[24,128,512]{2,1,0:T(8,128)(2,1)} custom-call(bf16[24,128,512]{2,1,0:T(8,128)(2,1)S(1)} %copy-done.6), custom_call_target="tpu_custom_call" | custom-call | flops 1 | bytes 1 | tf_op jit(solution)/shard_map/copy_cache/pallas_call | solution.py:440
  80.7 3.0 %page_list.1.page_ref = s32[8,24]{1,0:T(8,128)S(1)} custom-call(s32[2]{0:T(128)S(1)} %pad_add_fusion.1.dev_ref, s32[16]{0:T(128)S(1)} %copy-done.17, s32[32]{0:T(128)S(1)} %copy-done.18, s32[48,8]{1,0:T(8,128)S(1)} %copy.28.table_ref), custom_call_target="tpu_custom_call" | custom-call | flops 1 | bytes 1 | tf_op jit(solution)/shard_map/page_list/pallas_call | solution.py:494
  84.4 3.2 %down.6 = (bf16[192,768]{1,0:T(8,128)(2,1)S(1)}, bf16[192,768]{1,0:T(8,128)(2,1)S(1)}) custom-call(s32[2]{0:T(128)S(1)} %pad_add_fusion.mine_ref.col_ref, f32[2,8,192]{2,1,0:T(8,128)S(1)} %get-tuple-element.88.info_ref, bf16[3,40,512]{2,1,0:T(8,128)(2,1)S(1)} %activate.6.mine_ref, bf16[3,40,512]{2,1,0:T(8,128)(2,1)} %collective-permute-done.14.got_ref, ...), custom_call_target="tpu_custom_call" | custom-call | flops 1 | bytes 1 | tf_op jit(solution)/shard_map/down/pallas_call | solution.py:372
  87.9 3.0 %gate_up.8 = (bf16[3,80,1024]{2,1,0:T(8,128)(2,1)S(1)}, f32[3,80,1024]{2,1,0:T(8,128)S(1)}, f32[4,8,192]{2,1,0:T(8,128)S(1)}) custom-call(s32[2]{0:T(128)S(1)} %pad_add_fusion.mine_ref.col_ref, bf16[2,3,768,512]{3,2,1,0:T(8,128)(2,1)S(1)} %bitcast.67, bf16[2,208,768]{2,1,0:T(8,128)(2,1)S(1)} %collective-permute-done.15.refs_0_, ...), custom_call_target="tpu_custom_call" | custom-call | flops 1 | bytes 1 | tf_op jit(solution)/shard_map/gate_up/pallas_call | solution.py:277
  93.4 2.8 %activate.7.mine_ref = bf16[3,80,512]{2,1,0:T(8,128)(2,1)S(1)} custom-call(s32[2]{0:T(128)S(1)} %pad_add_fusion.mine_ref.col_ref, f32[4,8,192]{2,1,0:T(8,128)S(1)} %get-tuple-element.104.info_ref, f32[3,80,1024]{2,1,0:T(8,128)S(1)} %copy-done.8, bf16[3,80,1024]{2,1,0:T(8,128)(2,1)} %collective-permute-done.20.got_ref), custom_call_target="tpu_custom_call" | custom-call | flops 1 | bytes 1 | tf_op jit(solution)/shard_map/activate/pallas_call | solution.py:319
  97.6 4.0 %gate_up.9 = (bf16[3,80,1024]{2,1,0:T(8,128)(2,1)S(1)}, f32[3,80,1024]{2,1,0:T(8,128)S(1)}, f32[4,8,192]{2,1,0:T(8,128)S(1)}) custom-call(s32[2]{0:T(128)S(1)} %pad_add_fusion.mine_ref.col_ref, bf16[2,3,768,512]{3,2,1,0:T(8,128)(2,1)S(1)} %bitcast.68, bf16[208,768]{1,0:T(8,128)(2,1)} %collective-permute-done.13.refs_0_, ...), custom_call_target="tpu_custom_call" | custom-call | flops 1 | bytes 1 | tf_op jit(solution)/shard_map/gate_up/pallas_call | solution.py:277
  101.6 8.1 %collective-permute-done.24.got_ref = bf16[3,80,512]{2,1,0:T(8,128)(2,1)S(1)} collective-permute-done((bf16[3,80,512]{2,1,0:T(8,128)(2,1)S(1)}, bf16[3,80,512]{2,1,0:T(8,128)(2,1)S(1)}, u32[]{:S(2)}, u32[]{:S(2)}) %collective-permute-start.24) | collective-permute-done | bytes 245792 | tf_op jit(solution)/shard_map/ppermute | solution.py:214
  116.5 6.1 %collective-permute-done.28.got_ref = bf16[3,80,512]{2,1,0:T(8,128)(2,1)S(1)} collective-permute-done((bf16[3,80,512]{2,1,0:T(8,128)(2,1)S(1)}, bf16[3,80,512]{2,1,0:T(8,128)(2,1)S(1)}, u32[]{:S(2)}, u32[]{:S(2)}) %collective-permute-start.28) | collective-permute-done | bytes 245792 | tf_op jit(solution)/shard_map/ppermute | solution.py:214
  125.5 6.8 %collective-permute-done.29.got_ref = bf16[3,80,1024]{2,1,0:T(8,128)(2,1)S(1)} collective-permute-done((bf16[3,80,1024]{2,1,0:T(8,128)(2,1)S(1)}, bf16[3,80,1024]{2,1,0:T(8,128)(2,1)S(1)}, u32[]{:S(2)}, u32[]{:S(2)}) %collective-permute-start.29) | collective-permute-done | bytes 491552 | tf_op jit(solution)/shard_map/ppermute | solution.py:214
  135.9 5.6 %collective-permute-done.35.got_ref = bf16[3,80,512]{2,1,0:T(8,128)(2,1)S(1)} collective-permute-done((bf16[3,80,512]{2,1,0:T(8,128)(2,1)S(1)}, bf16[3,80,512]{2,1,0:T(8,128)(2,1)S(1)}, u32[]{:S(2)}, u32[]{:S(2)}) %collective-permute-start.35) | collective-permute-done | bytes 245792 | tf_op jit(solution)/shard_map/ppermute | solution.py:214
  148.8 2.7 %collective-permute-start.33 = (bf16[192,768]{1,0:T(8,128)(2,1)S(1)}, bf16[192,768]{1,0:T(8,128)(2,1)S(1)}, u32[]{:S(2)}, u32[]{:S(2)}) collective-permute-start(bf16[192,768]{1,0:T(8,128)(2,1)S(1)} %get-tuple-element.146), channel_id=1, source_target_pairs={{0,24},{2,26},{4,28},{6,30},{8,0},{10,2},{12,4},{14,6},{16,8},{18,... | collective-permute-start | bytes 884744 | tf_op jit(solution)/shard_map/ppermute | solution.py:202
  151.5 4.2 %collective-permute-done.38 = bf16[192,768]{1,0:T(8,128)(2,1)S(1)} collective-permute-done((bf16[192,768]{1,0:T(8,128)(2,1)S(1)}, bf16[192,768]{1,0:T(8,128)(2,1)S(1)}, u32[]{:S(2)}, u32[]{:S(2)}) %collective-permute-start.38) | collective-permute-done | bytes 294944 | tf_op jit(solution)/shard_map/ppermute | solution.py:206
  158.9 6.9 %collective-permute-done.34 = bf16[192,768]{1,0:T(8,128)(2,1)S(1)} collective-permute-done((bf16[192,768]{1,0:T(8,128)(2,1)S(1)}, bf16[192,768]{1,0:T(8,128)(2,1)S(1)}, u32[]{:S(2)}, u32[]{:S(2)}) %collective-permute-start.34) | collective-permute-done | bytes 294944 | tf_op jit(solution)/shard_map/ppermute | solution.py:202
  165.8 10.8 %collective-permute-done.39 = bf16[192,768]{1,0:T(8,128)(2,1)S(1)} collective-permute-done((bf16[192,768]{1,0:T(8,128)(2,1)S(1)}, bf16[192,768]{1,0:T(8,128)(2,1)S(1)}, u32[]{:S(2)}, u32[]{:S(2)}) %collective-permute-start.39) | collective-permute-done | bytes 294944 | tf_op jit(solution)/shard_map/ppermute | solution.py:202
  179.1 6.4 %collective-permute-done.40 = bf16[192,768]{1,0:T(8,128)(2,1)S(1)} collective-permute-done((bf16[192,768]{1,0:T(8,128)(2,1)S(1)}, bf16[192,768]{1,0:T(8,128)(2,1)S(1)}, u32[]{:S(2)}, u32[]{:S(2)}) %collective-permute-start.40) | collective-permute-done | bytes 294944 | tf_op jit(solution)/shard_map/ppermute | solution.py:214
  187.3 3.8 %collective-permute-start.53 = (bf16[192,512]{1,0:T(8,128)(2,1)S(1)}, bf16[192,512]{1,0:T(8,128)(2,1)S(1)}, u32[]{:S(2)}, u32[]{:S(2)}) collective-permute-start(bf16[192,512]{1,0:T(8,128)(2,1)S(1)} %fusion.22.refs_0_), channel_id=1, source_target_pairs={{0,24},{2,26},{4,28},{6,30},{8,0},{10,2},{12,4},{14,6},{16,8},{18,... | collective-permute-start | bytes 589832 | tf_op jit(solution)/shard_map/ppermute | solution.py:202
  192.4 4.4 %collective-permute-done.45.refs_4_ = bf16[192,512]{1,0:T(8,128)(2,1)S(1)} collective-permute-done((bf16[192,512]{1,0:T(8,128)(2,1)S(1)}, bf16[192,512]{1,0:T(8,128)(2,1)S(1)}, u32[]{:S(2)}, u32[]{:S(2)}) %collective-permute-start.45) | collective-permute-done | bytes 196640 | tf_op jit(solution)/shard_map/ppermute | solution.py:202
  199.4 4.9 %collective-permute-done.49.refs_8_ = bf16[192,512]{1,0:T(8,128)(2,1)S(1)} collective-permute-done((bf16[192,512]{1,0:T(8,128)(2,1)S(1)}, bf16[192,512]{1,0:T(8,128)(2,1)S(1)}, u32[]{:S(2)}, u32[]{:S(2)}) %collective-permute-start.49) | collective-permute-done | bytes 196640 | tf_op jit(solution)/shard_map/ppermute | solution.py:202
  207.6 2.3 %collective-permute-done.51.refs_10_ = bf16[192,512]{1,0:T(8,128)(2,1)S(1)} collective-permute-done((bf16[192,512]{1,0:T(8,128)(2,1)S(1)}, bf16[192,512]{1,0:T(8,128)(2,1)S(1)}, u32[]{:S(2)}, u32[]{:S(2)}) %collective-permute-start.51) | collective-permute-done | bytes 196640 | tf_op jit(solution)/shard_map/ppermute | solution.py:206
  211.4 7.8 %write_pages.1 = bf16[24,128,512]{2,1,0:T(8,128)(2,1)} custom-call(s32[16]{0:T(128)S(1)} %stack.93.place_ref, s32[8,24]{1,0:T(8,128)S(1)} %page_list.1.page_ref, bf16[192,512]{1,0:T(8,128)(2,1)S(1)} %fusion.22.refs_0_, bf16[192,512]{1,0:T(8,128)(2,1)S(1)} %collective-permute-done.42.refs_1_, ...), custom_call_target="tpu_custom_call", output_to_operand_aliasing={{}: (18, {})} | custom-call | flops 1 | bytes 1 | tf_op jit(solution)/shard_map/write_pages/pallas_call | solution.py:553
  (216 shorter events, 79.1 us)
Async XLA Ops:
  0.6 10.9 %collective-permute-start = (bf16[192,768]{1,0:T(8,128)(2,1)}, bf16[192,768]{1,0:T(8,128)(2,1)}, u32[]{:S(2)}, u32[]{:S(2)}) collective-permute-start(bf16[192,768]{1,0:T(8,128)(2,1)} %param.14), channel_id=1, source_target_pairs={{0,1},{1,0},{2,3},{3,2},{4,5},{5,4},{6,7},{7,6},{8,9},{9,8},{10,11... | collective-permute-start | bytes 884744 | tf_op jit(solution)/shard_map/ppermute | solution.py:214
  17.1 17.1 %collective-permute-start.4 = (bf16[208,768]{1,0:T(8,128)(2,1)S(1)}, bf16[208,768]{1,0:T(8,128)(2,1)}, u32[]{:S(2)}, u32[]{:S(2)}) collective-permute-start(bf16[208,768]{1,0:T(8,128)(2,1)S(1)} %pad_maximum_fusion.1.refs_0_), channel_id=1, source_target_pairs={{0,4},{2,6},{4,0},{6,2},{8,12},{10,14},{12,8},{14,10},{16,20},{18,... | collective-permute-start | bytes 958472 | tf_op jit(solution)/shard_map/ppermute | solution.py:206
  18.6 19.0 %collective-permute-start.6 = (bf16[208,768]{1,0:T(8,128)(2,1)S(1)}, bf16[208,768]{1,0:T(8,128)(2,1)S(1)}, u32[]{:S(2)}, u32[]{:S(2)}) collective-permute-start(bf16[208,768]{1,0:T(8,128)(2,1)S(1)} %pad_maximum_fusion.1.refs_0_), channel_id=1, source_target_pairs={{0,8},{2,10},{4,12},{6,14},{8,16},{10,18},{12,20},{14,22},{16,24},... | collective-permute-start | bytes 958472 | tf_op jit(solution)/shard_map/ppermute | solution.py:202
  20.2 17.9 %collective-permute-start.7 = (bf16[208,768]{1,0:T(8,128)(2,1)S(1)}, bf16[208,768]{1,0:T(8,128)(2,1)}, u32[]{:S(2)}, u32[]{:S(2)}) collective-permute-start(bf16[208,768]{1,0:T(8,128)(2,1)S(1)} %pad_maximum_fusion.1.refs_0_), channel_id=1, source_target_pairs={{0,24},{2,26},{4,28},{6,30},{8,0},{10,2},{12,4},{14,6},{16,8},{18,... | collective-permute-start | bytes 958472 | tf_op jit(solution)/shard_map/ppermute | solution.py:202
  37.6 15.1 %collective-permute-start.8 = (bf16[208,768]{1,0:T(8,128)(2,1)S(1)}, bf16[208,768]{1,0:T(8,128)(2,1)S(1)}, u32[]{:S(2)}, u32[]{:S(2)}) collective-permute-start(bf16[208,768]{1,0:T(8,128)(2,1)S(1)} %collective-permute-done.6.refs_0_.a_ref), channel_id=1, source_target_pairs={{0,2},{2,0},{4,6},{6,4},{8,10},{10,8},{12,14},{14,12},{16,18},{18,... | collective-permute-start | bytes 958472 | tf_op jit(solution)/shard_map/ppermute | solution.py:210
  38.1 25.3 %collective-permute-start.13 = (bf16[208,768]{1,0:T(8,128)(2,1)S(1)}, bf16[208,768]{1,0:T(8,128)(2,1)}, u32[]{:S(2)}, u32[]{:S(2)}) collective-permute-start(bf16[208,768]{1,0:T(8,128)(2,1)S(1)} %collective-permute-done.6.refs_0_.a_ref), channel_id=1, source_target_pairs={{0,8},{2,10},{4,12},{6,14},{8,16},{10,18},{12,20},{14,22},{16,24},... | collective-permute-start | bytes 958472 | tf_op jit(solution)/shard_map/ppermute | solution.py:202
  38.1 15.8 %collective-permute-start.9 = (bf16[208,768]{1,0:T(8,128)(2,1)}, bf16[208,768]{1,0:T(8,128)(2,1)}, u32[]{:S(2)}, u32[]{:S(2)}) collective-permute-start(bf16[208,768]{1,0:T(8,128)(2,1)} %collective-permute-done.7.refs_1_.b_ref), channel_id=1, source_target_pairs={{0,2},{2,0},{4,6},{6,4},{8,10},{10,8},{12,14},{14,12},{16,18},{18,... | collective-permute-start | bytes 958472 | tf_op jit(solution)/shard_map/ppermute | solution.py:210
  47.5 21.3 %collective-permute-start.11 = (bf16[3,40,1024]{2,1,0:T(8,128)(2,1)}, bf16[3,40,1024]{2,1,0:T(8,128)(2,1)}, u32[]{:S(2)}, u32[]{:S(2)}) collective-permute-start(bf16[3,40,1024]{2,1,0:T(8,128)(2,1)} %get-tuple-element.89), channel_id=1, source_target_pairs={{0,1},{1,0},{2,3},{3,2},{4,5},{5,4},{6,7},{7,6},{8,9},{9,8},{10,11... | collective-permute-start | bytes 737288 | tf_op jit(solution)/shard_map/ppermute | solution.py:214
  49.2 15.7 %collective-permute-start.10 = (bf16[3,40,512]{2,1,0:T(8,128)(2,1)S(1)}, bf16[3,40,512]{2,1,0:T(8,128)(2,1)}, u32[]{:S(2)}, u32[]{:S(2)}) collective-permute-start(bf16[3,40,512]{2,1,0:T(8,128)(2,1)S(1)} %activate.5.mine_ref), channel_id=1, source_target_pairs={{0,1},{1,0},{2,3},{3,2},{4,5},{5,4},{6,7},{7,6},{8,9},{9,8},{10,11... | collective-permute-start | bytes 368648 | tf_op jit(solution)/shard_map/ppermute | solution.py:214
  53.4 20.7 %collective-permute-start.15 = (bf16[2,208,768]{2,1,0:T(8,128)(2,1)}, bf16[2,208,768]{2,1,0:T(8,128)(2,1)S(1)}, u32[]{:S(2)}, u32[]{:S(2)}) collective-permute-start(bf16[2,208,768]{2,1,0:T(8,128)(2,1)} %stack.94), channel_id=1, source_target_pairs={{0,4},{2,6},{4,0},{6,2},{8,12},{10,14},{12,8},{14,10},{16,20},{18,... | collective-permute-start | bytes 1916936 | tf_op jit(solution)/shard_map/ppermute | solution.py:206
  62.1 31.3 %collective-permute-start.20 = (bf16[3,80,1024]{2,1,0:T(8,128)(2,1)}, bf16[3,80,1024]{2,1,0:T(8,128)(2,1)}, u32[]{:S(2)}, u32[]{:S(2)}) collective-permute-start(bf16[3,80,1024]{2,1,0:T(8,128)(2,1)} %get-tuple-element.105), channel_id=1, source_target_pairs={{0,1},{1,0},{2,3},{3,2},{4,5},{5,4},{6,7},{7,6},{8,9},{9,8},{10,11... | collective-permute-start | bytes 1474568 | tf_op jit(solution)/shard_map/ppermute | solution.py:214
  63.4 28.9 %collective-permute-start.21 = (bf16[208,768]{1,0:T(8,128)(2,1)}, bf16[208,768]{1,0:T(8,128)(2,1)}, u32[]{:S(2)}, u32[]{:S(2)}) collective-permute-start(bf16[208,768]{1,0:T(8,128)(2,1)} %collective-permute-done.13.refs_0_), channel_id=1, source_target_pairs={{0,4},{2,6},{4,0},{6,2},{8,12},{10,14},{12,8},{14,10},{16,20},{18,... | collective-permute-start | bytes 958472 | tf_op jit(solution)/shard_map/ppermute | solution.py:206
  71.3 13.0 %collective-permute-start.14 = (bf16[3,40,512]{2,1,0:T(8,128)(2,1)S(1)}, bf16[3,40,512]{2,1,0:T(8,128)(2,1)}, u32[]{:S(2)}, u32[]{:S(2)}) collective-permute-start(bf16[3,40,512]{2,1,0:T(8,128)(2,1)S(1)} %activate.6.mine_ref), channel_id=1, source_target_pairs={{0,1},{1,0},{2,3},{3,2},{4,5},{5,4},{6,7},{7,6},{8,9},{9,8},{10,11... | collective-permute-start | bytes 368648 | tf_op jit(solution)/shard_map/ppermute | solution.py:214
  74.1 13.8 %collective-permute-start.16 = (bf16[208,768]{1,0:T(8,128)(2,1)S(1)}, bf16[208,768]{1,0:T(8,128)(2,1)S(1)}, u32[]{:S(2)}, u32[]{:S(2)}) collective-permute-start(bf16[208,768]{1,0:T(8,128)(2,1)S(1)} %get-tuple-element.145), channel_id=1, source_target_pairs={{0,2},{2,0},{4,6},{6,4},{8,10},{10,8},{12,14},{14,12},{16,18},{18,... | collective-permute-start | bytes 958472 | tf_op jit(solution)/shard_map/ppermute | solution.py:210
  74.4 13.5 %collective-permute-start.17 = (bf16[208,768]{1,0:T(8,128)(2,1)S(1)}, bf16[208,768]{1,0:T(8,128)(2,1)S(1)}, u32[]{:S(2)}, u32[]{:S(2)}) collective-permute-start(bf16[208,768]{1,0:T(8,128)(2,1)S(1)} %get-tuple-element.144), channel_id=1, source_target_pairs={{0,2},{2,0},{4,6},{6,4},{8,10},{10,8},{12,14},{14,12},{16,18},{18,... | collective-permute-start | bytes 958472 | tf_op jit(solution)/shard_map/ppermute | solution.py:210
  91.0 21.6 %collective-permute-start.25 = (bf16[3,80,1024]{2,1,0:T(8,128)(2,1)S(1)}, bf16[3,80,1024]{2,1,0:T(8,128)(2,1)S(1)}, u32[]{:S(2)}, u32[]{:S(2)}) collective-permute-start(bf16[3,80,1024]{2,1,0:T(8,128)(2,1)S(1)} %get-tuple-element.112), channel_id=1, source_target_pairs={{0,1},{1,0},{2,3},{3,2},{4,5},{5,4},{6,7},{7,6},{8,9},{9,8},{10,11... | collective-permute-start | bytes 1474568 | tf_op jit(solution)/shard_map/ppermute | solution.py:214
  96.2 13.6 %collective-permute-start.24 = (bf16[3,80,512]{2,1,0:T(8,128)(2,1)S(1)}, bf16[3,80,512]{2,1,0:T(8,128)(2,1)S(1)}, u32[]{:S(2)}, u32[]{:S(2)}) collective-permute-start(bf16[3,80,512]{2,1,0:T(8,128)(2,1)S(1)} %activate.7.mine_ref), channel_id=1, source_target_pairs={{0,1},{1,0},{2,3},{3,2},{4,5},{5,4},{6,7},{7,6},{8,9},{9,8},{10,11... | collective-permute-start | bytes 737288 | tf_op jit(solution)/shard_map/ppermute | solution.py:214
  97.1 18.8 %collective-permute-start.19 = (bf16[192,768]{1,0:T(8,128)(2,1)S(1)}, bf16[192,768]{1,0:T(8,128)(2,1)S(1)}, u32[]{:S(2)}, u32[]{:S(2)}) collective-permute-start(bf16[192,768]{1,0:T(8,128)(2,1)S(1)} %add.463), channel_id=1, source_target_pairs={{0,4},{2,6},{4,0},{6,2},{8,12},{10,14},{12,8},{14,10},{16,20},{18,... | collective-permute-start | bytes 884744 | tf_op jit(solution)/shard_map/ppermute | solution.py:206
  113.7 8.9 %collective-permute-start.28 = (bf16[3,80,512]{2,1,0:T(8,128)(2,1)S(1)}, bf16[3,80,512]{2,1,0:T(8,128)(2,1)S(1)}, u32[]{:S(2)}, u32[]{:S(2)}) collective-permute-start(bf16[3,80,512]{2,1,0:T(8,128)(2,1)S(1)} %activate.8.mine_ref), channel_id=1, source_target_pairs={{0,1},{1,0},{2,3},{3,2},{4,5},{5,4},{6,7},{7,6},{8,9},{9,8},{10,11... | collective-permute-start | bytes 737288 | tf_op jit(solution)/shard_map/ppermute | solution.py:214
  115.0 17.3 %collective-permute-start.29 = (bf16[3,80,1024]{2,1,0:T(8,128)(2,1)S(1)}, bf16[3,80,1024]{2,1,0:T(8,128)(2,1)S(1)}, u32[]{:S(2)}, u32[]{:S(2)}) collective-permute-start(bf16[3,80,1024]{2,1,0:T(8,128)(2,1)S(1)} %get-tuple-element.123), channel_id=1, source_target_pairs={{0,1},{1,0},{2,3},{3,2},{4,5},{5,4},{6,7},{7,6},{8,9},{9,8},{10,11... | collective-permute-start | bytes 1474568 | tf_op jit(solution)/shard_map/ppermute | solution.py:214
  124.9 8.5 %collective-permute-start.30 = (bf16[192,768]{1,0:T(8,128)(2,1)S(1)}, bf16[192,768]{1,0:T(8,128)(2,1)S(1)}, u32[]{:S(2)}, u32[]{:S(2)}) collective-permute-start(bf16[192,768]{1,0:T(8,128)(2,1)S(1)} %get-tuple-element.126), channel_id=1, source_target_pairs={{0,2},{2,0},{4,6},{6,4},{8,10},{10,8},{12,14},{14,12},{16,18},{18,... | collective-permute-start | bytes 884744 | tf_op jit(solution)/shard_map/ppermute | solution.py:210
  134.1 14.5 %collective-permute-start.32 = (bf16[2,192,768]{2,1,0:T(8,128)(2,1)S(1)}, bf16[2,192,768]{2,1,0:T(8,128)(2,1)S(1)}, u32[]{:S(2)}, u32[]{:S(2)}) collective-permute-start(bf16[2,192,768]{2,1,0:T(8,128)(2,1)S(1)} %add.465), channel_id=1, source_target_pairs={{0,4},{2,6},{4,0},{6,2},{8,12},{10,14},{12,8},{14,10},{16,20},{18,... | collective-permute-start | bytes 1769480 | tf_op jit(solution)/shard_map/ppermute | solution.py:206
  146.5 9.1 %collective-permute-start.38 = (bf16[192,768]{1,0:T(8,128)(2,1)S(1)}, bf16[192,768]{1,0:T(8,128)(2,1)S(1)}, u32[]{:S(2)}, u32[]{:S(2)}) collective-permute-start(bf16[192,768]{1,0:T(8,128)(2,1)S(1)} %get-tuple-element.135), channel_id=1, source_target_pairs={{0,4},{2,6},{4,0},{6,2},{8,12},{10,14},{12,8},{14,10},{16,20},{18,... | collective-permute-start | bytes 884744 | tf_op jit(solution)/shard_map/ppermute | solution.py:206
  148.8 10.1 %collective-permute-start.33 = (bf16[192,768]{1,0:T(8,128)(2,1)S(1)}, bf16[192,768]{1,0:T(8,128)(2,1)S(1)}, u32[]{:S(2)}, u32[]{:S(2)}) collective-permute-start(bf16[192,768]{1,0:T(8,128)(2,1)S(1)} %get-tuple-element.146), channel_id=1, source_target_pairs={{0,24},{2,26},{4,28},{6,30},{8,0},{10,2},{12,4},{14,6},{16,8},{18,... | collective-permute-start | bytes 884744 | tf_op jit(solution)/shard_map/ppermute | solution.py:202
  151.5 14.3 %collective-permute-start.34 = (bf16[192,768]{1,0:T(8,128)(2,1)S(1)}, bf16[192,768]{1,0:T(8,128)(2,1)S(1)}, u32[]{:S(2)}, u32[]{:S(2)}) collective-permute-start(bf16[192,768]{1,0:T(8,128)(2,1)S(1)} %get-tuple-element.147), channel_id=1, source_target_pairs={{0,8},{2,10},{4,12},{6,14},{8,16},{10,18},{12,20},{14,22},{16,24},... | collective-permute-start | bytes 884744 | tf_op jit(solution)/shard_map/ppermute | solution.py:202
  155.8 20.8 %collective-permute-start.39 = (bf16[192,768]{1,0:T(8,128)(2,1)S(1)}, bf16[192,768]{1,0:T(8,128)(2,1)S(1)}, u32[]{:S(2)}, u32[]{:S(2)}) collective-permute-start(bf16[192,768]{1,0:T(8,128)(2,1)S(1)} %add_convert_fusion), channel_id=1, source_target_pairs={{0,16},{2,18},{4,20},{6,22},{8,24},{10,26},{12,28},{14,30},{16,0},... | collective-permute-start | bytes 884744 | tf_op jit(solution)/shard_map/ppermute | solution.py:202
  176.9 8.7 %collective-permute-start.40 = (bf16[192,768]{1,0:T(8,128)(2,1)S(1)}, bf16[192,768]{1,0:T(8,128)(2,1)S(1)}, u32[]{:S(2)}, u32[]{:S(2)}) collective-permute-start(bf16[192,768]{1,0:T(8,128)(2,1)S(1)} %fusion.16), channel_id=1, source_target_pairs={{0,1},{1,0},{2,3},{3,2},{4,5},{5,4},{6,7},{7,6},{8,9},{9,8},{10,11... | collective-permute-start | bytes 884744 | tf_op jit(solution)/shard_map/ppermute | solution.py:214
  187.3 9.6 %collective-permute-start.45 = (bf16[192,512]{1,0:T(8,128)(2,1)S(1)}, bf16[192,512]{1,0:T(8,128)(2,1)S(1)}, u32[]{:S(2)}, u32[]{:S(2)}) collective-permute-start(bf16[192,512]{1,0:T(8,128)(2,1)S(1)} %fusion.22.refs_0_), channel_id=1, source_target_pairs={{0,8},{2,10},{4,12},{6,14},{8,16},{10,18},{12,20},{14,22},{16,24},... | collective-permute-start | bytes 589832 | tf_op jit(solution)/shard_map/ppermute | solution.py:202
  187.3 10.9 %collective-permute-start.53 = (bf16[192,512]{1,0:T(8,128)(2,1)S(1)}, bf16[192,512]{1,0:T(8,128)(2,1)S(1)}, u32[]{:S(2)}, u32[]{:S(2)}) collective-permute-start(bf16[192,512]{1,0:T(8,128)(2,1)S(1)} %fusion.22.refs_0_), channel_id=1, source_target_pairs={{0,24},{2,26},{4,28},{6,30},{8,0},{10,2},{12,4},{14,6},{16,8},{18,... | collective-permute-start | bytes 589832 | tf_op jit(solution)/shard_map/ppermute | solution.py:202
  196.8 8.8 %collective-permute-start.47 = (bf16[192,512]{1,0:T(8,128)(2,1)S(1)}, bf16[192,512]{1,0:T(8,128)(2,1)S(1)}, u32[]{:S(2)}, u32[]{:S(2)}) collective-permute-start(bf16[192,512]{1,0:T(8,128)(2,1)S(1)} %collective-permute-done.45.refs_4_), channel_id=1, source_target_pairs={{0,4},{2,6},{4,0},{6,2},{8,12},{10,14},{12,8},{14,10},{16,20},{18,... | collective-permute-start | bytes 589832 | tf_op jit(solution)/shard_map/ppermute | solution.py:206
  198.2 8.8 %collective-permute-start.55 = (bf16[192,512]{1,0:T(8,128)(2,1)S(1)}, bf16[192,512]{1,0:T(8,128)(2,1)S(1)}, u32[]{:S(2)}, u32[]{:S(2)}) collective-permute-start(bf16[192,512]{1,0:T(8,128)(2,1)S(1)} %collective-permute-done.53.refs_12_), channel_id=1, source_target_pairs={{0,4},{2,6},{4,0},{6,2},{8,12},{10,14},{12,8},{14,10},{16,20},{18,... | collective-permute-start | bytes 589832 | tf_op jit(solution)/shard_map/ppermute | solution.py:206
  198.9 8.7 %collective-permute-start.46 = (bf16[192,512]{1,0:T(8,128)(2,1)S(1)}, bf16[192,512]{1,0:T(8,128)(2,1)S(1)}, u32[]{:S(2)}, u32[]{:S(2)}) collective-permute-start(bf16[192,512]{1,0:T(8,128)(2,1)S(1)} %collective-permute-done.45.refs_4_), channel_id=1, source_target_pairs={{0,2},{2,0},{4,6},{6,4},{8,10},{10,8},{12,14},{14,12},{16,18},{18,... | collective-permute-start | bytes 589832 | tf_op jit(solution)/shard_map/ppermute | solution.py:210
  (59 other events, 396.3 us)

commit v3 on v2

--- a/solution.py
+++ b/solution.py
@@ -414,19 +414,19 @@
     )(mine, *left, *right)
 
 
-def stack_kernel(a_ref, b_ref, out_ref):
-    out_ref[0] = a_ref[...]
-    out_ref[1] = b_ref[...]
-
-
-def stack(a, b):
+def stack_kernel(*refs):
+    for i, ref in enumerate(refs[:-1]):
+        refs[-1][i] = ref[...]
+
+
+def stack(*arrays):
     return pl.pallas_call(
         stack_kernel,
-        out_shape=jax.ShapeDtypeStruct((2,) + a.shape, a.dtype),
+        out_shape=jax.ShapeDtypeStruct((len(arrays),) + arrays[0].shape, arrays[0].dtype),
         cost_estimate=LIGHT,
         compiler_params=ROOM,
         name="stack",
-    )(a, b)
+    )(*arrays)
 
 
 def copy_kernel(cache_ref, out_ref):
@@ -449,9 +449,19 @@
     )(cache)
 
 
-def page_list_kernel(dev_ref, lens_ref, pos_ref, table_ref, out_ref):
-    prompts, pages_here = lens_ref.shape[0], dev_ref[1]
-    dev = dev_ref[0]
+ARRIVALS = tuple(
+    (dz, dx, dc)
+    for together in (((0, 0), (0, 1)), ((1, 0), (3, 0), (1, 1)), ((2, 0), (3, 1)), ((2, 1),))
+    for dc in range(NC)
+    for dz, dx in together
+)
+
+
+def page_list_kernel(mine_ref, lens_ref, pos_ref, table_ref, out_ref, position_ref):
+    prompts, pages_here = lens_ref.shape[0], mine_ref[3]
+    dev = mine_ref[2]
+    row = lax.broadcasted_iota(jnp.int32, position_ref.shape, 0)
+    stream = dev * PRE_DEV + row
 
     def put(found, page, base, offset, low, high, skip):
         local = page - dev * pages_here
@@ -467,6 +477,9 @@
     def prompt(q, carry):
         begin, found = carry
         length = lens_ref[q]
+        position_ref[...] = jnp.where(
+            stream >= begin, (stream - begin).astype(F32), position_ref[...]
+        )
 
         def page(k, found):
             start = begin + k * PAGE
@@ -485,33 +498,96 @@
         offset = PRE_DEV + c - base * DEC_DEV - low
         return put(found, table_ref[prompts + c, k], base, offset, low, low + 1, jnp.int32(0))
 
+    position_ref[...] = jnp.zeros(position_ref.shape, F32)
     _, found = lax.fori_loop(0, prompts, prompt, (jnp.int32(0), jnp.int32(0)))
     out_ref[6, 0] = lax.fori_loop(0, pos_ref.shape[0], decode, found)
-
-
-def page_list(my_dev, pages_here, prompt_lens, decode_pos, page_table):
+    for e in range(DEC_DEV):
+        own = pos_ref[dev * DEC_DEV + e].astype(F32)
+        position_ref[...] = jnp.where(row == PRE_DEV + e, own, position_ref[...])
+    z, x, c = lax.div(dev, NX * NC), lax.rem(lax.div(dev, NC), NX), lax.rem(dev, NC)
+    for k, (dz, dx, dc) in enumerate(ARRIVALS):
+        other_x = 1 - x if dx else x
+        other_c = 1 - c if dc else c
+        out_ref[7, k] = at(lax.rem(z + NZ - dz, NZ), other_x, other_c)
+
+
+def page_list(mine, pages_here, prompt_lens, decode_pos, page_table):
     smem = pl.BlockSpec(memory_space=pltpu.SMEM)
     return pl.pallas_call(
         page_list_kernel,
-        out_shape=jax.ShapeDtypeStruct((8, pages_here), jnp.int32),
+        out_shape=(
+            jax.ShapeDtypeStruct((8, max(pages_here, NZ * NX * NC)), jnp.int32),
+            jax.ShapeDtypeStruct((ROWS_DEV, 128), F32),
+        ),
         in_specs=[smem] * 4,
-        out_specs=smem,
+        out_specs=(smem, pl.BlockSpec(memory_space=pltpu.VMEM)),
         cost_estimate=LIGHT,
         compiler_params=ROOM,
         name="page_list",
-    )(jnp.stack([my_dev, jnp.int32(pages_here)]), prompt_lens, decode_pos, page_table)
-
-
-def page_kernel(place_ref, page_ref, *refs):
-    count = len(refs) - 7
-    cache_ref, out_ref, everything, held, kv_sem, in_sem, out_sem = refs[count:]
-    tokens = everything.shape[1]
+    )(mine, prompt_lens, decode_pos, page_table)
+
+
+def turn_kernel(mine_ref, w_ref, out_ref):
+    w = w_ref[...].astype(F32)
+    n, half = w.shape[1], HD // 2
+    lane = lax.broadcasted_iota(jnp.int32, w.shape, 1)
+    second, first = pltpu.roll(w, n - half, 1), pltpu.roll(w, half, 1)
+    out_ref[0, :, :n] = w_ref[...]
+    out_ref[0, :, n:] = jnp.where(lane % HD < half, -second, first).astype(BF)
+
+
+def turn(mine, w):
+    rows, n = w.shape
+    steps = 4
+    return pl.pallas_call(
+        turn_kernel,
+        out_shape=jax.ShapeDtypeStruct((2, rows // 2, 2 * n), BF),
+        grid_spec=pltpu.PrefetchScalarGridSpec(
+            num_scalar_prefetch=1,
+            grid=(2, steps),
+            in_specs=[pl.BlockSpec((rows // 2 // steps, n), lambda h, i, m: (h * steps + i, 0))],
+            out_specs=pl.BlockSpec(
+                (1, rows // 2 // steps, 2 * n),
+                lambda h, i, m: (h + m[0] - 2 * h * m[0], i, 0),
+            ),
+        ),
+        cost_estimate=LIGHT,
+        compiler_params=ROOM,
+        name="turn",
+    )(mine, w)
+
+
+def kv_kernel(own_ref, other_ref, gain_ref, other_gain_ref, w_ref, cos_ref, sin_ref, out_ref):
+    own, other = own_ref[...].astype(F32), other_ref[...].astype(F32)
+    squares = jnp.sum(own * own, axis=1, keepdims=True) + jnp.sum(
+        other * other, axis=1, keepdims=True
+    )
+    scale = lax.rsqrt(squares / D + NORM_EPS)
+    both = jnp.dot(
+        (own * scale * gain_ref[...]).astype(BF), w_ref[0], preferred_element_type=F32
+    ) + jnp.dot(
+        (other * scale * other_gain_ref[...]).astype(BF), w_ref[1], preferred_element_type=F32
+    )
+    n = out_ref.shape[1]
+    out_ref[...] = (both[:, :n] * cos_ref[...] + both[:, n:] * sin_ref[...]).astype(BF)
+
+
+def keys_values(own, other, gain, other_gain, w, cosine, sine):
+    return pl.pallas_call(
+        kv_kernel,
+        out_shape=jax.ShapeDtypeStruct(cosine.shape, BF),
+        cost_estimate=LIGHT,
+        compiler_params=ROOM,
+        name="keys_values",
+    )(own, other, gain[None], other_gain[None], w, cosine, sine)
+
+
+def page_kernel(page_ref, *refs):
+    *sources, cache_ref, out_ref, window, held, in_sem, out_sem = refs
+    blocks = [b for r in sources for b in ([r] if len(r.shape) == 2 else [r.at[i] for i in range(r.shape[0])])]
+    tokens = blocks[0].shape[0]
     length = held.shape[1]
     pages = page_ref[6, 0]
-    block_copies = [
-        pltpu.make_async_copy(refs[i], everything.at[place_ref[i]], kv_sem.at[i])
-        for i in range(count)
-    ]
     page_in = lambda k: pltpu.make_async_copy(
         cache_ref.at[page_ref[0, k]], held.at[k], in_sem.at[k]
     )
@@ -519,23 +595,27 @@
         held.at[k], out_ref.at[page_ref[0, k]], out_sem.at[k]
     )
     lax.fori_loop(0, pages, lambda k, x: (page_in(k).start(), x)[1], 0)
-    for copy in block_copies:
-        copy.start()
     i = lax.broadcasted_iota(jnp.int32, (length, 2 * tokens), 0)
     m = lax.broadcasted_iota(jnp.int32, (length, 2 * tokens), 1)
     row = lax.broadcasted_iota(jnp.int32, (length, 1), 0)
-    for copy in block_copies:
-        copy.wait()
 
     def step(k, carry):
         base, offset = page_ref[1, k], page_ref[2, k]
         low, high, skip = page_ref[3, k], page_ref[4, k], page_ref[5, k]
+        after_base = jnp.minimum(base + 1, len(blocks) - 1)
+        for b, block in enumerate(blocks):
+
+            @pl.when(page_ref[7, b] == base)
+            def _():
+                window[:tokens] = block[...]
+
+            @pl.when(page_ref[7, b] == after_base)
+            def _():
+                window[tokens:] = block[...]
+
         source = i + offset + jnp.where(i + offset >= PRE_DEV, skip, 0)
         select = (m == source).astype(F32).astype(BF)
-        after_base = jnp.minimum(base + 1, count - 1)
-        taken = jnp.dot(
-            select[:, :tokens], everything[base], preferred_element_type=F32
-        ) + jnp.dot(select[:, tokens:], everything[after_base], preferred_element_type=F32)
+        taken = jnp.dot(select, window[...], preferred_element_type=F32)
         hit = (row >= low) & (row < high)
         page_in(k).wait()
         held[k] = jnp.where(hit, taken, held[k].astype(F32)).astype(BF)
@@ -546,31 +626,30 @@
     lax.fori_loop(0, pages, lambda k, x: (page_out(k).wait(), x)[1], 0)
 
 
-def write_pages(place, page_data, blocks, cache):
+def write_pages(page_data, blocks, cache):
     pages, length, width = cache.shape
-    tokens = blocks[0].shape[0]
+    tokens = blocks[0].shape[-2]
     in_hbm = pl.BlockSpec(memory_space=pltpu.HBM)
     return pl.pallas_call(
         page_kernel,
         out_shape=jax.ShapeDtypeStruct(cache.shape, cache.dtype),
         grid_spec=pltpu.PrefetchScalarGridSpec(
-            num_scalar_prefetch=2,
+            num_scalar_prefetch=1,
             grid=(),
-            in_specs=[pl.BlockSpec(memory_space=pl.ANY)] * len(blocks) + [in_hbm],
+            in_specs=[pl.BlockSpec(memory_space=pltpu.VMEM)] * len(blocks) + [in_hbm],
             out_specs=in_hbm,
             scratch_shapes=[
-                pltpu.VMEM((len(blocks), tokens, width), cache.dtype),
+                pltpu.VMEM((2 * tokens, width), cache.dtype),
                 pltpu.VMEM(cache.shape, cache.dtype),
-                pltpu.SemaphoreType.DMA((len(blocks),)),
                 pltpu.SemaphoreType.DMA((pages,)),
                 pltpu.SemaphoreType.DMA((pages,)),
             ],
         ),
-        input_output_aliases={2 + len(blocks): 0},
+        input_output_aliases={1 + len(blocks): 0},
         cost_estimate=LIGHT,
         compiler_params=ROOM,
         name="write_pages",
-    )(place, page_data, *blocks, cache)
+    )(page_data, *blocks, cache)
 
 
 def on_device_16x2(
@@ -602,7 +681,9 @@
     )
 
     attn_other = y_move(attn_out)
-    weight = gate_up_w.transpose(2, 0, 1, 3)
+    mine = jnp.stack([my_col, my_dev * slots_here, my_dev, jnp.int32(kv_cache.shape[0])])
+    table = jnp.maximum(page_table, 0)
+    mine, table = lax.optimization_barrier((mine.astype(jnp.int32), table))
     proj_own, proj_other = own_first(out_proj)
     first_half = residual.astype(F32) + dot(attn_out, proj_own)
     gates = gate_weights.T
@@ -616,7 +697,7 @@
         axis=1,
     )
     meta = jnp.concatenate([names, gates], axis=0).astype(BF)
-    weight, first_half, meta = lax.optimization_barrier((weight, first_half, meta))
+    first_half, meta, attn_other = lax.optimization_barrier((first_half, meta, attn_other))
     hidden = (first_half + dot(attn_other, proj_other)).astype(BF)
     hidden = lax.optimization_barrier(hidden)
     res_f = hidden.astype(F32)
@@ -626,7 +707,6 @@
     normed = (res_f * scale * gain_attn[None, :]).astype(BF)
     own = jnp.concatenate([normed, meta], axis=0)
 
-    mine = jnp.stack([my_col, my_dev * slots_here]).astype(jnp.int32)
     infos, keeps, moving, acts, parts, sums = {}, {}, {}, {}, {}, {}
 
     def up_step(g, blocks, *earlier):
@@ -653,97 +733,82 @@
     x0 = x_move(own)
     z1 = z_move(own, 1)
     z3 = z_move(own, 3)
-    t = up_step(0, [own, own_c])
+    weight = after(gate_up_w, own).transpose(2, 0, 1, 3)
+    x0, z1 = lax.optimization_barrier((x0, z1))
+    x0_c = core_move(x0)
+    x1 = x_move(z1)
+    z1_c = core_move(z1)
+    z2 = z_move(z1, 1)
+    t = up_step(0, [own, x0, own_c, x0_c])
 
     columns = kv_proj.shape[1]
-    proj = after(kv_proj, t)
-    halves = proj.reshape(-1, columns // HD, 2, HD // 2)
-    turned = jnp.stack([-halves[:, :, 1], halves[:, :, 0]], axis=2).reshape(kv_proj.shape)
-    kv_own, kv_other = own_first(jnp.concatenate([proj, turned], axis=1))
-    kv_own, kv_other = lax.optimization_barrier((kv_own, kv_other))
-
-    t = act_step(0, t, kv_own, kv_other)
-    x0_c = core_move(x0)
-    t = up_step(1, [x0, x0_c], t)
-    x13 = x_move(stack(after(z1, t), z3))
-    z1_c, z3_c = core_move(z1), core_move(z3)
-    z2 = z_move(z1, 1)
-    t = up_step(2, [z1, z3, z1_c, z3_c], t)
-    t = down_step(0, t)
-    t = act_step(1, t)
-
-    lens, positions, cache = lax.optimization_barrier((prompt_lens, decode_pos, kv_cache, t))[:3]
-    pages = page_list(my_dev, kv_cache.shape[0], lens, positions, page_table)
-    row_ids = my_dev * rows_here + jnp.arange(rows_here, dtype=jnp.int32)
-    position, _ = row_places(row_ids, lens, positions, page_table)
+    kv_w = turn(after(mine, t), kv_proj)
+    pages, position = page_list(
+        after(mine, kv_w), kv_cache.shape[0], prompt_lens, decode_pos, table
+    )
     lane = jnp.arange(columns, dtype=jnp.int32)
     inverse = jnp.exp(-((lane % (HD // 2)).astype(F32) * (2.0 / HD)) * jnp.log(F32(ROPE_BASE)))
-    angles = position.astype(F32)[:, None] * inverse[None, :]
+    angles = position[:, :1] * inverse[None, :]
     is_key = (my_col * columns + lane < KVH * HD)[None, :]
     cosine = jnp.where(is_key, jnp.cos(angles), 1.0)
     sine = jnp.where(is_key, jnp.sin(angles), 0.0)
-    cache = copy_cache(cache)
-    z, x, c = my_dev // (NX * NC), my_dev // NC % NX, my_dev % NC
-    places = jnp.stack(
-        [
-            at((z + NZ - dz) % NZ, x ^ dx, c ^ dc)
-            for dz in range(NZ)
-            for dx in range(NX)
-            for dc in range(NC)
-        ]
-    ).astype(jnp.int32)
-    pages, cosine, sine, cache, places = lax.optimization_barrier(
-        (pages, cosine, sine, cache, places)
-    )
-
-    t = sum_step(0, False, t, cosine)
+    kv_w, pages, cosine, sine = lax.optimization_barrier((kv_w, pages, cosine, sine))
+
+    x1_c = core_move(x1)
+    t = up_step(1, [z1, x1, z1_c, x1_c], t, cosine)
+    z2 = after(z2, t)
+    x2 = x_move(z2)
     z2_c = core_move(z2)
-    x2 = x_move(z2)
-    t = down_step(1, t, z2)
-    x1_c, x3_c = core_move(x13[0]), core_move(x13[1])
-    t = up_step(3, [x13, x1_c, x3_c], t)
+    t = act_step(0, t)
+    cache = copy_cache(after(kv_cache, t))
+    x2_c = core_move(after(x2, cache))
+    t = up_step(2, [z2, x2, z2_c, x2_c], t, cache)
+    x3 = x_move(after(z3, x2))
+    t = act_step(1, t)
+    t = down_step(0, t)
+    z3_c = core_move(after(z3, t))
+    x3_c = core_move(after(x3, t))
+    t = up_step(3, [z3, x3, z3_c, x3_c], t)
+    t = sum_step(0, False, t)
+    back_x0 = x_move(t)
+    t = down_step(1, t)
+    t = act_step(2, t)
     t = sum_step(1, False, t)
-    back_x0 = x_move(sums[1][0])
-    t = act_step(2, t)
-    x2_c = core_move(x2)
-    t = up_step(4, [z2, x2, z2_c, x2_c], t)
-    t = down_step(2, t)
+    back_x1 = x_move(t)
+    t = down_step(2, t, back_x0)
+    (t,) = add(after(mine, t), sums[1][:1], [back_x1], False)
+    back_1 = z_move(t, 3)
     t = act_step(3, t)
-    t = sum_step(2, False, t, back_x0)
-    t = down_step(3, t)
-    t = act_step(4, t)
-    t = sum_step(3, True, t)
-    back_x13 = x_move(sums[3])
-    t = down_step(4, t)
-    sum_step(4, False, t)
-    back_x2 = x_move(sums[4][1])
+    t = sum_step(2, False, t)
+    back_x2 = x_move(t)
+    t = down_step(3, t, back_1)
+    (t,) = add(after(mine, t), sums[2][:1], [back_x2], False)
+    back_2 = z_move(t, 2)
+    t = sum_step(3, False, t)
+    back_x3 = x_move(t)
+    (t,) = add(after(mine, t), sums[3][:1], [back_x3], False)
+    back_3 = z_move(t, 1)
     whole = lambda a, b: a.astype(F32) + b.astype(F32)
-    back_1 = z_move(whole(sums[2][0], back_x13[0]).astype(BF), 3)
-    back_3 = z_move(whole(sums[2][1], back_x13[1]).astype(BF), 1)
-    back_2 = z_move(whole(sums[4][0], back_x2).astype(BF), 2)
     mixture = whole(sums[0][0], back_x0) + whole(back_1, back_3) + back_2.astype(F32)
     layer_out = lax.optimization_barrier((res_f + mixture).astype(BF))
 
-    out_other = y_move(layer_out)
-    gain_other = y_move(gain_moe)
-    own_f, other_f = layer_out.astype(F32), out_other.astype(F32)
-    out_squares = jnp.sum(own_f * own_f, axis=1) + jnp.sum(other_f * other_f, axis=1)
-    scale = lax.rsqrt(out_squares / D + NORM_EPS)[:, None]
-    v_own = (own_f * scale * gain_moe[None, :]).astype(BF)
-    v_other = (other_f * scale * gain_other[None, :]).astype(BF)
-    both = dot(v_own, kv_own) + dot(v_other, kv_other)
-    rotated = (both[:, :columns] * cosine + both[:, columns:] * sine).astype(BF)
-
-    kv = {(0, 0, 0): rotated}
-    kv[1, 0, 0] = z_move(rotated, 1)
-    kv[3, 0, 0] = z_move(rotated, 3)
-    kv[2, 0, 0] = z_move(kv[1, 0, 0], 1)
-    for dz in (0, 1, 3, 2):
-        kv[dz, 1, 0] = x_move(kv[dz, 0, 0])
-        for dx in range(NX):
-            kv[dz, dx, 1] = core_move(kv[dz, dx, 0])
-    kv_blocks = [kv[dz, dx, dc] for dz in range(NZ) for dx in range(NX) for dc in range(NC)]
-    written = write_pages(places, pages, kv_blocks, cache)
+    gain_other = y_move(after(gain_moe, sums[2][0]))
+    rotated = keys_values(
+        layer_out, y_move(layer_out), gain_moe, gain_other, kv_w, cosine, sine
+    )
+
+    x0 = x_move(rotated)
+    z1 = z_move(rotated, 1)
+    z3 = z_move(rotated, 3)
+    x1 = x_move(after(z1, x0))
+    z2 = z_move(z1, 1)
+    x3 = x_move(z3)
+    x2 = x_move(after(z2, x1))
+    kv_blocks = []
+    for together in ((rotated, x0), (z1, z3, x1), (z2, x3), (x2,)):
+        block = stack(*together) if len(together) > 1 else together[0]
+        kv_blocks += [block, core_move(block)]
+    written = write_pages(pages, kv_blocks, cache)
     return (layer_out, written)
 
 

time: 221 us -> 190 us (0.86)
  waiting for transfers between devices: 76.8 us -> 95.5 us
  local copies, waits for them, and re-layouts: 21.8 us -> 3.42 us
  Pallas kernels: 60.3 us -> 43.8 us
  other arithmetic: 11.2 us -> 3.57 us
  starting transfers between devices: 44.6 us -> 39.7 us
    unnamed x70 -> x25, local copies, waits for them, and re-layouts: 19 us -> 0.15 us
    ppermute x10 -> x12, waiting for transfers between devices: 8.42 us -> 23 us  [x_move(): return lax.ppermute(value, 'dp', moves(0, 1, 0))]
    pallas_call x5 -> x4, Pallas kernels: 19.5 us -> 13.3 us  [gate_up(): pl.pallas_call(functools.partial(gate_up_kernel, n), out_shape=(jax.Shape...]
    pallas_call x5 -> x4, Pallas kernels: 14 us -> 9.13 us  [down(): pl.pallas_call(down_kernel, out_shape=[jax.ShapeDtypeStruct((tokens, widt...]
    ppermute x14 -> x12, waiting for transfers between devices: 36.5 us -> 41.1 us  [y_move(): return lax.ppermute(value, 'mp', [(0, 1), (1, 0)])]
    pallas_call x1, Pallas kernels: 7.77 us -> 3.16 us  [write_pages(): pl.pallas_call(page_kernel, out_shape=jax.ShapeDtypeStruct(cache.shape, c...]
    ppermute x14 -> x12, starting transfers between devices: 17.2 us -> 13.1 us  [y_move(): return lax.ppermute(value, 'mp', [(0, 1), (1, 0)])]
    pallas_call x5 -> x4, Pallas kernels: 8.32 us -> 4.46 us  [activate(): pl.pallas_call(act_kernel, out_shape=jax.ShapeDtypeStruct((slots, rows, h...]
  transfers between devices with their start and end apart: 57 -> 53, of which waited for: 19 -> 25; matrix products, arithmetic and copies ran while one was open for 9% -> 4% of each run, Pallas kernels for 24% -> 21%
where the time goes in v3:
time: 190 us; the launch traced here: 189 us
  waiting for transfers between devices  95.5 us (50%)
  Pallas kernels  43.8 us (23%)
  starting transfers between devices  39.7 us (21%)
  other arithmetic  3.57 us (2%)
  local copies, waits for them, and re-layouts  3.42 us (2%)
    ppermute x12, waiting for transfers between devices, y_move(): return lax.ppermute(value, 'mp', [(0, 1), (1, 0)])  41.1 us
    ppermute x9, waiting for transfers between devices, z_move(): return lax.ppermute(value, 'dp', moves(dz, 0, 0))  28.9 us
    ppermute x12, waiting for transfers between devices, x_move(): return lax.ppermute(value, 'dp', moves(0, 1, 0))  23 us
    pallas_call x4, Pallas kernels, gate_up(): pl.pallas_call(functools.partial(gate_up_kernel, n), out_shape=(jax.Shape...  13.3 us
    ppermute x12, starting transfers between devices, y_move(): return lax.ppermute(value, 'mp', [(0, 1), (1, 0)])  13.1 us
    ppermute x9, starting transfers between devices, z_move(): return lax.ppermute(value, 'dp', moves(dz, 0, 0))  11.4 us
    ppermute x12, starting transfers between devices, x_move(): return lax.ppermute(value, 'dp', moves(0, 1, 0))  11 us
    pallas_call x4, Pallas kernels, down(): pl.pallas_call(down_kernel, out_shape=[jax.ShapeDtypeStruct((tokens, widt...  9.13 us
  transfers between devices with their start and end apart: 53, of which 25 were waited for; matrix products, arithmetic and copies ran while one was open for 4% of the time, Pallas kernels for 21%

profile of v3, /device:TPU:0, one launch (start us, length us, event | category | flops | bytes accessed | tf_op | source)
XLA Modules:
  0.0 189.3 jit_solution(3990899322566271620)
XLA Ops:
  0.6 3.1 %collective-permute-start = (bf16[192,768]{1,0:T(8,128)(2,1)}, bf16[192,768]{1,0:T(8,128)(2,1)S(1)}, u32[]{:S(2)}, u32[]{:S(2)}) collective-permute-start(bf16[192,768]{1,0:T(8,128)(2,1)} %param.14), channel_id=1, source_target_pairs={{0,1},{1,0},{2,3},{3,2},{4,5},{5,4},{6,7},{7,6},{8,9},{9,8},{10,11... | collective-permute-start | bytes 884744 | tf_op jit(solution)/shard_map/ppermute | solution.py:214
  6.6 4.3 %collective-permute-done = bf16[192,768]{1,0:T(8,128)(2,1)S(1)} collective-permute-done((bf16[192,768]{1,0:T(8,128)(2,1)}, bf16[192,768]{1,0:T(8,128)(2,1)S(1)}, u32[]{:S(2)}, u32[]{:S(2)}) %collective-permute-start) | collective-permute-done | bytes 294944 | tf_op jit(solution)/shard_map/ppermute | solution.py:214
  18.9 4.2 %collective-permute-done.2.refs_1_ = bf16[208,768]{1,0:T(8,128)(2,1)} collective-permute-done((bf16[208,768]{1,0:T(8,128)(2,1)S(1)}, bf16[208,768]{1,0:T(8,128)(2,1)}, u32[]{:S(2)}, u32[]{:S(2)}) %collective-permute-start.2) | collective-permute-done | bytes 319520 | tf_op jit(solution)/shard_map/ppermute | solution.py:206
  23.1 2.9 %collective-permute-done.3.refs_0_ = bf16[208,768]{1,0:T(8,128)(2,1)S(1)} collective-permute-done((bf16[208,768]{1,0:T(8,128)(2,1)S(1)}, bf16[208,768]{1,0:T(8,128)(2,1)S(1)}, u32[]{:S(2)}, u32[]{:S(2)}) %collective-permute-start.3) | collective-permute-done | bytes 319520 | tf_op jit(solution)/shard_map/ppermute | solution.py:202
  26.6 3.2 %copy.22 = bf16[3,768,2,512]{3,1,0,2:T(8,128)(2,1)S(1)} copy(bf16[3,768,2,512]{3,2,1,0:T(2,128)(2,1)} %param.20) | data formatting | bytes 9437184 | tf_op jit(solution)/shard_map/optimization_barrier | solution.py:218
  30.1 4.1 %gate_up.4 = (bf16[3,80,1024]{2,1,0:T(8,128)(2,1)S(1)}, f32[3,80,1024]{2,1,0:T(8,128)S(1)}, f32[4,8,192]{2,1,0:T(8,128)S(1)}) custom-call(s32[4]{0:T(128)S(1)} %pad_add_fusion.mine_ref.col_ref, bf16[2,3,768,512]{3,2,1,0:T(8,128)(2,1)S(1)} %bitcast.21, bf16[208,768]{1,0:T(8,128)(2,1)S(1)} %pad_maximum_fusion.refs_0_, ...), custom_call_target="tpu_custom_call" | custom-call | flops 1 | bytes 1 | tf_op jit(solution)/shard_map/gate_up/pallas_call | solution.py:277
  34.3 2.4 %turn.1.w_ref = bf16[2,768,1024]{2,1,0:T(8,128)(2,1)S(1)} custom-call(s32[4]{0:T(128)S(1)} %pad_add_fusion.mine_ref.col_ref, bf16[1536,512]{1,0:T(8,128)(2,1)S(1)} %copy-done.3), custom_call_target="tpu_custom_call" | custom-call | flops 1 | bytes 1 | tf_op jit(solution)/shard_map/turn/pallas_call | solution.py:542
  38.3 3.1 %page_list.1 = (s32[8,24]{1,0:T(8,128)S(1)}, f32[192,128]{1,0:T(8,128)S(1)}) custom-call(s32[4]{0:T(128)S(1)} %pad_add_fusion.mine_ref.col_ref, s32[16]{0:T(128)S(1)} %copy-done.5, s32[32]{0:T(128)S(1)} %copy-done.6, s32[48,8]{1,0:T(8,128)S(1)} %broadcast_maximum_fusion.table_ref), custom_call_target="tpu_custom_call" | custom-call | flops 1 | bytes 1 | tf_op jit(solution)/shard_map/page_list/pallas_call | solution.py:516
  43.1 3.0 %gate_up.5 = (bf16[3,80,1024]{2,1,0:T(8,128)(2,1)S(1)}, f32[3,80,1024]{2,1,0:T(8,128)S(1)}, f32[4,8,192]{2,1,0:T(8,128)S(1)}) custom-call(s32[4]{0:T(128)S(1)} %pad_add_fusion.mine_ref.col_ref, bf16[2,3,768,512]{3,2,1,0:T(8,128)(2,1)S(1)} %bitcast.22, bf16[208,768]{1,0:T(8,128)(2,1)S(1)} %collective-permute-done.3.refs_0_, ...), custom_call_target="tpu_custom_call" | custom-call | flops 1 | bytes 1 | tf_op jit(solution)/shard_map/gate_up/pallas_call | solution.py:277
  47.7 3.8 %collective-permute-start.16 = (bf16[208,768]{1,0:T(8,128)(2,1)S(1)}, bf16[208,768]{1,0:T(8,128)(2,1)S(1)}, u32[]{:S(2)}, u32[]{:S(2)}) collective-permute-start(bf16[208,768]{1,0:T(8,128)(2,1)S(1)} %pad_maximum_fusion.refs_0_), channel_id=1, source_target_pairs={{0,24},{2,26},{4,28},{6,30},{8,0},{10,2},{12,4},{14,6},{16,8},{18,... | collective-permute-start | bytes 958472 | tf_op jit(solution)/shard_map/ppermute | solution.py:202
  53.2 2.7 %copy_cache.1.refs_8_ = bf16[24,128,512]{2,1,0:T(8,128)(2,1)} custom-call(bf16[24,128,512]{2,1,0:T(8,128)(2,1)S(1)} %copy-done.2), custom_call_target="tpu_custom_call" | custom-call | flops 1 | bytes 1 | tf_op jit(solution)/shard_map/copy_cache/pallas_call | solution.py:440
  56.4 2.3 %collective-permute-done.16.refs_0_ = bf16[208,768]{1,0:T(8,128)(2,1)S(1)} collective-permute-done((bf16[208,768]{1,0:T(8,128)(2,1)S(1)}, bf16[208,768]{1,0:T(8,128)(2,1)S(1)}, u32[]{:S(2)}, u32[]{:S(2)}) %collective-permute-start.16) | collective-permute-done | bytes 319520 | tf_op jit(solution)/shard_map/ppermute | solution.py:202
  59.8 3.0 %gate_up.6 = (bf16[3,80,1024]{2,1,0:T(8,128)(2,1)S(1)}, f32[3,80,1024]{2,1,0:T(8,128)S(1)}, f32[4,8,192]{2,1,0:T(8,128)S(1)}) custom-call(s32[4]{0:T(128)S(1)} %pad_add_fusion.mine_ref.col_ref, bf16[2,3,768,512]{3,2,1,0:T(8,128)(2,1)S(1)} %bitcast.23, bf16[208,768]{1,0:T(8,128)(2,1)S(1)} %collective-permute-done.10.refs_0_, ...), custom_call_target="tpu_custom_call" | custom-call | flops 1 | bytes 1 | tf_op jit(solution)/shard_map/gate_up/pallas_call | solution.py:277
  62.8 2.8 %collective-permute-done.14.got_ref = bf16[3,80,1024]{2,1,0:T(8,128)(2,1)S(1)} collective-permute-done((bf16[3,80,1024]{2,1,0:T(8,128)(2,1)S(1)}, bf16[3,80,1024]{2,1,0:T(8,128)(2,1)S(1)}, u32[]{:S(2)}, u32[]{:S(2)}) %collective-permute-start.14) | collective-permute-done | bytes 491552 | tf_op jit(solution)/shard_map/ppermute | solution.py:214
  66.8 3.1 %collective-permute-done.15.got_ref = bf16[3,80,512]{2,1,0:T(8,128)(2,1)S(1)} collective-permute-done((bf16[3,80,512]{2,1,0:T(8,128)(2,1)S(1)}, bf16[3,80,512]{2,1,0:T(8,128)(2,1)S(1)}, u32[]{:S(2)}, u32[]{:S(2)}) %collective-permute-start.15) | collective-permute-done | bytes 245792 | tf_op jit(solution)/shard_map/ppermute | solution.py:214
  69.9 2.3 %down.4 = (bf16[192,768]{1,0:T(8,128)(2,1)S(1)}, bf16[192,768]{1,0:T(8,128)(2,1)S(1)}, bf16[192,768]{1,0:T(8,128)(2,1)S(1)}, bf16[192,768]{1,0:T(8,128)(2,1)S(1)}) custom-call(s32[4]{0:T(128)S(1)} %pad_add_fusion.mine_ref.col_ref, f32[4,8,192]{2,1,0:T(8,128)S(1)} %get-tuple-element.98.info_ref, bf16[3,80,512]{2,1,0:T(8,128)(2,1)S(1)} %activate.4.mine_ref, ...), custom_call_target="tpu_custom_call" | custom-call | flops 1 | bytes 1 | tf_op jit(solution)/shard_map/down/pallas_call | solution.py:372
  75.3 3.0 %gate_up.7 = (bf16[3,80,1024]{2,1,0:T(8,128)(2,1)S(1)}, f32[3,80,1024]{2,1,0:T(8,128)S(1)}, f32[4,8,192]{2,1,0:T(8,128)S(1)}) custom-call(s32[4]{0:T(128)S(1)} %pad_add_fusion.mine_ref.col_ref, bf16[2,3,768,512]{3,2,1,0:T(8,128)(2,1)S(1)} %bitcast.24, bf16[208,768]{1,0:T(8,128)(2,1)S(1)} %collective-permute-done.16.refs_0_, ...), custom_call_target="tpu_custom_call" | custom-call | flops 1 | bytes 1 | tf_op jit(solution)/shard_map/gate_up/pallas_call | solution.py:277
  79.1 3.0 %collective-permute-done.23.got_ref = bf16[3,80,512]{2,1,0:T(8,128)(2,1)S(1)} collective-permute-done((bf16[3,80,512]{2,1,0:T(8,128)(2,1)S(1)}, bf16[3,80,512]{2,1,0:T(8,128)(2,1)S(1)}, u32[]{:S(2)}, u32[]{:S(2)}) %collective-permute-start.23) | collective-permute-done | bytes 245792 | tf_op jit(solution)/shard_map/ppermute | solution.py:214
  82.1 2.3 %down.5 = (bf16[192,768]{1,0:T(8,128)(2,1)S(1)}, bf16[192,768]{1,0:T(8,128)(2,1)S(1)}, bf16[192,768]{1,0:T(8,128)(2,1)S(1)}, bf16[192,768]{1,0:T(8,128)(2,1)S(1)}) custom-call(s32[4]{0:T(128)S(1)} %pad_add_fusion.mine_ref.col_ref, f32[4,8,192]{2,1,0:T(8,128)S(1)} %get-tuple-element.106.info_ref, bf16[3,80,512]{2,1,0:T(8,128)(2,1)S(1)} %activate.5.mine_ref, ...), custom_call_target="tpu_custom_call" | custom-call | flops 1 | bytes 1 | tf_op jit(solution)/shard_map/down/pallas_call | solution.py:372
  86.0 6.6 %collective-permute-done.24.got_ref = bf16[3,80,1024]{2,1,0:T(8,128)(2,1)S(1)} collective-permute-done((bf16[3,80,1024]{2,1,0:T(8,128)(2,1)S(1)}, bf16[3,80,1024]{2,1,0:T(8,128)(2,1)S(1)}, u32[]{:S(2)}, u32[]{:S(2)}) %collective-permute-start.24) | collective-permute-done | bytes 491552 | tf_op jit(solution)/shard_map/ppermute | solution.py:214
  95.6 12.0 %collective-permute-done.27.got_ref = bf16[3,80,512]{2,1,0:T(8,128)(2,1)S(1)} collective-permute-done((bf16[3,80,512]{2,1,0:T(8,128)(2,1)S(1)}, bf16[3,80,512]{2,1,0:T(8,128)(2,1)S(1)}, u32[]{:S(2)}, u32[]{:S(2)}) %collective-permute-start.27) | collective-permute-done | bytes 245792 | tf_op jit(solution)/shard_map/ppermute | solution.py:214
  107.6 2.3 %down.6 = (bf16[192,768]{1,0:T(8,128)(2,1)S(1)}, bf16[192,768]{1,0:T(8,128)(2,1)S(1)}, bf16[192,768]{1,0:T(8,128)(2,1)S(1)}, bf16[192,768]{1,0:T(8,128)(2,1)S(1)}) custom-call(s32[4]{0:T(128)S(1)} %pad_add_fusion.mine_ref.col_ref, f32[4,8,192]{2,1,0:T(8,128)S(1)} %get-tuple-element.124.info_ref, bf16[3,80,512]{2,1,0:T(8,128)(2,1)S(1)} %activate.6.mine_ref, ...), custom_call_target="tpu_custom_call" | custom-call | flops 1 | bytes 1 | tf_op jit(solution)/shard_map/down/pallas_call | solution.py:372
  115.7 4.4 %collective-permute-done.29 = bf16[192,768]{1,0:T(8,128)(2,1)S(1)} collective-permute-done((bf16[192,768]{1,0:T(8,128)(2,1)S(1)}, bf16[192,768]{1,0:T(8,128)(2,1)S(1)}, u32[]{:S(2)}, u32[]{:S(2)}) %collective-permute-start.29) | collective-permute-done | bytes 294944 | tf_op jit(solution)/shard_map/ppermute | solution.py:202
  127.1 7.6 %collective-permute-done.37.refs_1_ = bf16[192,768]{1,0:T(8,128)(2,1)S(1)} collective-permute-done((bf16[192,768]{1,0:T(8,128)(2,1)S(1)}, bf16[192,768]{1,0:T(8,128)(2,1)S(1)}, u32[]{:S(2)}, u32[]{:S(2)}) %collective-permute-start.37) | collective-permute-done | bytes 294944 | tf_op jit(solution)/shard_map/ppermute | solution.py:206
  136.8 12.6 %collective-permute-done.39 = bf16[192,768]{1,0:T(8,128)(2,1)S(1)} collective-permute-done((bf16[192,768]{1,0:T(8,128)(2,1)S(1)}, bf16[192,768]{1,0:T(8,128)(2,1)S(1)}, u32[]{:S(2)}, u32[]{:S(2)}) %collective-permute-start.39) | collective-permute-done | bytes 294944 | tf_op jit(solution)/shard_map/ppermute | solution.py:202
  151.7 7.0 %collective-permute-done.41 = f32[768]{0:T(1024)S(1)} collective-permute-done((f32[768]{0:T(1024)S(1)}, f32[768]{0:T(1024)S(1)}, u32[]{:S(2)}, u32[]{:S(2)}) %collective-permute-start.41) | collective-permute-done | bytes 3104 | tf_op jit(solution)/shard_map/ppermute | solution.py:214
  159.8 3.8 %collective-permute-start.45 = (bf16[192,512]{1,0:T(8,128)(2,1)S(1)}, bf16[192,512]{1,0:T(8,128)(2,1)S(1)}, u32[]{:S(2)}, u32[]{:S(2)}) collective-permute-start(bf16[192,512]{1,0:T(8,128)(2,1)S(1)} %keys_values.1.refs_0_), channel_id=1, source_target_pairs={{0,24},{2,26},{4,28},{6,30},{8,0},{10,2},{12,4},{14,6},{16,8},{18,... | collective-permute-start | bytes 589832 | tf_op jit(solution)/shard_map/ppermute | solution.py:202
  165.7 3.7 %collective-permute-done.44.refs_0_ = bf16[192,512]{1,0:T(8,128)(2,1)S(1)} collective-permute-done((bf16[192,512]{1,0:T(8,128)(2,1)S(1)}, bf16[192,512]{1,0:T(8,128)(2,1)S(1)}, u32[]{:S(2)}, u32[]{:S(2)}) %collective-permute-start.44) | collective-permute-done | bytes 196640 | tf_op jit(solution)/shard_map/ppermute | solution.py:202
  171.7 3.4 %collective-permute-done.46.refs_2_ = bf16[192,512]{1,0:T(8,128)(2,1)S(1)} collective-permute-done((bf16[192,512]{1,0:T(8,128)(2,1)S(1)}, bf16[192,512]{1,0:T(8,128)(2,1)S(1)}, u32[]{:S(2)}, u32[]{:S(2)}) %collective-permute-start.46) | collective-permute-done | bytes 196640 | tf_op jit(solution)/shard_map/ppermute | solution.py:206
  175.8 3.0 %collective-permute-done.48.refs_0_ = bf16[192,512]{1,0:T(8,128)(2,1)S(1)} collective-permute-done((bf16[192,512]{1,0:T(8,128)(2,1)S(1)}, bf16[192,512]{1,0:T(8,128)(2,1)S(1)}, u32[]{:S(2)}, u32[]{:S(2)}) %collective-permute-start.48) | collective-permute-done | bytes 196640 | tf_op jit(solution)/shard_map/ppermute | solution.py:202
  179.0 5.5 %collective-permute-done.51.refs_6_ = bf16[192,512]{1,0:T(8,128)(2,1)S(1)} collective-permute-done((bf16[192,512]{1,0:T(8,128)(2,1)S(1)}, bf16[192,512]{1,0:T(8,128)(2,1)S(1)}, u32[]{:S(2)}, u32[]{:S(2)}) %collective-permute-start.51) | collective-permute-done | bytes 196640 | tf_op jit(solution)/shard_map/ppermute | solution.py:206
  185.9 3.2 %write_pages.1 = bf16[24,128,512]{2,1,0:T(8,128)(2,1)} custom-call(s32[8,24]{1,0:T(8,128)S(1)} %get-tuple-element.154.page_ref, bf16[2,192,512]{2,1,0:T(8,128)(2,1)S(1)} %stack.19.refs_0_, bf16[2,192,512]{2,1,0:T(8,128)(2,1)S(1)} %collective-permute-done.43.refs_1_, bf16[3,192,512]{2,1,0:T(8,128)(2,1)S(1)} %stack.20.refs_2_, ...), custom_call_target="tpu_custom_call", output_to_operand_aliasing={{}: (9, {})} | custom-call | flops 1 | bytes 1 | tf_op jit(solution)/shard_map/write_pages/pallas_call | solution.py:633
  (146 shorter events, 54.2 us)
Async XLA Ops:
  0.6 10.3 %collective-permute-start = (bf16[192,768]{1,0:T(8,128)(2,1)}, bf16[192,768]{1,0:T(8,128)(2,1)S(1)}, u32[]{:S(2)}, u32[]{:S(2)}) collective-permute-start(bf16[192,768]{1,0:T(8,128)(2,1)} %param.14), channel_id=1, source_target_pairs={{0,1},{1,0},{2,3},{3,2},{4,5},{5,4},{6,7},{7,6},{8,9},{9,8},{10,11... | collective-permute-start | bytes 884744 | tf_op jit(solution)/shard_map/ppermute | solution.py:214
  17.2 8.9 %collective-permute-start.3 = (bf16[208,768]{1,0:T(8,128)(2,1)S(1)}, bf16[208,768]{1,0:T(8,128)(2,1)S(1)}, u32[]{:S(2)}, u32[]{:S(2)}) collective-permute-start(bf16[208,768]{1,0:T(8,128)(2,1)S(1)} %pad_maximum_fusion.refs_0_), channel_id=1, source_target_pairs={{0,8},{2,10},{4,12},{6,14},{8,16},{10,18},{12,20},{14,22},{16,24},... | collective-permute-start | bytes 958472 | tf_op jit(solution)/shard_map/ppermute | solution.py:202
  18.8 11.3 %collective-permute-start.4 = (bf16[208,768]{1,0:T(8,128)(2,1)S(1)}, bf16[208,768]{1,0:T(8,128)(2,1)}, u32[]{:S(2)}, u32[]{:S(2)}) collective-permute-start(bf16[208,768]{1,0:T(8,128)(2,1)S(1)} %pad_maximum_fusion.refs_0_), channel_id=1, source_target_pairs={{0,2},{2,0},{4,6},{6,4},{8,10},{10,8},{12,14},{14,12},{16,18},{18,... | collective-permute-start | bytes 958472 | tf_op jit(solution)/shard_map/ppermute | solution.py:210
  26.0 15.4 %collective-permute-start.6 = (bf16[208,768]{1,0:T(8,128)(2,1)S(1)}, bf16[208,768]{1,0:T(8,128)(2,1)S(1)}, u32[]{:S(2)}, u32[]{:S(2)}) collective-permute-start(bf16[208,768]{1,0:T(8,128)(2,1)S(1)} %collective-permute-done.3.refs_0_), channel_id=1, source_target_pairs={{0,4},{2,6},{4,0},{6,2},{8,12},{10,14},{12,8},{14,10},{16,20},{18,... | collective-permute-start | bytes 958472 | tf_op jit(solution)/shard_map/ppermute | solution.py:206
  29.8 13.3 %collective-permute-start.7 = (bf16[208,768]{1,0:T(8,128)(2,1)S(1)}, bf16[208,768]{1,0:T(8,128)(2,1)S(1)}, u32[]{:S(2)}, u32[]{:S(2)}) collective-permute-start(bf16[208,768]{1,0:T(8,128)(2,1)S(1)} %collective-permute-done.3.refs_0_), channel_id=1, source_target_pairs={{0,2},{2,0},{4,6},{6,4},{8,10},{10,8},{12,14},{14,12},{16,18},{18,... | collective-permute-start | bytes 958472 | tf_op jit(solution)/shard_map/ppermute | solution.py:210
  30.1 16.1 %collective-permute-start.10 = (bf16[208,768]{1,0:T(8,128)(2,1)S(1)}, bf16[208,768]{1,0:T(8,128)(2,1)S(1)}, u32[]{:S(2)}, u32[]{:S(2)}) collective-permute-start(bf16[208,768]{1,0:T(8,128)(2,1)S(1)} %collective-permute-done.3.refs_0_), channel_id=1, source_target_pairs={{0,8},{2,10},{4,12},{6,14},{8,16},{10,18},{12,20},{14,22},{16,24},... | collective-permute-start | bytes 958472 | tf_op jit(solution)/shard_map/ppermute | solution.py:202
  36.7 15.3 %collective-permute-start.9 = (bf16[3,80,1024]{2,1,0:T(8,128)(2,1)S(1)}, bf16[3,80,1024]{2,1,0:T(8,128)(2,1)S(1)}, u32[]{:S(2)}, u32[]{:S(2)}) collective-permute-start(bf16[3,80,1024]{2,1,0:T(8,128)(2,1)S(1)} %get-tuple-element.99), channel_id=1, source_target_pairs={{0,1},{1,0},{2,3},{3,2},{4,5},{5,4},{6,7},{7,6},{8,9},{9,8},{10,11... | collective-permute-start | bytes 1474568 | tf_op jit(solution)/shard_map/ppermute | solution.py:214
  46.2 10.0 %collective-permute-start.11 = (bf16[208,768]{1,0:T(8,128)(2,1)S(1)}, bf16[208,768]{1,0:T(8,128)(2,1)S(1)}, u32[]{:S(2)}, u32[]{:S(2)}) collective-permute-start(bf16[208,768]{1,0:T(8,128)(2,1)S(1)} %collective-permute-done.10.refs_0_), channel_id=1, source_target_pairs={{0,4},{2,6},{4,0},{6,2},{8,12},{10,14},{12,8},{14,10},{16,20},{18,... | collective-permute-start | bytes 958472 | tf_op jit(solution)/shard_map/ppermute | solution.py:206
  47.7 11.0 %collective-permute-start.16 = (bf16[208,768]{1,0:T(8,128)(2,1)S(1)}, bf16[208,768]{1,0:T(8,128)(2,1)S(1)}, u32[]{:S(2)}, u32[]{:S(2)}) collective-permute-start(bf16[208,768]{1,0:T(8,128)(2,1)S(1)} %pad_maximum_fusion.refs_0_), channel_id=1, source_target_pairs={{0,24},{2,26},{4,28},{6,30},{8,0},{10,2},{12,4},{14,6},{16,8},{18,... | collective-permute-start | bytes 958472 | tf_op jit(solution)/shard_map/ppermute | solution.py:202
  51.6 14.1 %collective-permute-start.14 = (bf16[3,80,1024]{2,1,0:T(8,128)(2,1)S(1)}, bf16[3,80,1024]{2,1,0:T(8,128)(2,1)S(1)}, u32[]{:S(2)}, u32[]{:S(2)}) collective-permute-start(bf16[3,80,1024]{2,1,0:T(8,128)(2,1)S(1)} %get-tuple-element.107), channel_id=1, source_target_pairs={{0,1},{1,0},{2,3},{3,2},{4,5},{5,4},{6,7},{7,6},{8,9},{9,8},{10,11... | collective-permute-start | bytes 1474568 | tf_op jit(solution)/shard_map/ppermute | solution.py:214
  58.7 13.5 %collective-permute-start.17 = (bf16[208,768]{1,0:T(8,128)(2,1)S(1)}, bf16[208,768]{1,0:T(8,128)(2,1)S(1)}, u32[]{:S(2)}, u32[]{:S(2)}) collective-permute-start(bf16[208,768]{1,0:T(8,128)(2,1)S(1)} %collective-permute-done.16.refs_0_), channel_id=1, source_target_pairs={{0,4},{2,6},{4,0},{6,2},{8,12},{10,14},{12,8},{14,10},{16,20},{18,... | collective-permute-start | bytes 958472 | tf_op jit(solution)/shard_map/ppermute | solution.py:206
  59.3 10.6 %collective-permute-start.15 = (bf16[3,80,512]{2,1,0:T(8,128)(2,1)S(1)}, bf16[3,80,512]{2,1,0:T(8,128)(2,1)S(1)}, u32[]{:S(2)}, u32[]{:S(2)}) collective-permute-start(bf16[3,80,512]{2,1,0:T(8,128)(2,1)S(1)} %activate.4.mine_ref), channel_id=1, source_target_pairs={{0,1},{1,0},{2,3},{3,2},{4,5},{5,4},{6,7},{7,6},{8,9},{9,8},{10,11... | collective-permute-start | bytes 737288 | tf_op jit(solution)/shard_map/ppermute | solution.py:214
  73.3 8.8 %collective-permute-start.23 = (bf16[3,80,512]{2,1,0:T(8,128)(2,1)S(1)}, bf16[3,80,512]{2,1,0:T(8,128)(2,1)S(1)}, u32[]{:S(2)}, u32[]{:S(2)}) collective-permute-start(bf16[3,80,512]{2,1,0:T(8,128)(2,1)S(1)} %activate.5.mine_ref), channel_id=1, source_target_pairs={{0,1},{1,0},{2,3},{3,2},{4,5},{5,4},{6,7},{7,6},{8,9},{9,8},{10,11... | collective-permute-start | bytes 737288 | tf_op jit(solution)/shard_map/ppermute | solution.py:214
  73.9 18.8 %collective-permute-start.24 = (bf16[3,80,1024]{2,1,0:T(8,128)(2,1)S(1)}, bf16[3,80,1024]{2,1,0:T(8,128)(2,1)S(1)}, u32[]{:S(2)}, u32[]{:S(2)}) collective-permute-start(bf16[3,80,1024]{2,1,0:T(8,128)(2,1)S(1)} %get-tuple-element.125), channel_id=1, source_target_pairs={{0,1},{1,0},{2,3},{3,2},{4,5},{5,4},{6,7},{7,6},{8,9},{9,8},{10,11... | collective-permute-start | bytes 1474568 | tf_op jit(solution)/shard_map/ppermute | solution.py:214
  84.4 9.4 %collective-permute-start.25 = (bf16[192,768]{1,0:T(8,128)(2,1)S(1)}, bf16[192,768]{1,0:T(8,128)(2,1)S(1)}, u32[]{:S(2)}, u32[]{:S(2)}) collective-permute-start(bf16[192,768]{1,0:T(8,128)(2,1)S(1)} %get-tuple-element.128), channel_id=1, source_target_pairs={{0,2},{2,0},{4,6},{6,4},{8,10},{10,8},{12,14},{14,12},{16,18},{18,... | collective-permute-start | bytes 884744 | tf_op jit(solution)/shard_map/ppermute | solution.py:210
  84.5 9.3 %collective-permute-start.26 = (bf16[192,768]{1,0:T(8,128)(2,1)S(1)}, bf16[192,768]{1,0:T(8,128)(2,1)S(1)}, u32[]{:S(2)}, u32[]{:S(2)}) collective-permute-start(bf16[192,768]{1,0:T(8,128)(2,1)S(1)} %get-tuple-element.129), channel_id=1, source_target_pairs={{0,2},{2,0},{4,6},{6,4},{8,10},{10,8},{12,14},{14,12},{16,18},{18,... | collective-permute-start | bytes 884744 | tf_op jit(solution)/shard_map/ppermute | solution.py:210
  85.0 26.7 %collective-permute-start.30 = (bf16[3,80,1024]{2,1,0:T(8,128)(2,1)S(1)}, bf16[3,80,1024]{2,1,0:T(8,128)(2,1)S(1)}, u32[]{:S(2)}, u32[]{:S(2)}) collective-permute-start(bf16[3,80,1024]{2,1,0:T(8,128)(2,1)S(1)} %get-tuple-element.137), channel_id=1, source_target_pairs={{0,1},{1,0},{2,3},{3,2},{4,5},{5,4},{6,7},{7,6},{8,9},{9,8},{10,11... | collective-permute-start | bytes 1474568 | tf_op jit(solution)/shard_map/ppermute | solution.py:214
  85.5 10.1 %collective-permute-start.22 = (bf16[192,768]{1,0:T(8,128)(2,1)S(1)}, bf16[192,768]{1,0:T(8,128)(2,1)S(1)}, u32[]{:S(2)}, u32[]{:S(2)}) collective-permute-start(bf16[192,768]{1,0:T(8,128)(2,1)S(1)} %get-tuple-element.120), channel_id=1, source_target_pairs={{0,4},{2,6},{4,0},{6,2},{8,12},{10,14},{12,8},{14,10},{16,20},{18,... | collective-permute-start | bytes 884744 | tf_op jit(solution)/shard_map/ppermute | solution.py:206
  94.5 16.0 %collective-permute-start.28 = (bf16[192,768]{1,0:T(8,128)(2,1)S(1)}, bf16[192,768]{1,0:T(8,128)(2,1)S(1)}, u32[]{:S(2)}, u32[]{:S(2)}) collective-permute-start(bf16[192,768]{1,0:T(8,128)(2,1)S(1)} %get-tuple-element.130), channel_id=1, source_target_pairs={{0,4},{2,6},{4,0},{6,2},{8,12},{10,14},{12,8},{14,10},{16,20},{18,... | collective-permute-start | bytes 884744 | tf_op jit(solution)/shard_map/ppermute | solution.py:206
  95.1 12.5 %collective-permute-start.27 = (bf16[3,80,512]{2,1,0:T(8,128)(2,1)S(1)}, bf16[3,80,512]{2,1,0:T(8,128)(2,1)S(1)}, u32[]{:S(2)}, u32[]{:S(2)}) collective-permute-start(bf16[3,80,512]{2,1,0:T(8,128)(2,1)S(1)} %activate.6.mine_ref), channel_id=1, source_target_pairs={{0,1},{1,0},{2,3},{3,2},{4,5},{5,4},{6,7},{7,6},{8,9},{9,8},{10,11... | collective-permute-start | bytes 737288 | tf_op jit(solution)/shard_map/ppermute | solution.py:214
  111.0 9.0 %collective-permute-start.29 = (bf16[192,768]{1,0:T(8,128)(2,1)S(1)}, bf16[192,768]{1,0:T(8,128)(2,1)S(1)}, u32[]{:S(2)}, u32[]{:S(2)}) collective-permute-start(bf16[192,768]{1,0:T(8,128)(2,1)S(1)} %add.122), channel_id=1, source_target_pairs={{0,24},{2,26},{4,28},{6,30},{8,0},{10,2},{12,4},{14,6},{16,8},{18,... | collective-permute-start | bytes 884744 | tf_op jit(solution)/shard_map/ppermute | solution.py:202
  112.8 7.7 %collective-permute-start.33 = (bf16[3,80,512]{2,1,0:T(8,128)(2,1)S(1)}, bf16[3,80,512]{2,1,0:T(8,128)(2,1)S(1)}, u32[]{:S(2)}, u32[]{:S(2)}) collective-permute-start(bf16[3,80,512]{2,1,0:T(8,128)(2,1)S(1)} %activate.7.mine_ref), channel_id=1, source_target_pairs={{0,1},{1,0},{2,3},{3,2},{4,5},{5,4},{6,7},{7,6},{8,9},{9,8},{10,11... | collective-permute-start | bytes 737288 | tf_op jit(solution)/shard_map/ppermute | solution.py:214
  114.2 9.2 %collective-permute-start.34 = (bf16[192,768]{1,0:T(8,128)(2,1)S(1)}, bf16[192,768]{1,0:T(8,128)(2,1)S(1)}, u32[]{:S(2)}, u32[]{:S(2)}) collective-permute-start(bf16[192,768]{1,0:T(8,128)(2,1)S(1)} %get-tuple-element.142), channel_id=1, source_target_pairs={{0,4},{2,6},{4,0},{6,2},{8,12},{10,14},{12,8},{14,10},{16,20},{18,... | collective-permute-start | bytes 884744 | tf_op jit(solution)/shard_map/ppermute | solution.py:206
  125.6 9.1 %collective-permute-start.37 = (bf16[192,768]{1,0:T(8,128)(2,1)S(1)}, bf16[192,768]{1,0:T(8,128)(2,1)S(1)}, u32[]{:S(2)}, u32[]{:S(2)}) collective-permute-start(bf16[192,768]{1,0:T(8,128)(2,1)S(1)} %get-tuple-element.151), channel_id=1, source_target_pairs={{0,4},{2,6},{4,0},{6,2},{8,12},{10,14},{12,8},{14,10},{16,20},{18,... | collective-permute-start | bytes 884744 | tf_op jit(solution)/shard_map/ppermute | solution.py:206
  127.1 22.2 %collective-permute-start.39 = (bf16[192,768]{1,0:T(8,128)(2,1)S(1)}, bf16[192,768]{1,0:T(8,128)(2,1)S(1)}, u32[]{:S(2)}, u32[]{:S(2)}) collective-permute-start(bf16[192,768]{1,0:T(8,128)(2,1)S(1)} %add.124), channel_id=1, source_target_pairs={{0,16},{2,18},{4,20},{6,22},{8,24},{10,26},{12,28},{14,30},{16,0},... | collective-permute-start | bytes 884744 | tf_op jit(solution)/shard_map/ppermute | solution.py:202
  135.3 14.0 %collective-permute-start.38 = (bf16[192,768]{1,0:T(8,128)(2,1)S(1)}, bf16[192,768]{1,0:T(8,128)(2,1)S(1)}, u32[]{:S(2)}, u32[]{:S(2)}) collective-permute-start(bf16[192,768]{1,0:T(8,128)(2,1)S(1)} %add.126), channel_id=1, source_target_pairs={{0,8},{2,10},{4,12},{6,14},{8,16},{10,18},{12,20},{14,22},{16,24},... | collective-permute-start | bytes 884744 | tf_op jit(solution)/shard_map/ppermute | solution.py:202
  149.6 9.1 %collective-permute-start.40 = (bf16[192,768]{1,0:T(8,128)(2,1)S(1)}, bf16[192,768]{1,0:T(8,128)(2,1)S(1)}, u32[]{:S(2)}, u32[]{:S(2)}) collective-permute-start(bf16[192,768]{1,0:T(8,128)(2,1)S(1)} %fusion.7.own_ref), channel_id=1, source_target_pairs={{0,1},{1,0},{2,3},{3,2},{4,5},{5,4},{6,7},{7,6},{8,9},{9,8},{10,11... | collective-permute-start | bytes 884744 | tf_op jit(solution)/shard_map/ppermute | solution.py:214
  150.2 8.5 %collective-permute-start.41 = (f32[768]{0:T(1024)S(1)}, f32[768]{0:T(1024)S(1)}, u32[]{:S(2)}, u32[]{:S(2)}) collective-permute-start(f32[768]{0:T(1024)S(1)} %copy-done.11), channel_id=1, source_target_pairs={{0,1},{1,0},{2,3},{3,2},{4,5},{5,4},{6,7},{7,6},{8,9},{9,8},{10,11... | collective-permute-start | bytes 9224 | tf_op jit(solution)/shard_map/ppermute | solution.py:214
  159.7 9.6 %collective-permute-start.44 = (bf16[192,512]{1,0:T(8,128)(2,1)S(1)}, bf16[192,512]{1,0:T(8,128)(2,1)S(1)}, u32[]{:S(2)}, u32[]{:S(2)}) collective-permute-start(bf16[192,512]{1,0:T(8,128)(2,1)S(1)} %keys_values.1.refs_0_), channel_id=1, source_target_pairs={{0,8},{2,10},{4,12},{6,14},{8,16},{10,18},{12,20},{14,22},{16,24},... | collective-permute-start | bytes 589832 | tf_op jit(solution)/shard_map/ppermute | solution.py:202
  159.8 11.5 %collective-permute-start.45 = (bf16[192,512]{1,0:T(8,128)(2,1)S(1)}, bf16[192,512]{1,0:T(8,128)(2,1)S(1)}, u32[]{:S(2)}, u32[]{:S(2)}) collective-permute-start(bf16[192,512]{1,0:T(8,128)(2,1)S(1)} %keys_values.1.refs_0_), channel_id=1, source_target_pairs={{0,24},{2,26},{4,28},{6,30},{8,0},{10,2},{12,4},{14,6},{16,8},{18,... | collective-permute-start | bytes 589832 | tf_op jit(solution)/shard_map/ppermute | solution.py:202
  175.1 10.8 %collective-permute-start.47 = (bf16[3,192,512]{2,1,0:T(8,128)(2,1)S(1)}, bf16[3,192,512]{2,1,0:T(8,128)(2,1)S(1)}, u32[]{:S(2)}, u32[]{:S(2)}) collective-permute-start(bf16[3,192,512]{2,1,0:T(8,128)(2,1)S(1)} %stack.20.refs_2_), channel_id=1, source_target_pairs={{0,2},{2,0},{4,6},{6,4},{8,10},{10,8},{12,14},{14,12},{16,18},{18,... | collective-permute-start | bytes 1769480 | tf_op jit(solution)/shard_map/ppermute | solution.py:210
  175.2 9.3 %collective-permute-start.43 = (bf16[2,192,512]{2,1,0:T(8,128)(2,1)S(1)}, bf16[2,192,512]{2,1,0:T(8,128)(2,1)S(1)}, u32[]{:S(2)}, u32[]{:S(2)}) collective-permute-start(bf16[2,192,512]{2,1,0:T(8,128)(2,1)S(1)} %stack.19.refs_0_), channel_id=1, source_target_pairs={{0,2},{2,0},{4,6},{6,4},{8,10},{10,8},{12,14},{14,12},{16,18},{18,... | collective-permute-start | bytes 1179656 | tf_op jit(solution)/shard_map/ppermute | solution.py:210
  (33 other events, 229.6 us)

commit v4 on v3

--- a/solution.py
+++ b/solution.py
@@ -576,7 +576,7 @@
     return pl.pallas_call(
         kv_kernel,
         out_shape=jax.ShapeDtypeStruct(cosine.shape, BF),
-        cost_estimate=LIGHT,
+        cost_estimate=pl.CostEstimate(flops=4294967296, bytes_accessed=1, transcendentals=0),
         compiler_params=ROOM,
         name="keys_values",
     )(own, other, gain[None], other_gain[None], w, cosine, sine)
@@ -646,10 +646,18 @@
             ],
         ),
         input_output_aliases={1 + len(blocks): 0},
-        cost_estimate=LIGHT,
+        cost_estimate=pl.CostEstimate(flops=1073741824, bytes_accessed=1, transcendentals=0),
         compiler_params=ROOM,
         name="write_pages",
     )(page_data, *blocks, cache)
+
+
+ORDER = (
+    ("U", 0), ("K", 0), ("B", 1), ("U", 1), ("N", 2), ("A", 0), ("Q", 2), ("C", 0), ("B", 2), ("U", 2),
+    ("A", 1), ("N", 3), ("Q", 3), ("b", 3), ("D", 0), ("S", 0), ("D", 1), ("A", 2), ("U", 3), ("V", 0),
+    ("S", 1), ("D", 2), ("T", 1), ("S", 2), ("A", 3), ("H", 1), ("D", 3), ("T", 2), ("S", 3), ("V", 1),
+    ("T", 3),
+)
 
 
 def on_device_16x2(
@@ -729,67 +737,89 @@
         sums[g] = add(after(mine, *earlier), *parts[g], stacked)
         return sums[g] if stacked else sums[g][-1]
 
-    own_c = core_move(own)
-    x0 = x_move(own)
-    z1 = z_move(own, 1)
-    z3 = z_move(own, 3)
+    columns = kv_proj.shape[1]
+    got = {"own": own, "own_c": core_move(own), "x0": x_move(own)}
+    got["z1"], got["z3"] = z_move(own, 1), z_move(own, 3)
     weight = after(gate_up_w, own).transpose(2, 0, 1, 3)
-    x0, z1 = lax.optimization_barrier((x0, z1))
-    x0_c = core_move(x0)
-    x1 = x_move(z1)
-    z1_c = core_move(z1)
-    z2 = z_move(z1, 1)
-    t = up_step(0, [own, x0, own_c, x0_c])
-
-    columns = kv_proj.shape[1]
-    kv_w = turn(after(mine, t), kv_proj)
-    pages, position = page_list(
-        after(mine, kv_w), kv_cache.shape[0], prompt_lens, decode_pos, table
-    )
-    lane = jnp.arange(columns, dtype=jnp.int32)
-    inverse = jnp.exp(-((lane % (HD // 2)).astype(F32) * (2.0 / HD)) * jnp.log(F32(ROPE_BASE)))
-    angles = position[:, :1] * inverse[None, :]
-    is_key = (my_col * columns + lane < KVH * HD)[None, :]
-    cosine = jnp.where(is_key, jnp.cos(angles), 1.0)
-    sine = jnp.where(is_key, jnp.sin(angles), 0.0)
-    kv_w, pages, cosine, sine = lax.optimization_barrier((kv_w, pages, cosine, sine))
-
-    x1_c = core_move(x1)
-    t = up_step(1, [z1, x1, z1_c, x1_c], t, cosine)
-    z2 = after(z2, t)
-    x2 = x_move(z2)
-    z2_c = core_move(z2)
-    t = act_step(0, t)
-    cache = copy_cache(after(kv_cache, t))
-    x2_c = core_move(after(x2, cache))
-    t = up_step(2, [z2, x2, z2_c, x2_c], t, cache)
-    x3 = x_move(after(z3, x2))
-    t = act_step(1, t)
-    t = down_step(0, t)
-    z3_c = core_move(after(z3, t))
-    x3_c = core_move(after(x3, t))
-    t = up_step(3, [z3, x3, z3_c, x3_c], t)
-    t = sum_step(0, False, t)
-    back_x0 = x_move(t)
-    t = down_step(1, t)
-    t = act_step(2, t)
-    t = sum_step(1, False, t)
-    back_x1 = x_move(t)
-    t = down_step(2, t, back_x0)
-    (t,) = add(after(mine, t), sums[1][:1], [back_x1], False)
-    back_1 = z_move(t, 3)
-    t = act_step(3, t)
-    t = sum_step(2, False, t)
-    back_x2 = x_move(t)
-    t = down_step(3, t, back_1)
-    (t,) = add(after(mine, t), sums[2][:1], [back_x2], False)
-    back_2 = z_move(t, 2)
-    t = sum_step(3, False, t)
-    back_x3 = x_move(t)
-    (t,) = add(after(mine, t), sums[3][:1], [back_x3], False)
-    back_3 = z_move(t, 1)
+    got["x0_c"] = core_move(got["x0"])
+    got["x1"], got["z1_c"] = x_move(got["z1"]), core_move(got["z1"])
+    got["z2"] = z_move(got["z1"], 1)
+    groups = (("own", "x0"), ("z1", "x1"), ("z2", "x2"), ("z3", "x3"))
+    t = [own]
+
+    def up(g):
+        near, far = groups[g]
+        blocks = [got[k] for k in (near, far, near + "_c", far + "_c")]
+        t[:] = [up_step(g, blocks, *t)]
+
+    def act(g):
+        t[:] = [act_step(g, *t)]
+
+    def lower(g):
+        t[:] = [down_step(g, *t)]
+
+    def gather(g):
+        t[:] = [sum_step(g, False, *t)]
+        moving["x", g] = x_move(t[0])
+
+    def total(g):
+        whole = add(after(mine, *t), sums[g][:1], [moving["x", g]], False)
+        t[:] = whole
+        moving["z", g] = z_move(whole[0], (0, 3, 2, 1)[g])
+
+    def across(g):
+        got["x%d" % g] = x_move(after(got["z%d" % g], *t))
+
+    def b_free(g):
+        got["x%d_c" % g] = core_move(got["x%d" % g])
+
+    def across_next(g):
+        got["x%d" % g] = x_move(after(got["z%d" % g], got["x%d" % (g - 1)]))
+
+    def near_core(g):
+        got["z%d_c" % g] = core_move(after(got["z%d" % g], *t))
+
+    def far_core(g):
+        got["x%d_c" % g] = core_move(after(got["x%d" % g], *t))
+
+    def tables(g):
+        kv_w = turn(after(mine, *t), kv_proj)
+        pages, position = page_list(
+            after(mine, kv_w), kv_cache.shape[0], prompt_lens, decode_pos, table
+        )
+        lane = jnp.arange(columns, dtype=jnp.int32)
+        inverse = jnp.exp(
+            -((lane % (HD // 2)).astype(F32) * (2.0 / HD)) * jnp.log(F32(ROPE_BASE))
+        )
+        angles = position[:, :1] * inverse[None, :]
+        is_key = (my_col * columns + lane < KVH * HD)[None, :]
+        cosine = jnp.where(is_key, jnp.cos(angles), 1.0)
+        sine = jnp.where(is_key, jnp.sin(angles), 0.0)
+        got["tables"] = lax.optimization_barrier((kv_w, pages, cosine, sine))
+        t.append(got["tables"][2])
+
+    def cache_copy(g):
+        got["cache"] = copy_cache(after(kv_cache, *t))
+        t.append(got["cache"])
+
+    def arrived(g):
+        t.append(got["z%d" % g])
+
+    def back(g):
+        t.append(moving["x", g])
+
+    def home(g):
+        t.append(moving["z", g])
+
+    steps = dict(U=up, A=act, D=lower, S=gather, T=total, X=across, N=across_next, Q=near_core, B=far_core)
+    steps.update(b=b_free, K=tables, C=cache_copy, W=arrived, V=back, H=home)
+    for name, g in ORDER:
+        steps[name](g)
+    kv_w, pages, cosine, sine = got["tables"]
+    cache = got["cache"]
     whole = lambda a, b: a.astype(F32) + b.astype(F32)
-    mixture = whole(sums[0][0], back_x0) + whole(back_1, back_3) + back_2.astype(F32)
+    mixture = whole(sums[0][0], moving["x", 0]) + whole(moving["z", 1], moving["z", 3])
+    mixture = mixture + moving["z", 2].astype(F32)
     layer_out = lax.optimization_barrier((res_f + mixture).astype(BF))
 
     gain_other = y_move(after(gain_moe, sums[2][0]))

time: 190 us -> 184 us (0.968)
  waiting for transfers between devices: 95.5 us -> 73.5 us
  starting transfers between devices: 39.7 us -> 54.4 us
    ppermute x12, waiting for transfers between devices: 41.1 us -> 26.1 us  [y_move(): return lax.ppermute(value, 'mp', [(0, 1), (1, 0)])]
    ppermute x9, starting transfers between devices: 11.4 us -> 18.8 us  [z_move(): return lax.ppermute(value, 'dp', moves(dz, 0, 0))]
    ppermute x9, waiting for transfers between devices: 28.9 us -> 23.7 us  [z_move(): return lax.ppermute(value, 'dp', moves(dz, 0, 0))]
    ppermute x12, starting transfers between devices: 11 us -> 14.9 us  [x_move(): return lax.ppermute(value, 'dp', moves(0, 1, 0))]
    ppermute x12, starting transfers between devices: 13.1 us -> 16.5 us  [y_move(): return lax.ppermute(value, 'mp', [(0, 1), (1, 0)])]
  transfers between devices with their start and end apart: 53 -> 53, of which waited for: 25 -> 23; matrix products, arithmetic and copies ran while one was open for 4% -> 4% of each run, Pallas kernels for 21% -> 21%
where the time goes in v4:
time: 184 us; the launch traced here: 182 us
  waiting for transfers between devices  73.5 us (40%)
  starting transfers between devices  54.4 us (30%)
  Pallas kernels  43.7 us (24%)
  other arithmetic  3.6 us (2%)
  local copies, waits for them, and re-layouts  3.41 us (2%)
  matrix products  1.86 us (1%)
    ppermute x12, waiting for transfers between devices, y_move(): return lax.ppermute(value, 'mp', [(0, 1), (1, 0)])  26.1 us
    ppermute x9, waiting for transfers between devices, z_move(): return lax.ppermute(value, 'dp', moves(dz, 0, 0))  23.7 us
    ppermute x12, waiting for transfers between devices, x_move(): return lax.ppermute(value, 'dp', moves(0, 1, 0))  21.2 us
    ppermute x9, starting transfers between devices, z_move(): return lax.ppermute(value, 'dp', moves(dz, 0, 0))  18.8 us
    ppermute x12, starting transfers between devices, y_move(): return lax.ppermute(value, 'mp', [(0, 1), (1, 0)])  16.5 us
    ppermute x12, starting transfers between devices, x_move(): return lax.ppermute(value, 'dp', moves(0, 1, 0))  14.9 us
    pallas_call x4, Pallas kernels, gate_up(): pl.pallas_call(functools.partial(gate_up_kernel, n), out_shape=(jax.Shape...  13.2 us
    pallas_call x4, Pallas kernels, down(): pl.pallas_call(down_kernel, out_shape=[jax.ShapeDtypeStruct((tokens, widt...  9.13 us
  transfers between devices with their start and end apart: 53, of which 23 were waited for; matrix products, arithmetic and copies ran while one was open for 4% of the time, Pallas kernels for 21%

profile of v4, /device:TPU:0, one launch (start us, length us, event | category | flops | bytes accessed | tf_op | source)
XLA Modules:
  0.0 181.8 jit_solution(11815239366307035947)
XLA Ops:
  0.6 3.1 %collective-permute-start = (bf16[192,768]{1,0:T(8,128)(2,1)}, bf16[192,768]{1,0:T(8,128)(2,1)S(1)}, u32[]{:S(2)}, u32[]{:S(2)}) collective-permute-start(bf16[192,768]{1,0:T(8,128)(2,1)} %param.14), channel_id=1, source_target_pairs={{0,1},{1,0},{2,3},{3,2},{4,5},{5,4},{6,7},{7,6},{8,9},{9,8},{10,11... | collective-permute-start | bytes 884744 | tf_op jit(solution)/shard_map/ppermute | solution.py:214
  6.6 4.3 %collective-permute-done = bf16[192,768]{1,0:T(8,128)(2,1)S(1)} collective-permute-done((bf16[192,768]{1,0:T(8,128)(2,1)}, bf16[192,768]{1,0:T(8,128)(2,1)S(1)}, u32[]{:S(2)}, u32[]{:S(2)}) %collective-permute-start) | collective-permute-done | bytes 294944 | tf_op jit(solution)/shard_map/ppermute | solution.py:214
  13.4 1.8 %collective-permute-done.1 = f32[192]{0:T(256)S(1)} collective-permute-done((f32[192]{0:T(256)S(1)}, f32[192]{0:T(256)S(1)}, u32[]{:S(2)}, u32[]{:S(2)}) %collective-permute-start.1) | collective-permute-done | bytes 800 | tf_op jit(solution)/shard_map/ppermute | solution.py:214
  19.0 4.0 %collective-permute-done.2.refs_1_ = bf16[208,768]{1,0:T(8,128)(2,1)S(1)} collective-permute-done((bf16[208,768]{1,0:T(8,128)(2,1)S(1)}, bf16[208,768]{1,0:T(8,128)(2,1)S(1)}, u32[]{:S(2)}, u32[]{:S(2)}) %collective-permute-start.2) | collective-permute-done | bytes 319520 | tf_op jit(solution)/shard_map/ppermute | solution.py:206
  23.1 3.2 %copy.22 = bf16[3,768,2,512]{3,1,0,2:T(8,128)(2,1)S(1)} copy(bf16[3,768,2,512]{3,2,1,0:T(2,128)(2,1)} %param.20) | data formatting | bytes 9437184 | tf_op jit(solution)/shard_map/optimization_barrier | solution.py:218
  26.3 2.9 %collective-permute-done.5.refs_0_ = bf16[208,768]{1,0:T(8,128)(2,1)S(1)} collective-permute-done((bf16[208,768]{1,0:T(8,128)(2,1)S(1)}, bf16[208,768]{1,0:T(8,128)(2,1)S(1)}, u32[]{:S(2)}, u32[]{:S(2)}) %collective-permute-start.5) | collective-permute-done | bytes 319520 | tf_op jit(solution)/shard_map/ppermute | solution.py:202
  29.7 4.0 %gate_up.4 = (bf16[3,80,1024]{2,1,0:T(8,128)(2,1)S(1)}, f32[3,80,1024]{2,1,0:T(8,128)S(1)}, f32[4,8,192]{2,1,0:T(8,128)S(1)}) custom-call(s32[4]{0:T(128)S(1)} %pad_add_fusion.mine_ref.col_ref, bf16[2,3,768,512]{3,2,1,0:T(8,128)(2,1)S(1)} %bitcast.21, bf16[208,768]{1,0:T(8,128)(2,1)S(1)} %pad_maximum_fusion.refs_0_, ...), custom_call_target="tpu_custom_call" | custom-call | flops 1 | bytes 1 | tf_op jit(solution)/shard_map/gate_up/pallas_call | solution.py:277
  33.8 2.4 %turn.1.w_ref = bf16[2,768,1024]{2,1,0:T(8,128)(2,1)S(1)} custom-call(s32[4]{0:T(128)S(1)} %pad_add_fusion.mine_ref.col_ref, bf16[1536,512]{1,0:T(8,128)(2,1)S(1)} %copy-done.3), custom_call_target="tpu_custom_call" | custom-call | flops 1 | bytes 1 | tf_op jit(solution)/shard_map/turn/pallas_call | solution.py:542
  37.8 3.1 %page_list.1 = (s32[8,24]{1,0:T(8,128)S(1)}, f32[192,128]{1,0:T(8,128)S(1)}) custom-call(s32[4]{0:T(128)S(1)} %pad_add_fusion.mine_ref.col_ref, s32[16]{0:T(128)S(1)} %copy-done.5, s32[32]{0:T(128)S(1)} %copy-done.6, s32[48,8]{1,0:T(8,128)S(1)} %broadcast_maximum_fusion.table_ref), custom_call_target="tpu_custom_call" | custom-call | flops 1 | bytes 1 | tf_op jit(solution)/shard_map/page_list/pallas_call | solution.py:516
  44.3 3.0 %gate_up.5 = (bf16[3,80,1024]{2,1,0:T(8,128)(2,1)S(1)}, f32[3,80,1024]{2,1,0:T(8,128)S(1)}, f32[4,8,192]{2,1,0:T(8,128)S(1)}) custom-call(s32[4]{0:T(128)S(1)} %pad_add_fusion.mine_ref.col_ref, bf16[2,3,768,512]{3,2,1,0:T(8,128)(2,1)S(1)} %bitcast.22, bf16[208,768]{1,0:T(8,128)(2,1)S(1)} %collective-permute-done.5.refs_0_, ...), custom_call_target="tpu_custom_call" | custom-call | flops 1 | bytes 1 | tf_op jit(solution)/shard_map/gate_up/pallas_call | solution.py:277
  47.9 3.7 %collective-permute-start.21 = (bf16[208,768]{1,0:T(8,128)(2,1)S(1)}, bf16[208,768]{1,0:T(8,128)(2,1)S(1)}, u32[]{:S(2)}, u32[]{:S(2)}) collective-permute-start(bf16[208,768]{1,0:T(8,128)(2,1)S(1)} %pad_maximum_fusion.refs_0_), channel_id=1, source_target_pairs={{0,24},{2,26},{4,28},{6,30},{8,0},{10,2},{12,4},{14,6},{16,8},{18,... | collective-permute-start | bytes 958472 | tf_op jit(solution)/shard_map/ppermute | solution.py:202
  52.7 2.7 %copy_cache.1.refs_8_ = bf16[24,128,512]{2,1,0:T(8,128)(2,1)} custom-call(bf16[24,128,512]{2,1,0:T(8,128)(2,1)S(1)} %copy-done.2), custom_call_target="tpu_custom_call" | custom-call | flops 1 | bytes 1 | tf_op jit(solution)/shard_map/copy_cache/pallas_call | solution.py:440
  59.9 3.0 %gate_up.6 = (bf16[3,80,1024]{2,1,0:T(8,128)(2,1)S(1)}, f32[3,80,1024]{2,1,0:T(8,128)S(1)}, f32[4,8,192]{2,1,0:T(8,128)S(1)}) custom-call(s32[4]{0:T(128)S(1)} %pad_add_fusion.mine_ref.col_ref, bf16[2,3,768,512]{3,2,1,0:T(8,128)(2,1)S(1)} %bitcast.23, bf16[208,768]{1,0:T(8,128)(2,1)S(1)} %collective-permute-done.10.refs_0_, ...), custom_call_target="tpu_custom_call" | custom-call | flops 1 | bytes 1 | tf_op jit(solution)/shard_map/gate_up/pallas_call | solution.py:277
  66.7 2.3 %down.4 = (bf16[192,768]{1,0:T(8,128)(2,1)S(1)}, bf16[192,768]{1,0:T(8,128)(2,1)S(1)}, bf16[192,768]{1,0:T(8,128)(2,1)S(1)}, bf16[192,768]{1,0:T(8,128)(2,1)S(1)}) custom-call(s32[4]{0:T(128)S(1)} %pad_add_fusion.mine_ref.col_ref, f32[4,8,192]{2,1,0:T(8,128)S(1)} %get-tuple-element.98.info_ref, bf16[3,80,512]{2,1,0:T(8,128)(2,1)S(1)} %activate.4.mine_ref, ...), custom_call_target="tpu_custom_call" | custom-call | flops 1 | bytes 1 | tf_op jit(solution)/shard_map/down/pallas_call | solution.py:372
  73.3 8.4 %collective-permute-done.19.got_ref = bf16[3,80,512]{2,1,0:T(8,128)(2,1)S(1)} collective-permute-done((bf16[3,80,512]{2,1,0:T(8,128)(2,1)S(1)}, bf16[3,80,512]{2,1,0:T(8,128)(2,1)S(1)}, u32[]{:S(2)}, u32[]{:S(2)}) %collective-permute-start.19) | collective-permute-done | bytes 245792 | tf_op jit(solution)/shard_map/ppermute | solution.py:214
  81.7 2.3 %down.5 = (bf16[192,768]{1,0:T(8,128)(2,1)S(1)}, bf16[192,768]{1,0:T(8,128)(2,1)S(1)}, bf16[192,768]{1,0:T(8,128)(2,1)S(1)}, bf16[192,768]{1,0:T(8,128)(2,1)S(1)}) custom-call(s32[4]{0:T(128)S(1)} %pad_add_fusion.mine_ref.col_ref, f32[4,8,192]{2,1,0:T(8,128)S(1)} %get-tuple-element.107.info_ref, bf16[3,80,512]{2,1,0:T(8,128)(2,1)S(1)} %activate.5.mine_ref, ...), custom_call_target="tpu_custom_call" | custom-call | flops 1 | bytes 1 | tf_op jit(solution)/shard_map/down/pallas_call | solution.py:372
  87.1 3.0 %gate_up.7 = (bf16[3,80,1024]{2,1,0:T(8,128)(2,1)S(1)}, f32[3,80,1024]{2,1,0:T(8,128)S(1)}, f32[4,8,192]{2,1,0:T(8,128)S(1)}) custom-call(s32[4]{0:T(128)S(1)} %pad_add_fusion.mine_ref.col_ref, bf16[2,3,768,512]{3,2,1,0:T(8,128)(2,1)S(1)} %bitcast.24, bf16[208,768]{1,0:T(8,128)(2,1)S(1)} %collective-permute-done.21.refs_0_, ...), custom_call_target="tpu_custom_call" | custom-call | flops 1 | bytes 1 | tf_op jit(solution)/shard_map/gate_up/pallas_call | solution.py:277
  94.6 2.3 %down.6 = (bf16[192,768]{1,0:T(8,128)(2,1)S(1)}, bf16[192,768]{1,0:T(8,128)(2,1)S(1)}, bf16[192,768]{1,0:T(8,128)(2,1)S(1)}, bf16[192,768]{1,0:T(8,128)(2,1)S(1)}) custom-call(s32[4]{0:T(128)S(1)} %pad_add_fusion.mine_ref.col_ref, f32[4,8,192]{2,1,0:T(8,128)S(1)} %get-tuple-element.120.info_ref, bf16[3,80,512]{2,1,0:T(8,128)(2,1)S(1)} %activate.6.mine_ref, ...), custom_call_target="tpu_custom_call" | custom-call | flops 1 | bytes 1 | tf_op jit(solution)/shard_map/down/pallas_call | solution.py:372
  97.4 2.6 %collective-permute-done.28.refs_1_ = bf16[192,768]{1,0:T(8,128)(2,1)S(1)} collective-permute-done((bf16[192,768]{1,0:T(8,128)(2,1)S(1)}, bf16[192,768]{1,0:T(8,128)(2,1)S(1)}, u32[]{:S(2)}, u32[]{:S(2)}) %collective-permute-start.28) | collective-permute-done | bytes 294944 | tf_op jit(solution)/shard_map/ppermute | solution.py:206
  100.7 3.8 %collective-permute-start.29 = (bf16[192,768]{1,0:T(8,128)(2,1)S(1)}, bf16[192,768]{1,0:T(8,128)(2,1)S(1)}, u32[]{:S(2)}, u32[]{:S(2)}) collective-permute-start(bf16[192,768]{1,0:T(8,128)(2,1)S(1)} %add.122), channel_id=1, source_target_pairs={{0,24},{2,26},{4,28},{6,30},{8,0},{10,2},{12,4},{14,6},{16,8},{18,... | collective-permute-start | bytes 884744 | tf_op jit(solution)/shard_map/ppermute | solution.py:202
  109.6 3.0 %collective-permute-done.33.got_ref = bf16[3,80,512]{2,1,0:T(8,128)(2,1)S(1)} collective-permute-done((bf16[3,80,512]{2,1,0:T(8,128)(2,1)S(1)}, bf16[3,80,512]{2,1,0:T(8,128)(2,1)S(1)}, u32[]{:S(2)}, u32[]{:S(2)}) %collective-permute-start.33) | collective-permute-done | bytes 245792 | tf_op jit(solution)/shard_map/ppermute | solution.py:214
  112.6 2.3 %down.7 = (bf16[192,768]{1,0:T(8,128)(2,1)S(1)}, bf16[192,768]{1,0:T(8,128)(2,1)S(1)}, bf16[192,768]{1,0:T(8,128)(2,1)S(1)}, bf16[192,768]{1,0:T(8,128)(2,1)S(1)}) custom-call(s32[4]{0:T(128)S(1)} %pad_add_fusion.mine_ref.col_ref, f32[4,8,192]{2,1,0:T(8,128)S(1)} %get-tuple-element.141.info_ref, bf16[3,80,512]{2,1,0:T(8,128)(2,1)S(1)} %activate.7.mine_ref, ...), custom_call_target="tpu_custom_call" | custom-call | flops 1 | bytes 1 | tf_op jit(solution)/shard_map/down/pallas_call | solution.py:372
  119.2 2.1 %collective-permute-start.39 = (bf16[192,768]{1,0:T(8,128)(2,1)S(1)}, bf16[192,768]{1,0:T(8,128)(2,1)S(1)}, u32[]{:S(2)}, u32[]{:S(2)}) collective-permute-start(bf16[192,768]{1,0:T(8,128)(2,1)S(1)} %add.124), channel_id=1, source_target_pairs={{0,16},{2,18},{4,20},{6,22},{8,24},{10,26},{12,28},{14,30},{16,0},... | collective-permute-start | bytes 884744 | tf_op jit(solution)/shard_map/ppermute | solution.py:202
  121.3 5.5 %collective-permute-done.37.refs_1_ = bf16[192,768]{1,0:T(8,128)(2,1)S(1)} collective-permute-done((bf16[192,768]{1,0:T(8,128)(2,1)S(1)}, bf16[192,768]{1,0:T(8,128)(2,1)S(1)}, u32[]{:S(2)}, u32[]{:S(2)}) %collective-permute-start.37) | collective-permute-done | bytes 294944 | tf_op jit(solution)/shard_map/ppermute | solution.py:206
  128.7 12.8 %collective-permute-done.39 = bf16[192,768]{1,0:T(8,128)(2,1)S(1)} collective-permute-done((bf16[192,768]{1,0:T(8,128)(2,1)S(1)}, bf16[192,768]{1,0:T(8,128)(2,1)S(1)}, u32[]{:S(2)}, u32[]{:S(2)}) %collective-permute-start.39) | collective-permute-done | bytes 294944 | tf_op jit(solution)/shard_map/ppermute | solution.py:202
  143.9 6.0 %collective-permute-done.41 = f32[768]{0:T(1024)S(1)} collective-permute-done((f32[768]{0:T(1024)S(1)}, f32[768]{0:T(1024)S(1)}, u32[]{:S(2)}, u32[]{:S(2)}) %collective-permute-start.41) | collective-permute-done | bytes 3104 | tf_op jit(solution)/shard_map/ppermute | solution.py:214
  152.9 2.8 %collective-permute-start.45 = (bf16[192,512]{1,0:T(8,128)(2,1)S(1)}, bf16[192,512]{1,0:T(8,128)(2,1)S(1)}, u32[]{:S(2)}, u32[]{:S(2)}) collective-permute-start(bf16[192,512]{1,0:T(8,128)(2,1)S(1)} %keys_values.1.refs_0_), channel_id=1, source_target_pairs={{0,24},{2,26},{4,28},{6,30},{8,0},{10,2},{12,4},{14,6},{16,8},{18,... | collective-permute-start | bytes 589832 | tf_op jit(solution)/shard_map/ppermute | solution.py:202
  156.6 4.8 %collective-permute-done.44.refs_0_ = bf16[192,512]{1,0:T(8,128)(2,1)S(1)} collective-permute-done((bf16[192,512]{1,0:T(8,128)(2,1)S(1)}, bf16[192,512]{1,0:T(8,128)(2,1)S(1)}, u32[]{:S(2)}, u32[]{:S(2)}) %collective-permute-start.44) | collective-permute-done | bytes 196640 | tf_op jit(solution)/shard_map/ppermute | solution.py:202
  162.7 2.1 %collective-permute-start.48 = (bf16[192,512]{1,0:T(8,128)(2,1)S(1)}, bf16[192,512]{1,0:T(8,128)(2,1)S(1)}, u32[]{:S(2)}, u32[]{:S(2)}) collective-permute-start(bf16[192,512]{1,0:T(8,128)(2,1)S(1)} %collective-permute-done.44.refs_0_), channel_id=1, source_target_pairs={{0,8},{2,10},{4,12},{6,14},{8,16},{10,18},{12,20},{14,22},{16,24},... | collective-permute-start | bytes 589832 | tf_op jit(solution)/shard_map/ppermute | solution.py:202
  165.7 3.2 %collective-permute-done.46.refs_2_ = bf16[192,512]{1,0:T(8,128)(2,1)S(1)} collective-permute-done((bf16[192,512]{1,0:T(8,128)(2,1)S(1)}, bf16[192,512]{1,0:T(8,128)(2,1)S(1)}, u32[]{:S(2)}, u32[]{:S(2)}) %collective-permute-start.46) | collective-permute-done | bytes 196640 | tf_op jit(solution)/shard_map/ppermute | solution.py:206
  172.2 4.8 %collective-permute-done.51.refs_6_ = bf16[192,512]{1,0:T(8,128)(2,1)S(1)} collective-permute-done((bf16[192,512]{1,0:T(8,128)(2,1)S(1)}, bf16[192,512]{1,0:T(8,128)(2,1)S(1)}, u32[]{:S(2)}, u32[]{:S(2)}) %collective-permute-start.51) | collective-permute-done | bytes 196640 | tf_op jit(solution)/shard_map/ppermute | solution.py:206
  178.5 3.2 %write_pages.1 = bf16[24,128,512]{2,1,0:T(8,128)(2,1)} custom-call(s32[8,24]{1,0:T(8,128)S(1)} %get-tuple-element.154.page_ref, bf16[2,192,512]{2,1,0:T(8,128)(2,1)S(1)} %stack.19.refs_0_, bf16[2,192,512]{2,1,0:T(8,128)(2,1)S(1)} %collective-permute-done.43.refs_1_, bf16[3,192,512]{2,1,0:T(8,128)(2,1)S(1)} %stack.20.refs_2_, ...), custom_call_target="tpu_custom_call", output_to_operand_aliasing={{}: (9, {})} | custom-call | flops 1073741824 | bytes 1 | tf_op jit(solution)/shard_map/write_pages/pallas_call | solution.py:633
  (146 shorter events, 61.9 us)
Async XLA Ops:
  0.6 10.3 %collective-permute-start = (bf16[192,768]{1,0:T(8,128)(2,1)}, bf16[192,768]{1,0:T(8,128)(2,1)S(1)}, u32[]{:S(2)}, u32[]{:S(2)}) collective-permute-start(bf16[192,768]{1,0:T(8,128)(2,1)} %param.14), channel_id=1, source_target_pairs={{0,1},{1,0},{2,3},{3,2},{4,5},{5,4},{6,7},{7,6},{8,9},{9,8},{10,11... | collective-permute-start | bytes 884744 | tf_op jit(solution)/shard_map/ppermute | solution.py:214
  17.3 12.4 %collective-permute-start.3 = (bf16[208,768]{1,0:T(8,128)(2,1)S(1)}, bf16[208,768]{1,0:T(8,128)(2,1)}, u32[]{:S(2)}, u32[]{:S(2)}) collective-permute-start(bf16[208,768]{1,0:T(8,128)(2,1)S(1)} %pad_maximum_fusion.refs_0_), channel_id=1, source_target_pairs={{0,2},{2,0},{4,6},{6,4},{8,10},{10,8},{12,14},{14,12},{16,18},{18,... | collective-permute-start | bytes 958472 | tf_op jit(solution)/shard_map/ppermute | solution.py:210
  17.3 11.8 %collective-permute-start.5 = (bf16[208,768]{1,0:T(8,128)(2,1)S(1)}, bf16[208,768]{1,0:T(8,128)(2,1)S(1)}, u32[]{:S(2)}, u32[]{:S(2)}) collective-permute-start(bf16[208,768]{1,0:T(8,128)(2,1)S(1)} %pad_maximum_fusion.refs_0_), channel_id=1, source_target_pairs={{0,8},{2,10},{4,12},{6,14},{8,16},{10,18},{12,20},{14,22},{16,24},... | collective-permute-start | bytes 958472 | tf_op jit(solution)/shard_map/ppermute | solution.py:202
  29.1 13.3 %collective-permute-start.6 = (bf16[208,768]{1,0:T(8,128)(2,1)S(1)}, bf16[208,768]{1,0:T(8,128)(2,1)S(1)}, u32[]{:S(2)}, u32[]{:S(2)}) collective-permute-start(bf16[208,768]{1,0:T(8,128)(2,1)S(1)} %collective-permute-done.5.refs_0_), channel_id=1, source_target_pairs={{0,4},{2,6},{4,0},{6,2},{8,12},{10,14},{12,8},{14,10},{16,20},{18,... | collective-permute-start | bytes 958472 | tf_op jit(solution)/shard_map/ppermute | solution.py:206
  29.7 14.6 %collective-permute-start.7 = (bf16[208,768]{1,0:T(8,128)(2,1)S(1)}, bf16[208,768]{1,0:T(8,128)(2,1)S(1)}, u32[]{:S(2)}, u32[]{:S(2)}) collective-permute-start(bf16[208,768]{1,0:T(8,128)(2,1)S(1)} %collective-permute-done.5.refs_0_), channel_id=1, source_target_pairs={{0,2},{2,0},{4,6},{6,4},{8,10},{10,8},{12,14},{14,12},{16,18},{18,... | collective-permute-start | bytes 958472 | tf_op jit(solution)/shard_map/ppermute | solution.py:210
  29.7 13.1 %collective-permute-start.10 = (bf16[208,768]{1,0:T(8,128)(2,1)S(1)}, bf16[208,768]{1,0:T(8,128)(2,1)S(1)}, u32[]{:S(2)}, u32[]{:S(2)}) collective-permute-start(bf16[208,768]{1,0:T(8,128)(2,1)S(1)} %collective-permute-done.5.refs_0_), channel_id=1, source_target_pairs={{0,8},{2,10},{4,12},{6,14},{8,16},{10,18},{12,20},{14,22},{16,24},... | collective-permute-start | bytes 958472 | tf_op jit(solution)/shard_map/ppermute | solution.py:202
  36.2 15.4 %collective-permute-start.9 = (bf16[3,80,1024]{2,1,0:T(8,128)(2,1)S(1)}, bf16[3,80,1024]{2,1,0:T(8,128)(2,1)S(1)}, u32[]{:S(2)}, u32[]{:S(2)}) collective-permute-start(bf16[3,80,1024]{2,1,0:T(8,128)(2,1)S(1)} %get-tuple-element.99), channel_id=1, source_target_pairs={{0,1},{1,0},{2,3},{3,2},{4,5},{5,4},{6,7},{7,6},{8,9},{9,8},{10,11... | collective-permute-start | bytes 1474568 | tf_op jit(solution)/shard_map/ppermute | solution.py:214
  42.8 12.6 %collective-permute-start.11 = (bf16[208,768]{1,0:T(8,128)(2,1)S(1)}, bf16[208,768]{1,0:T(8,128)(2,1)S(1)}, u32[]{:S(2)}, u32[]{:S(2)}) collective-permute-start(bf16[208,768]{1,0:T(8,128)(2,1)S(1)} %collective-permute-done.10.refs_0_), channel_id=1, source_target_pairs={{0,4},{2,6},{4,0},{6,2},{8,12},{10,14},{12,8},{14,10},{16,20},{18,... | collective-permute-start | bytes 958472 | tf_op jit(solution)/shard_map/ppermute | solution.py:206
  47.3 17.2 %collective-permute-start.14 = (bf16[3,80,1024]{2,1,0:T(8,128)(2,1)S(1)}, bf16[3,80,1024]{2,1,0:T(8,128)(2,1)S(1)}, u32[]{:S(2)}, u32[]{:S(2)}) collective-permute-start(bf16[3,80,1024]{2,1,0:T(8,128)(2,1)S(1)} %get-tuple-element.108), channel_id=1, source_target_pairs={{0,1},{1,0},{2,3},{3,2},{4,5},{5,4},{6,7},{7,6},{8,9},{9,8},{10,11... | collective-permute-start | bytes 1474568 | tf_op jit(solution)/shard_map/ppermute | solution.py:214
  47.9 10.5 %collective-permute-start.21 = (bf16[208,768]{1,0:T(8,128)(2,1)S(1)}, bf16[208,768]{1,0:T(8,128)(2,1)S(1)}, u32[]{:S(2)}, u32[]{:S(2)}) collective-permute-start(bf16[208,768]{1,0:T(8,128)(2,1)S(1)} %pad_maximum_fusion.refs_0_), channel_id=1, source_target_pairs={{0,24},{2,26},{4,28},{6,30},{8,0},{10,2},{12,4},{14,6},{16,8},{18,... | collective-permute-start | bytes 958472 | tf_op jit(solution)/shard_map/ppermute | solution.py:202
  55.9 10.8 %collective-permute-start.15 = (bf16[3,80,512]{2,1,0:T(8,128)(2,1)S(1)}, bf16[3,80,512]{2,1,0:T(8,128)(2,1)S(1)}, u32[]{:S(2)}, u32[]{:S(2)}) collective-permute-start(bf16[3,80,512]{2,1,0:T(8,128)(2,1)S(1)} %activate.4.mine_ref), channel_id=1, source_target_pairs={{0,1},{1,0},{2,3},{3,2},{4,5},{5,4},{6,7},{7,6},{8,9},{9,8},{10,11... | collective-permute-start | bytes 737288 | tf_op jit(solution)/shard_map/ppermute | solution.py:214
  58.4 12.1 %collective-permute-start.22 = (bf16[208,768]{1,0:T(8,128)(2,1)S(1)}, bf16[208,768]{1,0:T(8,128)(2,1)S(1)}, u32[]{:S(2)}, u32[]{:S(2)}) collective-permute-start(bf16[208,768]{1,0:T(8,128)(2,1)S(1)} %collective-permute-done.21.refs_0_), channel_id=1, source_target_pairs={{0,4},{2,6},{4,0},{6,2},{8,12},{10,14},{12,8},{14,10},{16,20},{18,... | collective-permute-start | bytes 958472 | tf_op jit(solution)/shard_map/ppermute | solution.py:206
  63.0 21.1 %collective-permute-start.20 = (bf16[3,80,1024]{2,1,0:T(8,128)(2,1)S(1)}, bf16[3,80,1024]{2,1,0:T(8,128)(2,1)S(1)}, u32[]{:S(2)}, u32[]{:S(2)}) collective-permute-start(bf16[3,80,1024]{2,1,0:T(8,128)(2,1)S(1)} %get-tuple-element.121), channel_id=1, source_target_pairs={{0,1},{1,0},{2,3},{3,2},{4,5},{5,4},{6,7},{7,6},{8,9},{9,8},{10,11... | collective-permute-start | bytes 1474568 | tf_op jit(solution)/shard_map/ppermute | solution.py:214
  69.6 12.1 %collective-permute-start.19 = (bf16[3,80,512]{2,1,0:T(8,128)(2,1)S(1)}, bf16[3,80,512]{2,1,0:T(8,128)(2,1)S(1)}, u32[]{:S(2)}, u32[]{:S(2)}) collective-permute-start(bf16[3,80,512]{2,1,0:T(8,128)(2,1)S(1)} %activate.5.mine_ref), channel_id=1, source_target_pairs={{0,1},{1,0},{2,3},{3,2},{4,5},{5,4},{6,7},{7,6},{8,9},{9,8},{10,11... | collective-permute-start | bytes 737288 | tf_op jit(solution)/shard_map/ppermute | solution.py:214
  70.6 15.1 %collective-permute-start.24 = (bf16[208,768]{1,0:T(8,128)(2,1)S(1)}, bf16[208,768]{1,0:T(8,128)(2,1)S(1)}, u32[]{:S(2)}, u32[]{:S(2)}) collective-permute-start(bf16[208,768]{1,0:T(8,128)(2,1)S(1)} %collective-permute-done.22.refs_1_), channel_id=1, source_target_pairs={{0,2},{2,0},{4,6},{6,4},{8,10},{10,8},{12,14},{14,12},{16,18},{18,... | collective-permute-start | bytes 958472 | tf_op jit(solution)/shard_map/ppermute | solution.py:210
  70.7 16.4 %collective-permute-start.23 = (bf16[208,768]{1,0:T(8,128)(2,1)S(1)}, bf16[208,768]{1,0:T(8,128)(2,1)S(1)}, u32[]{:S(2)}, u32[]{:S(2)}) collective-permute-start(bf16[208,768]{1,0:T(8,128)(2,1)S(1)} %collective-permute-done.21.refs_0_), channel_id=1, source_target_pairs={{0,2},{2,0},{4,6},{6,4},{8,10},{10,8},{12,14},{14,12},{16,18},{18,... | collective-permute-start | bytes 958472 | tf_op jit(solution)/shard_map/ppermute | solution.py:210
  71.8 19.1 %collective-permute-start.18 = (bf16[192,768]{1,0:T(8,128)(2,1)S(1)}, bf16[192,768]{1,0:T(8,128)(2,1)S(1)}, u32[]{:S(2)}, u32[]{:S(2)}) collective-permute-start(bf16[192,768]{1,0:T(8,128)(2,1)S(1)} %get-tuple-element.116), channel_id=1, source_target_pairs={{0,4},{2,6},{4,0},{6,2},{8,12},{10,14},{12,8},{14,10},{16,20},{18,... | collective-permute-start | bytes 884744 | tf_op jit(solution)/shard_map/ppermute | solution.py:206
  85.7 8.9 %collective-permute-start.27 = (bf16[3,80,512]{2,1,0:T(8,128)(2,1)S(1)}, bf16[3,80,512]{2,1,0:T(8,128)(2,1)S(1)}, u32[]{:S(2)}, u32[]{:S(2)}) collective-permute-start(bf16[3,80,512]{2,1,0:T(8,128)(2,1)S(1)} %activate.6.mine_ref), channel_id=1, source_target_pairs={{0,1},{1,0},{2,3},{3,2},{4,5},{5,4},{6,7},{7,6},{8,9},{9,8},{10,11... | collective-permute-start | bytes 737288 | tf_op jit(solution)/shard_map/ppermute | solution.py:214
  90.1 15.0 %collective-permute-start.32 = (bf16[3,80,1024]{2,1,0:T(8,128)(2,1)S(1)}, bf16[3,80,1024]{2,1,0:T(8,128)(2,1)S(1)}, u32[]{:S(2)}, u32[]{:S(2)}) collective-permute-start(bf16[3,80,1024]{2,1,0:T(8,128)(2,1)S(1)} %get-tuple-element.142), channel_id=1, source_target_pairs={{0,1},{1,0},{2,3},{3,2},{4,5},{5,4},{6,7},{7,6},{8,9},{9,8},{10,11... | collective-permute-start | bytes 1474568 | tf_op jit(solution)/shard_map/ppermute | solution.py:214
  91.6 8.5 %collective-permute-start.28 = (bf16[192,768]{1,0:T(8,128)(2,1)S(1)}, bf16[192,768]{1,0:T(8,128)(2,1)S(1)}, u32[]{:S(2)}, u32[]{:S(2)}) collective-permute-start(bf16[192,768]{1,0:T(8,128)(2,1)S(1)} %get-tuple-element.130), channel_id=1, source_target_pairs={{0,4},{2,6},{4,0},{6,2},{8,12},{10,14},{12,8},{14,10},{16,20},{18,... | collective-permute-start | bytes 884744 | tf_op jit(solution)/shard_map/ppermute | solution.py:206
  96.9 7.6 %collective-permute-start.30 = (bf16[192,768]{1,0:T(8,128)(2,1)S(1)}, bf16[192,768]{1,0:T(8,128)(2,1)S(1)}, u32[]{:S(2)}, u32[]{:S(2)}) collective-permute-start(bf16[192,768]{1,0:T(8,128)(2,1)S(1)} %get-tuple-element.137), channel_id=1, source_target_pairs={{0,2},{2,0},{4,6},{6,4},{8,10},{10,8},{12,14},{14,12},{16,18},{18,... | collective-permute-start | bytes 884744 | tf_op jit(solution)/shard_map/ppermute | solution.py:210
  100.7 8.9 %collective-permute-start.29 = (bf16[192,768]{1,0:T(8,128)(2,1)S(1)}, bf16[192,768]{1,0:T(8,128)(2,1)S(1)}, u32[]{:S(2)}, u32[]{:S(2)}) collective-permute-start(bf16[192,768]{1,0:T(8,128)(2,1)S(1)} %add.122), channel_id=1, source_target_pairs={{0,24},{2,26},{4,28},{6,30},{8,0},{10,2},{12,4},{14,6},{16,8},{18,... | collective-permute-start | bytes 884744 | tf_op jit(solution)/shard_map/ppermute | solution.py:202
  107.5 8.0 %collective-permute-start.34 = (bf16[192,768]{1,0:T(8,128)(2,1)S(1)}, bf16[192,768]{1,0:T(8,128)(2,1)S(1)}, u32[]{:S(2)}, u32[]{:S(2)}) collective-permute-start(bf16[192,768]{1,0:T(8,128)(2,1)S(1)} %get-tuple-element.139), channel_id=1, source_target_pairs={{0,4},{2,6},{4,0},{6,2},{8,12},{10,14},{12,8},{14,10},{16,20},{18,... | collective-permute-start | bytes 884744 | tf_op jit(solution)/shard_map/ppermute | solution.py:206
  117.7 9.1 %collective-permute-start.37 = (bf16[192,768]{1,0:T(8,128)(2,1)S(1)}, bf16[192,768]{1,0:T(8,128)(2,1)S(1)}, u32[]{:S(2)}, u32[]{:S(2)}) collective-permute-start(bf16[192,768]{1,0:T(8,128)(2,1)S(1)} %get-tuple-element.151), channel_id=1, source_target_pairs={{0,4},{2,6},{4,0},{6,2},{8,12},{10,14},{12,8},{14,10},{16,20},{18,... | collective-permute-start | bytes 884744 | tf_op jit(solution)/shard_map/ppermute | solution.py:206
  119.2 22.3 %collective-permute-start.39 = (bf16[192,768]{1,0:T(8,128)(2,1)S(1)}, bf16[192,768]{1,0:T(8,128)(2,1)S(1)}, u32[]{:S(2)}, u32[]{:S(2)}) collective-permute-start(bf16[192,768]{1,0:T(8,128)(2,1)S(1)} %add.124), channel_id=1, source_target_pairs={{0,16},{2,18},{4,20},{6,22},{8,24},{10,26},{12,28},{14,30},{16,0},... | collective-permute-start | bytes 884744 | tf_op jit(solution)/shard_map/ppermute | solution.py:202
  127.4 14.1 %collective-permute-start.38 = (bf16[192,768]{1,0:T(8,128)(2,1)S(1)}, bf16[192,768]{1,0:T(8,128)(2,1)S(1)}, u32[]{:S(2)}, u32[]{:S(2)}) collective-permute-start(bf16[192,768]{1,0:T(8,128)(2,1)S(1)} %add.126), channel_id=1, source_target_pairs={{0,8},{2,10},{4,12},{6,14},{8,16},{10,18},{12,20},{14,22},{16,24},... | collective-permute-start | bytes 884744 | tf_op jit(solution)/shard_map/ppermute | solution.py:202
  141.8 8.1 %collective-permute-start.40 = (bf16[192,768]{1,0:T(8,128)(2,1)S(1)}, bf16[192,768]{1,0:T(8,128)(2,1)S(1)}, u32[]{:S(2)}, u32[]{:S(2)}) collective-permute-start(bf16[192,768]{1,0:T(8,128)(2,1)S(1)} %fusion.7.own_ref), channel_id=1, source_target_pairs={{0,1},{1,0},{2,3},{3,2},{4,5},{5,4},{6,7},{7,6},{8,9},{9,8},{10,11... | collective-permute-start | bytes 884744 | tf_op jit(solution)/shard_map/ppermute | solution.py:214
  151.5 9.9 %collective-permute-start.44 = (bf16[192,512]{1,0:T(8,128)(2,1)S(1)}, bf16[192,512]{1,0:T(8,128)(2,1)S(1)}, u32[]{:S(2)}, u32[]{:S(2)}) collective-permute-start(bf16[192,512]{1,0:T(8,128)(2,1)S(1)} %keys_values.1.refs_0_), channel_id=1, source_target_pairs={{0,8},{2,10},{4,12},{6,14},{8,16},{10,18},{12,20},{14,22},{16,24},... | collective-permute-start | bytes 589832 | tf_op jit(solution)/shard_map/ppermute | solution.py:202
  152.9 12.0 %collective-permute-start.45 = (bf16[192,512]{1,0:T(8,128)(2,1)S(1)}, bf16[192,512]{1,0:T(8,128)(2,1)S(1)}, u32[]{:S(2)}, u32[]{:S(2)}) collective-permute-start(bf16[192,512]{1,0:T(8,128)(2,1)S(1)} %keys_values.1.refs_0_), channel_id=1, source_target_pairs={{0,24},{2,26},{4,28},{6,30},{8,0},{10,2},{12,4},{14,6},{16,8},{18,... | collective-permute-start | bytes 589832 | tf_op jit(solution)/shard_map/ppermute | solution.py:202
  162.7 8.6 %collective-permute-start.48 = (bf16[192,512]{1,0:T(8,128)(2,1)S(1)}, bf16[192,512]{1,0:T(8,128)(2,1)S(1)}, u32[]{:S(2)}, u32[]{:S(2)}) collective-permute-start(bf16[192,512]{1,0:T(8,128)(2,1)S(1)} %collective-permute-done.44.refs_0_), channel_id=1, source_target_pairs={{0,8},{2,10},{4,12},{6,14},{8,16},{10,18},{12,20},{14,22},{16,24},... | collective-permute-start | bytes 589832 | tf_op jit(solution)/shard_map/ppermute | solution.py:202
  169.0 9.5 %collective-permute-start.47 = (bf16[3,192,512]{2,1,0:T(8,128)(2,1)S(1)}, bf16[3,192,512]{2,1,0:T(8,128)(2,1)S(1)}, u32[]{:S(2)}, u32[]{:S(2)}) collective-permute-start(bf16[3,192,512]{2,1,0:T(8,128)(2,1)S(1)} %stack.20.refs_2_), channel_id=1, source_target_pairs={{0,2},{2,0},{4,6},{6,4},{8,10},{10,8},{12,14},{14,12},{16,18},{18,... | collective-permute-start | bytes 1769480 | tf_op jit(solution)/shard_map/ppermute | solution.py:210
  169.1 7.9 %collective-permute-start.43 = (bf16[2,192,512]{2,1,0:T(8,128)(2,1)S(1)}, bf16[2,192,512]{2,1,0:T(8,128)(2,1)S(1)}, u32[]{:S(2)}, u32[]{:S(2)}) collective-permute-start(bf16[2,192,512]{2,1,0:T(8,128)(2,1)S(1)} %stack.19.refs_0_), channel_id=1, source_target_pairs={{0,2},{2,0},{4,6},{6,4},{8,10},{10,8},{12,14},{14,12},{16,18},{18,... | collective-permute-start | bytes 1179656 | tf_op jit(solution)/shard_map/ppermute | solution.py:210
  (33 other events, 231.4 us)

commit v5 on v4

--- a/solution.py
+++ b/solution.py
@@ -705,7 +705,9 @@
         axis=1,
     )
     meta = jnp.concatenate([names, gates], axis=0).astype(BF)
-    first_half, meta, attn_other = lax.optimization_barrier((first_half, meta, attn_other))
+    first_half, meta, attn_other, gain_other = lax.optimization_barrier(
+        (first_half, meta, attn_other, y_move(gain_moe))
+    )
     hidden = (first_half + dot(attn_other, proj_other)).astype(BF)
     hidden = lax.optimization_barrier(hidden)
     res_f = hidden.astype(F32)
@@ -822,7 +824,6 @@
     mixture = mixture + moving["z", 2].astype(F32)
     layer_out = lax.optimization_barrier((res_f + mixture).astype(BF))
 
-    gain_other = y_move(after(gain_moe, sums[2][0]))
     rotated = keys_values(
         layer_out, y_move(layer_out), gain_moe, gain_other, kv_w, cosine, sine
     )

time: 184 us -> 183 us (level)
  no operation moved by 1% of the time
where the time goes in v5:
time: 183 us; the launch traced here: 182 us
  waiting for transfers between devices  75 us (41%)
  starting transfers between devices  53.6 us (29%)
  Pallas kernels  44.2 us (24%)
  local copies, waits for them, and re-layouts  3.42 us (2%)
  other arithmetic  2.9 us (2%)
  matrix products  1.85 us (1%)
    ppermute x12, waiting for transfers between devices, y_move(): return lax.ppermute(value, 'mp', [(0, 1), (1, 0)])  27.5 us
    ppermute x9, waiting for transfers between devices, z_move(): return lax.ppermute(value, 'dp', moves(dz, 0, 0))  23.7 us
    ppermute x12, waiting for transfers between devices, x_move(): return lax.ppermute(value, 'dp', moves(0, 1, 0))  21.3 us
    ppermute x9, starting transfers between devices, z_move(): return lax.ppermute(value, 'dp', moves(dz, 0, 0))  18.7 us
    ppermute x12, starting transfers between devices, y_move(): return lax.ppermute(value, 'mp', [(0, 1), (1, 0)])  15.8 us
    ppermute x12, starting transfers between devices, x_move(): return lax.ppermute(value, 'dp', moves(0, 1, 0))  14.9 us
    pallas_call x4, Pallas kernels, gate_up(): pl.pallas_call(functools.partial(gate_up_kernel, n), out_shape=(jax.Shape...  13.2 us
    pallas_call x4, Pallas kernels, down(): pl.pallas_call(down_kernel, out_shape=[jax.ShapeDtypeStruct((tokens, widt...  9.13 us
  transfers between devices with their start and end apart: 53, of which 23 were waited for; matrix products, arithmetic and copies ran while one was open for 4% of the time, Pallas kernels for 21%

profile of v5, /device:TPU:0, one launch (start us, length us, event | category | flops | bytes accessed | tf_op | source)
XLA Modules:
  0.0 182.3 jit_solution(2207985164650757045)
XLA Ops:
  0.7 3.1 %collective-permute-start = (bf16[192,768]{1,0:T(8,128)(2,1)}, bf16[192,768]{1,0:T(8,128)(2,1)S(1)}, u32[]{:S(2)}, u32[]{:S(2)}) collective-permute-start(bf16[192,768]{1,0:T(8,128)(2,1)} %param.14), channel_id=1, source_target_pairs={{0,1},{1,0},{2,3},{3,2},{4,5},{5,4},{6,7},{7,6},{8,9},{9,8},{10,11... | collective-permute-start | bytes 884744 | tf_op jit(solution)/shard_map/ppermute | solution.py:214
  6.0 5.0 %collective-permute-done.1 = f32[768]{0:T(1024)S(1)} collective-permute-done((f32[768]{0:T(1024)}, f32[768]{0:T(1024)S(1)}, u32[]{:S(2)}, u32[]{:S(2)}) %collective-permute-start.1) | collective-permute-done | bytes 3104 | tf_op jit(solution)/shard_map/ppermute | solution.py:214
  13.5 1.8 %collective-permute-done.2 = f32[192]{0:T(256)S(1)} collective-permute-done((f32[192]{0:T(256)S(1)}, f32[192]{0:T(256)S(1)}, u32[]{:S(2)}, u32[]{:S(2)}) %collective-permute-start.2) | collective-permute-done | bytes 800 | tf_op jit(solution)/shard_map/ppermute | solution.py:214
  19.1 4.0 %collective-permute-done.3.refs_1_ = bf16[208,768]{1,0:T(8,128)(2,1)S(1)} collective-permute-done((bf16[208,768]{1,0:T(8,128)(2,1)S(1)}, bf16[208,768]{1,0:T(8,128)(2,1)S(1)}, u32[]{:S(2)}, u32[]{:S(2)}) %collective-permute-start.3) | collective-permute-done | bytes 319520 | tf_op jit(solution)/shard_map/ppermute | solution.py:206
  23.2 3.2 %copy.22 = bf16[3,768,2,512]{3,1,0,2:T(8,128)(2,1)S(1)} copy(bf16[3,768,2,512]{3,2,1,0:T(2,128)(2,1)} %param.20) | data formatting | bytes 9437184 | tf_op jit(solution)/shard_map/optimization_barrier | solution.py:218
  26.4 2.9 %collective-permute-done.6.refs_0_ = bf16[208,768]{1,0:T(8,128)(2,1)S(1)} collective-permute-done((bf16[208,768]{1,0:T(8,128)(2,1)S(1)}, bf16[208,768]{1,0:T(8,128)(2,1)S(1)}, u32[]{:S(2)}, u32[]{:S(2)}) %collective-permute-start.6) | collective-permute-done | bytes 319520 | tf_op jit(solution)/shard_map/ppermute | solution.py:202
  29.8 4.0 %gate_up.4 = (bf16[3,80,1024]{2,1,0:T(8,128)(2,1)S(1)}, f32[3,80,1024]{2,1,0:T(8,128)S(1)}, f32[4,8,192]{2,1,0:T(8,128)S(1)}) custom-call(s32[4]{0:T(128)S(1)} %pad_add_fusion.mine_ref.col_ref, bf16[2,3,768,512]{3,2,1,0:T(8,128)(2,1)S(1)} %bitcast.21, bf16[208,768]{1,0:T(8,128)(2,1)S(1)} %pad_maximum_fusion.refs_0_, ...), custom_call_target="tpu_custom_call" | custom-call | flops 1 | bytes 1 | tf_op jit(solution)/shard_map/gate_up/pallas_call | solution.py:277
  33.9 2.4 %turn.1.w_ref = bf16[2,768,1024]{2,1,0:T(8,128)(2,1)S(1)} custom-call(s32[4]{0:T(128)S(1)} %pad_add_fusion.mine_ref.col_ref, bf16[1536,512]{1,0:T(8,128)(2,1)S(1)} %copy-done.3), custom_call_target="tpu_custom_call" | custom-call | flops 1 | bytes 1 | tf_op jit(solution)/shard_map/turn/pallas_call | solution.py:542
  37.9 3.1 %page_list.1 = (s32[8,24]{1,0:T(8,128)S(1)}, f32[192,128]{1,0:T(8,128)S(1)}) custom-call(s32[4]{0:T(128)S(1)} %pad_add_fusion.mine_ref.col_ref, s32[16]{0:T(128)S(1)} %copy-done.5, s32[32]{0:T(128)S(1)} %copy-done.6, s32[48,8]{1,0:T(8,128)S(1)} %broadcast_maximum_fusion.table_ref), custom_call_target="tpu_custom_call" | custom-call | flops 1 | bytes 1 | tf_op jit(solution)/shard_map/page_list/pallas_call | solution.py:516
  44.4 3.0 %gate_up.5 = (bf16[3,80,1024]{2,1,0:T(8,128)(2,1)S(1)}, f32[3,80,1024]{2,1,0:T(8,128)S(1)}, f32[4,8,192]{2,1,0:T(8,128)S(1)}) custom-call(s32[4]{0:T(128)S(1)} %pad_add_fusion.mine_ref.col_ref, bf16[2,3,768,512]{3,2,1,0:T(8,128)(2,1)S(1)} %bitcast.22, bf16[208,768]{1,0:T(8,128)(2,1)S(1)} %collective-permute-done.6.refs_0_, ...), custom_call_target="tpu_custom_call" | custom-call | flops 1 | bytes 1 | tf_op jit(solution)/shard_map/gate_up/pallas_call | solution.py:277
  48.0 3.7 %collective-permute-start.22 = (bf16[208,768]{1,0:T(8,128)(2,1)S(1)}, bf16[208,768]{1,0:T(8,128)(2,1)S(1)}, u32[]{:S(2)}, u32[]{:S(2)}) collective-permute-start(bf16[208,768]{1,0:T(8,128)(2,1)S(1)} %pad_maximum_fusion.refs_0_), channel_id=1, source_target_pairs={{0,24},{2,26},{4,28},{6,30},{8,0},{10,2},{12,4},{14,6},{16,8},{18,... | collective-permute-start | bytes 958472 | tf_op jit(solution)/shard_map/ppermute | solution.py:202
  52.8 2.7 %copy_cache.1.refs_8_ = bf16[24,128,512]{2,1,0:T(8,128)(2,1)} custom-call(bf16[24,128,512]{2,1,0:T(8,128)(2,1)S(1)} %copy-done.2), custom_call_target="tpu_custom_call" | custom-call | flops 1 | bytes 1 | tf_op jit(solution)/shard_map/copy_cache/pallas_call | solution.py:440
  60.0 3.0 %gate_up.6 = (bf16[3,80,1024]{2,1,0:T(8,128)(2,1)S(1)}, f32[3,80,1024]{2,1,0:T(8,128)S(1)}, f32[4,8,192]{2,1,0:T(8,128)S(1)}) custom-call(s32[4]{0:T(128)S(1)} %pad_add_fusion.mine_ref.col_ref, bf16[2,3,768,512]{3,2,1,0:T(8,128)(2,1)S(1)} %bitcast.23, bf16[208,768]{1,0:T(8,128)(2,1)S(1)} %collective-permute-done.11.refs_0_, ...), custom_call_target="tpu_custom_call" | custom-call | flops 1 | bytes 1 | tf_op jit(solution)/shard_map/gate_up/pallas_call | solution.py:277
  66.9 2.3 %down.4 = (bf16[192,768]{1,0:T(8,128)(2,1)S(1)}, bf16[192,768]{1,0:T(8,128)(2,1)S(1)}, bf16[192,768]{1,0:T(8,128)(2,1)S(1)}, bf16[192,768]{1,0:T(8,128)(2,1)S(1)}) custom-call(s32[4]{0:T(128)S(1)} %pad_add_fusion.mine_ref.col_ref, f32[4,8,192]{2,1,0:T(8,128)S(1)} %get-tuple-element.98.info_ref, bf16[3,80,512]{2,1,0:T(8,128)(2,1)S(1)} %activate.4.mine_ref, ...), custom_call_target="tpu_custom_call" | custom-call | flops 1 | bytes 1 | tf_op jit(solution)/shard_map/down/pallas_call | solution.py:372
  73.4 8.4 %collective-permute-done.20.got_ref = bf16[3,80,512]{2,1,0:T(8,128)(2,1)S(1)} collective-permute-done((bf16[3,80,512]{2,1,0:T(8,128)(2,1)S(1)}, bf16[3,80,512]{2,1,0:T(8,128)(2,1)S(1)}, u32[]{:S(2)}, u32[]{:S(2)}) %collective-permute-start.20) | collective-permute-done | bytes 245792 | tf_op jit(solution)/shard_map/ppermute | solution.py:214
  81.8 2.3 %down.5 = (bf16[192,768]{1,0:T(8,128)(2,1)S(1)}, bf16[192,768]{1,0:T(8,128)(2,1)S(1)}, bf16[192,768]{1,0:T(8,128)(2,1)S(1)}, bf16[192,768]{1,0:T(8,128)(2,1)S(1)}) custom-call(s32[4]{0:T(128)S(1)} %pad_add_fusion.mine_ref.col_ref, f32[4,8,192]{2,1,0:T(8,128)S(1)} %get-tuple-element.107.info_ref, bf16[3,80,512]{2,1,0:T(8,128)(2,1)S(1)} %activate.5.mine_ref, ...), custom_call_target="tpu_custom_call" | custom-call | flops 1 | bytes 1 | tf_op jit(solution)/shard_map/down/pallas_call | solution.py:372
  87.2 3.0 %gate_up.7 = (bf16[3,80,1024]{2,1,0:T(8,128)(2,1)S(1)}, f32[3,80,1024]{2,1,0:T(8,128)S(1)}, f32[4,8,192]{2,1,0:T(8,128)S(1)}) custom-call(s32[4]{0:T(128)S(1)} %pad_add_fusion.mine_ref.col_ref, bf16[2,3,768,512]{3,2,1,0:T(8,128)(2,1)S(1)} %bitcast.24, bf16[208,768]{1,0:T(8,128)(2,1)S(1)} %collective-permute-done.22.refs_0_, ...), custom_call_target="tpu_custom_call" | custom-call | flops 1 | bytes 1 | tf_op jit(solution)/shard_map/gate_up/pallas_call | solution.py:277
  94.7 2.3 %down.6 = (bf16[192,768]{1,0:T(8,128)(2,1)S(1)}, bf16[192,768]{1,0:T(8,128)(2,1)S(1)}, bf16[192,768]{1,0:T(8,128)(2,1)S(1)}, bf16[192,768]{1,0:T(8,128)(2,1)S(1)}) custom-call(s32[4]{0:T(128)S(1)} %pad_add_fusion.mine_ref.col_ref, f32[4,8,192]{2,1,0:T(8,128)S(1)} %get-tuple-element.120.info_ref, bf16[3,80,512]{2,1,0:T(8,128)(2,1)S(1)} %activate.6.mine_ref, ...), custom_call_target="tpu_custom_call" | custom-call | flops 1 | bytes 1 | tf_op jit(solution)/shard_map/down/pallas_call | solution.py:372
  97.6 2.6 %collective-permute-done.29.refs_1_ = bf16[192,768]{1,0:T(8,128)(2,1)S(1)} collective-permute-done((bf16[192,768]{1,0:T(8,128)(2,1)S(1)}, bf16[192,768]{1,0:T(8,128)(2,1)S(1)}, u32[]{:S(2)}, u32[]{:S(2)}) %collective-permute-start.29) | collective-permute-done | bytes 294944 | tf_op jit(solution)/shard_map/ppermute | solution.py:206
  100.8 3.8 %collective-permute-start.30 = (bf16[192,768]{1,0:T(8,128)(2,1)S(1)}, bf16[192,768]{1,0:T(8,128)(2,1)S(1)}, u32[]{:S(2)}, u32[]{:S(2)}) collective-permute-start(bf16[192,768]{1,0:T(8,128)(2,1)S(1)} %add.122), channel_id=1, source_target_pairs={{0,24},{2,26},{4,28},{6,30},{8,0},{10,2},{12,4},{14,6},{16,8},{18,... | collective-permute-start | bytes 884744 | tf_op jit(solution)/shard_map/ppermute | solution.py:202
  109.7 3.0 %collective-permute-done.34.got_ref = bf16[3,80,512]{2,1,0:T(8,128)(2,1)S(1)} collective-permute-done((bf16[3,80,512]{2,1,0:T(8,128)(2,1)S(1)}, bf16[3,80,512]{2,1,0:T(8,128)(2,1)S(1)}, u32[]{:S(2)}, u32[]{:S(2)}) %collective-permute-start.34) | collective-permute-done | bytes 245792 | tf_op jit(solution)/shard_map/ppermute | solution.py:214
  112.7 2.3 %down.7 = (bf16[192,768]{1,0:T(8,128)(2,1)S(1)}, bf16[192,768]{1,0:T(8,128)(2,1)S(1)}, bf16[192,768]{1,0:T(8,128)(2,1)S(1)}, bf16[192,768]{1,0:T(8,128)(2,1)S(1)}) custom-call(s32[4]{0:T(128)S(1)} %pad_add_fusion.mine_ref.col_ref, f32[4,8,192]{2,1,0:T(8,128)S(1)} %get-tuple-element.141.info_ref, bf16[3,80,512]{2,1,0:T(8,128)(2,1)S(1)} %activate.7.mine_ref, ...), custom_call_target="tpu_custom_call" | custom-call | flops 1 | bytes 1 | tf_op jit(solution)/shard_map/down/pallas_call | solution.py:372
  119.3 2.1 %collective-permute-start.40 = (bf16[192,768]{1,0:T(8,128)(2,1)S(1)}, bf16[192,768]{1,0:T(8,128)(2,1)S(1)}, u32[]{:S(2)}, u32[]{:S(2)}) collective-permute-start(bf16[192,768]{1,0:T(8,128)(2,1)S(1)} %add.124), channel_id=1, source_target_pairs={{0,16},{2,18},{4,20},{6,22},{8,24},{10,26},{12,28},{14,30},{16,0},... | collective-permute-start | bytes 884744 | tf_op jit(solution)/shard_map/ppermute | solution.py:202
  121.4 5.5 %collective-permute-done.38.refs_1_ = bf16[192,768]{1,0:T(8,128)(2,1)S(1)} collective-permute-done((bf16[192,768]{1,0:T(8,128)(2,1)S(1)}, bf16[192,768]{1,0:T(8,128)(2,1)S(1)}, u32[]{:S(2)}, u32[]{:S(2)}) %collective-permute-start.38) | collective-permute-done | bytes 294944 | tf_op jit(solution)/shard_map/ppermute | solution.py:206
  128.8 12.8 %collective-permute-done.40 = bf16[192,768]{1,0:T(8,128)(2,1)S(1)} collective-permute-done((bf16[192,768]{1,0:T(8,128)(2,1)S(1)}, bf16[192,768]{1,0:T(8,128)(2,1)S(1)}, u32[]{:S(2)}, u32[]{:S(2)}) %collective-permute-start.40) | collective-permute-done | bytes 294944 | tf_op jit(solution)/shard_map/ppermute | solution.py:202
  143.2 6.7 %collective-permute-done.41.other_ref = bf16[192,768]{1,0:T(8,128)(2,1)S(1)} collective-permute-done((bf16[192,768]{1,0:T(8,128)(2,1)S(1)}, bf16[192,768]{1,0:T(8,128)(2,1)S(1)}, u32[]{:S(2)}, u32[]{:S(2)}) %collective-permute-start.41) | collective-permute-done | bytes 294944 | tf_op jit(solution)/shard_map/ppermute | solution.py:214
  152.9 2.8 %collective-permute-start.45 = (bf16[192,512]{1,0:T(8,128)(2,1)S(1)}, bf16[192,512]{1,0:T(8,128)(2,1)S(1)}, u32[]{:S(2)}, u32[]{:S(2)}) collective-permute-start(bf16[192,512]{1,0:T(8,128)(2,1)S(1)} %keys_values.1.refs_0_), channel_id=1, source_target_pairs={{0,24},{2,26},{4,28},{6,30},{8,0},{10,2},{12,4},{14,6},{16,8},{18,... | collective-permute-start | bytes 589832 | tf_op jit(solution)/shard_map/ppermute | solution.py:202
  156.7 4.8 %collective-permute-done.44.refs_0_ = bf16[192,512]{1,0:T(8,128)(2,1)S(1)} collective-permute-done((bf16[192,512]{1,0:T(8,128)(2,1)S(1)}, bf16[192,512]{1,0:T(8,128)(2,1)S(1)}, u32[]{:S(2)}, u32[]{:S(2)}) %collective-permute-start.44) | collective-permute-done | bytes 196640 | tf_op jit(solution)/shard_map/ppermute | solution.py:202
  162.8 2.1 %collective-permute-start.48 = (bf16[192,512]{1,0:T(8,128)(2,1)S(1)}, bf16[192,512]{1,0:T(8,128)(2,1)S(1)}, u32[]{:S(2)}, u32[]{:S(2)}) collective-permute-start(bf16[192,512]{1,0:T(8,128)(2,1)S(1)} %collective-permute-done.44.refs_0_), channel_id=1, source_target_pairs={{0,8},{2,10},{4,12},{6,14},{8,16},{10,18},{12,20},{14,22},{16,24},... | collective-permute-start | bytes 589832 | tf_op jit(solution)/shard_map/ppermute | solution.py:202
  165.7 3.2 %collective-permute-done.46.refs_2_ = bf16[192,512]{1,0:T(8,128)(2,1)S(1)} collective-permute-done((bf16[192,512]{1,0:T(8,128)(2,1)S(1)}, bf16[192,512]{1,0:T(8,128)(2,1)S(1)}, u32[]{:S(2)}, u32[]{:S(2)}) %collective-permute-start.46) | collective-permute-done | bytes 196640 | tf_op jit(solution)/shard_map/ppermute | solution.py:206
  172.2 4.9 %collective-permute-done.51.refs_6_ = bf16[192,512]{1,0:T(8,128)(2,1)S(1)} collective-permute-done((bf16[192,512]{1,0:T(8,128)(2,1)S(1)}, bf16[192,512]{1,0:T(8,128)(2,1)S(1)}, u32[]{:S(2)}, u32[]{:S(2)}) %collective-permute-start.51) | collective-permute-done | bytes 196640 | tf_op jit(solution)/shard_map/ppermute | solution.py:206
  178.5 3.7 %write_pages.1 = bf16[24,128,512]{2,1,0:T(8,128)(2,1)} custom-call(s32[8,24]{1,0:T(8,128)S(1)} %get-tuple-element.154.page_ref, bf16[2,192,512]{2,1,0:T(8,128)(2,1)S(1)} %stack.19.refs_0_, bf16[2,192,512]{2,1,0:T(8,128)(2,1)S(1)} %collective-permute-done.43.refs_1_, bf16[3,192,512]{2,1,0:T(8,128)(2,1)S(1)} %stack.20.refs_2_, ...), custom_call_target="tpu_custom_call", output_to_operand_aliasing={{}: (9, {})} | custom-call | flops 1073741824 | bytes 1 | tf_op jit(solution)/shard_map/write_pages/pallas_call | solution.py:633
  (148 shorter events, 60.5 us)
Async XLA Ops:
  0.7 10.4 %collective-permute-start = (bf16[192,768]{1,0:T(8,128)(2,1)}, bf16[192,768]{1,0:T(8,128)(2,1)S(1)}, u32[]{:S(2)}, u32[]{:S(2)}) collective-permute-start(bf16[192,768]{1,0:T(8,128)(2,1)} %param.14), channel_id=1, source_target_pairs={{0,1},{1,0},{2,3},{3,2},{4,5},{5,4},{6,7},{7,6},{8,9},{9,8},{10,11... | collective-permute-start | bytes 884744 | tf_op jit(solution)/shard_map/ppermute | solution.py:214
  17.4 12.4 %collective-permute-start.4 = (bf16[208,768]{1,0:T(8,128)(2,1)S(1)}, bf16[208,768]{1,0:T(8,128)(2,1)}, u32[]{:S(2)}, u32[]{:S(2)}) collective-permute-start(bf16[208,768]{1,0:T(8,128)(2,1)S(1)} %pad_maximum_fusion.refs_0_), channel_id=1, source_target_pairs={{0,2},{2,0},{4,6},{6,4},{8,10},{10,8},{12,14},{14,12},{16,18},{18,... | collective-permute-start | bytes 958472 | tf_op jit(solution)/shard_map/ppermute | solution.py:210
  17.4 11.8 %collective-permute-start.6 = (bf16[208,768]{1,0:T(8,128)(2,1)S(1)}, bf16[208,768]{1,0:T(8,128)(2,1)S(1)}, u32[]{:S(2)}, u32[]{:S(2)}) collective-permute-start(bf16[208,768]{1,0:T(8,128)(2,1)S(1)} %pad_maximum_fusion.refs_0_), channel_id=1, source_target_pairs={{0,8},{2,10},{4,12},{6,14},{8,16},{10,18},{12,20},{14,22},{16,24},... | collective-permute-start | bytes 958472 | tf_op jit(solution)/shard_map/ppermute | solution.py:202
  29.2 13.4 %collective-permute-start.7 = (bf16[208,768]{1,0:T(8,128)(2,1)S(1)}, bf16[208,768]{1,0:T(8,128)(2,1)S(1)}, u32[]{:S(2)}, u32[]{:S(2)}) collective-permute-start(bf16[208,768]{1,0:T(8,128)(2,1)S(1)} %collective-permute-done.6.refs_0_), channel_id=1, source_target_pairs={{0,4},{2,6},{4,0},{6,2},{8,12},{10,14},{12,8},{14,10},{16,20},{18,... | collective-permute-start | bytes 958472 | tf_op jit(solution)/shard_map/ppermute | solution.py:206
  29.8 14.6 %collective-permute-start.8 = (bf16[208,768]{1,0:T(8,128)(2,1)S(1)}, bf16[208,768]{1,0:T(8,128)(2,1)S(1)}, u32[]{:S(2)}, u32[]{:S(2)}) collective-permute-start(bf16[208,768]{1,0:T(8,128)(2,1)S(1)} %collective-permute-done.6.refs_0_), channel_id=1, source_target_pairs={{0,2},{2,0},{4,6},{6,4},{8,10},{10,8},{12,14},{14,12},{16,18},{18,... | collective-permute-start | bytes 958472 | tf_op jit(solution)/shard_map/ppermute | solution.py:210
  29.8 13.1 %collective-permute-start.11 = (bf16[208,768]{1,0:T(8,128)(2,1)S(1)}, bf16[208,768]{1,0:T(8,128)(2,1)S(1)}, u32[]{:S(2)}, u32[]{:S(2)}) collective-permute-start(bf16[208,768]{1,0:T(8,128)(2,1)S(1)} %collective-permute-done.6.refs_0_), channel_id=1, source_target_pairs={{0,8},{2,10},{4,12},{6,14},{8,16},{10,18},{12,20},{14,22},{16,24},... | collective-permute-start | bytes 958472 | tf_op jit(solution)/shard_map/ppermute | solution.py:202
  36.3 15.4 %collective-permute-start.10 = (bf16[3,80,1024]{2,1,0:T(8,128)(2,1)S(1)}, bf16[3,80,1024]{2,1,0:T(8,128)(2,1)S(1)}, u32[]{:S(2)}, u32[]{:S(2)}) collective-permute-start(bf16[3,80,1024]{2,1,0:T(8,128)(2,1)S(1)} %get-tuple-element.99), channel_id=1, source_target_pairs={{0,1},{1,0},{2,3},{3,2},{4,5},{5,4},{6,7},{7,6},{8,9},{9,8},{10,11... | collective-permute-start | bytes 1474568 | tf_op jit(solution)/shard_map/ppermute | solution.py:214
  42.9 12.6 %collective-permute-start.12 = (bf16[208,768]{1,0:T(8,128)(2,1)S(1)}, bf16[208,768]{1,0:T(8,128)(2,1)S(1)}, u32[]{:S(2)}, u32[]{:S(2)}) collective-permute-start(bf16[208,768]{1,0:T(8,128)(2,1)S(1)} %collective-permute-done.11.refs_0_), channel_id=1, source_target_pairs={{0,4},{2,6},{4,0},{6,2},{8,12},{10,14},{12,8},{14,10},{16,20},{18,... | collective-permute-start | bytes 958472 | tf_op jit(solution)/shard_map/ppermute | solution.py:206
  47.4 17.2 %collective-permute-start.15 = (bf16[3,80,1024]{2,1,0:T(8,128)(2,1)S(1)}, bf16[3,80,1024]{2,1,0:T(8,128)(2,1)S(1)}, u32[]{:S(2)}, u32[]{:S(2)}) collective-permute-start(bf16[3,80,1024]{2,1,0:T(8,128)(2,1)S(1)} %get-tuple-element.108), channel_id=1, source_target_pairs={{0,1},{1,0},{2,3},{3,2},{4,5},{5,4},{6,7},{7,6},{8,9},{9,8},{10,11... | collective-permute-start | bytes 1474568 | tf_op jit(solution)/shard_map/ppermute | solution.py:214
  48.0 10.5 %collective-permute-start.22 = (bf16[208,768]{1,0:T(8,128)(2,1)S(1)}, bf16[208,768]{1,0:T(8,128)(2,1)S(1)}, u32[]{:S(2)}, u32[]{:S(2)}) collective-permute-start(bf16[208,768]{1,0:T(8,128)(2,1)S(1)} %pad_maximum_fusion.refs_0_), channel_id=1, source_target_pairs={{0,24},{2,26},{4,28},{6,30},{8,0},{10,2},{12,4},{14,6},{16,8},{18,... | collective-permute-start | bytes 958472 | tf_op jit(solution)/shard_map/ppermute | solution.py:202
  56.0 10.8 %collective-permute-start.16 = (bf16[3,80,512]{2,1,0:T(8,128)(2,1)S(1)}, bf16[3,80,512]{2,1,0:T(8,128)(2,1)S(1)}, u32[]{:S(2)}, u32[]{:S(2)}) collective-permute-start(bf16[3,80,512]{2,1,0:T(8,128)(2,1)S(1)} %activate.4.mine_ref), channel_id=1, source_target_pairs={{0,1},{1,0},{2,3},{3,2},{4,5},{5,4},{6,7},{7,6},{8,9},{9,8},{10,11... | collective-permute-start | bytes 737288 | tf_op jit(solution)/shard_map/ppermute | solution.py:214
  58.5 12.1 %collective-permute-start.23 = (bf16[208,768]{1,0:T(8,128)(2,1)S(1)}, bf16[208,768]{1,0:T(8,128)(2,1)S(1)}, u32[]{:S(2)}, u32[]{:S(2)}) collective-permute-start(bf16[208,768]{1,0:T(8,128)(2,1)S(1)} %collective-permute-done.22.refs_0_), channel_id=1, source_target_pairs={{0,4},{2,6},{4,0},{6,2},{8,12},{10,14},{12,8},{14,10},{16,20},{18,... | collective-permute-start | bytes 958472 | tf_op jit(solution)/shard_map/ppermute | solution.py:206
  63.1 21.1 %collective-permute-start.21 = (bf16[3,80,1024]{2,1,0:T(8,128)(2,1)S(1)}, bf16[3,80,1024]{2,1,0:T(8,128)(2,1)S(1)}, u32[]{:S(2)}, u32[]{:S(2)}) collective-permute-start(bf16[3,80,1024]{2,1,0:T(8,128)(2,1)S(1)} %get-tuple-element.121), channel_id=1, source_target_pairs={{0,1},{1,0},{2,3},{3,2},{4,5},{5,4},{6,7},{7,6},{8,9},{9,8},{10,11... | collective-permute-start | bytes 1474568 | tf_op jit(solution)/shard_map/ppermute | solution.py:214
  69.7 12.1 %collective-permute-start.20 = (bf16[3,80,512]{2,1,0:T(8,128)(2,1)S(1)}, bf16[3,80,512]{2,1,0:T(8,128)(2,1)S(1)}, u32[]{:S(2)}, u32[]{:S(2)}) collective-permute-start(bf16[3,80,512]{2,1,0:T(8,128)(2,1)S(1)} %activate.5.mine_ref), channel_id=1, source_target_pairs={{0,1},{1,0},{2,3},{3,2},{4,5},{5,4},{6,7},{7,6},{8,9},{9,8},{10,11... | collective-permute-start | bytes 737288 | tf_op jit(solution)/shard_map/ppermute | solution.py:214
  70.7 15.1 %collective-permute-start.25 = (bf16[208,768]{1,0:T(8,128)(2,1)S(1)}, bf16[208,768]{1,0:T(8,128)(2,1)S(1)}, u32[]{:S(2)}, u32[]{:S(2)}) collective-permute-start(bf16[208,768]{1,0:T(8,128)(2,1)S(1)} %collective-permute-done.23.refs_1_), channel_id=1, source_target_pairs={{0,2},{2,0},{4,6},{6,4},{8,10},{10,8},{12,14},{14,12},{16,18},{18,... | collective-permute-start | bytes 958472 | tf_op jit(solution)/shard_map/ppermute | solution.py:210
  70.8 16.4 %collective-permute-start.24 = (bf16[208,768]{1,0:T(8,128)(2,1)S(1)}, bf16[208,768]{1,0:T(8,128)(2,1)S(1)}, u32[]{:S(2)}, u32[]{:S(2)}) collective-permute-start(bf16[208,768]{1,0:T(8,128)(2,1)S(1)} %collective-permute-done.22.refs_0_), channel_id=1, source_target_pairs={{0,2},{2,0},{4,6},{6,4},{8,10},{10,8},{12,14},{14,12},{16,18},{18,... | collective-permute-start | bytes 958472 | tf_op jit(solution)/shard_map/ppermute | solution.py:210
  71.9 19.1 %collective-permute-start.19 = (bf16[192,768]{1,0:T(8,128)(2,1)S(1)}, bf16[192,768]{1,0:T(8,128)(2,1)S(1)}, u32[]{:S(2)}, u32[]{:S(2)}) collective-permute-start(bf16[192,768]{1,0:T(8,128)(2,1)S(1)} %get-tuple-element.116), channel_id=1, source_target_pairs={{0,4},{2,6},{4,0},{6,2},{8,12},{10,14},{12,8},{14,10},{16,20},{18,... | collective-permute-start | bytes 884744 | tf_op jit(solution)/shard_map/ppermute | solution.py:206
  85.8 8.9 %collective-permute-start.28 = (bf16[3,80,512]{2,1,0:T(8,128)(2,1)S(1)}, bf16[3,80,512]{2,1,0:T(8,128)(2,1)S(1)}, u32[]{:S(2)}, u32[]{:S(2)}) collective-permute-start(bf16[3,80,512]{2,1,0:T(8,128)(2,1)S(1)} %activate.6.mine_ref), channel_id=1, source_target_pairs={{0,1},{1,0},{2,3},{3,2},{4,5},{5,4},{6,7},{7,6},{8,9},{9,8},{10,11... | collective-permute-start | bytes 737288 | tf_op jit(solution)/shard_map/ppermute | solution.py:214
  90.2 15.1 %collective-permute-start.33 = (bf16[3,80,1024]{2,1,0:T(8,128)(2,1)S(1)}, bf16[3,80,1024]{2,1,0:T(8,128)(2,1)S(1)}, u32[]{:S(2)}, u32[]{:S(2)}) collective-permute-start(bf16[3,80,1024]{2,1,0:T(8,128)(2,1)S(1)} %get-tuple-element.142), channel_id=1, source_target_pairs={{0,1},{1,0},{2,3},{3,2},{4,5},{5,4},{6,7},{7,6},{8,9},{9,8},{10,11... | collective-permute-start | bytes 1474568 | tf_op jit(solution)/shard_map/ppermute | solution.py:214
  91.7 8.5 %collective-permute-start.29 = (bf16[192,768]{1,0:T(8,128)(2,1)S(1)}, bf16[192,768]{1,0:T(8,128)(2,1)S(1)}, u32[]{:S(2)}, u32[]{:S(2)}) collective-permute-start(bf16[192,768]{1,0:T(8,128)(2,1)S(1)} %get-tuple-element.130), channel_id=1, source_target_pairs={{0,4},{2,6},{4,0},{6,2},{8,12},{10,14},{12,8},{14,10},{16,20},{18,... | collective-permute-start | bytes 884744 | tf_op jit(solution)/shard_map/ppermute | solution.py:206
  97.0 7.6 %collective-permute-start.31 = (bf16[192,768]{1,0:T(8,128)(2,1)S(1)}, bf16[192,768]{1,0:T(8,128)(2,1)S(1)}, u32[]{:S(2)}, u32[]{:S(2)}) collective-permute-start(bf16[192,768]{1,0:T(8,128)(2,1)S(1)} %get-tuple-element.137), channel_id=1, source_target_pairs={{0,2},{2,0},{4,6},{6,4},{8,10},{10,8},{12,14},{14,12},{16,18},{18,... | collective-permute-start | bytes 884744 | tf_op jit(solution)/shard_map/ppermute | solution.py:210
  100.8 8.9 %collective-permute-start.30 = (bf16[192,768]{1,0:T(8,128)(2,1)S(1)}, bf16[192,768]{1,0:T(8,128)(2,1)S(1)}, u32[]{:S(2)}, u32[]{:S(2)}) collective-permute-start(bf16[192,768]{1,0:T(8,128)(2,1)S(1)} %add.122), channel_id=1, source_target_pairs={{0,24},{2,26},{4,28},{6,30},{8,0},{10,2},{12,4},{14,6},{16,8},{18,... | collective-permute-start | bytes 884744 | tf_op jit(solution)/shard_map/ppermute | solution.py:202
  107.6 8.0 %collective-permute-start.35 = (bf16[192,768]{1,0:T(8,128)(2,1)S(1)}, bf16[192,768]{1,0:T(8,128)(2,1)S(1)}, u32[]{:S(2)}, u32[]{:S(2)}) collective-permute-start(bf16[192,768]{1,0:T(8,128)(2,1)S(1)} %get-tuple-element.139), channel_id=1, source_target_pairs={{0,4},{2,6},{4,0},{6,2},{8,12},{10,14},{12,8},{14,10},{16,20},{18,... | collective-permute-start | bytes 884744 | tf_op jit(solution)/shard_map/ppermute | solution.py:206
  117.8 9.1 %collective-permute-start.38 = (bf16[192,768]{1,0:T(8,128)(2,1)S(1)}, bf16[192,768]{1,0:T(8,128)(2,1)S(1)}, u32[]{:S(2)}, u32[]{:S(2)}) collective-permute-start(bf16[192,768]{1,0:T(8,128)(2,1)S(1)} %get-tuple-element.151), channel_id=1, source_target_pairs={{0,4},{2,6},{4,0},{6,2},{8,12},{10,14},{12,8},{14,10},{16,20},{18,... | collective-permute-start | bytes 884744 | tf_op jit(solution)/shard_map/ppermute | solution.py:206
  119.3 22.3 %collective-permute-start.40 = (bf16[192,768]{1,0:T(8,128)(2,1)S(1)}, bf16[192,768]{1,0:T(8,128)(2,1)S(1)}, u32[]{:S(2)}, u32[]{:S(2)}) collective-permute-start(bf16[192,768]{1,0:T(8,128)(2,1)S(1)} %add.124), channel_id=1, source_target_pairs={{0,16},{2,18},{4,20},{6,22},{8,24},{10,26},{12,28},{14,30},{16,0},... | collective-permute-start | bytes 884744 | tf_op jit(solution)/shard_map/ppermute | solution.py:202
  127.5 14.1 %collective-permute-start.39 = (bf16[192,768]{1,0:T(8,128)(2,1)S(1)}, bf16[192,768]{1,0:T(8,128)(2,1)S(1)}, u32[]{:S(2)}, u32[]{:S(2)}) collective-permute-start(bf16[192,768]{1,0:T(8,128)(2,1)S(1)} %add.126), channel_id=1, source_target_pairs={{0,8},{2,10},{4,12},{6,14},{8,16},{10,18},{12,20},{14,22},{16,24},... | collective-permute-start | bytes 884744 | tf_op jit(solution)/shard_map/ppermute | solution.py:202
  141.9 8.0 %collective-permute-start.41 = (bf16[192,768]{1,0:T(8,128)(2,1)S(1)}, bf16[192,768]{1,0:T(8,128)(2,1)S(1)}, u32[]{:S(2)}, u32[]{:S(2)}) collective-permute-start(bf16[192,768]{1,0:T(8,128)(2,1)S(1)} %fusion.7.own_ref), channel_id=1, source_target_pairs={{0,1},{1,0},{2,3},{3,2},{4,5},{5,4},{6,7},{7,6},{8,9},{9,8},{10,11... | collective-permute-start | bytes 884744 | tf_op jit(solution)/shard_map/ppermute | solution.py:214
  151.5 9.9 %collective-permute-start.44 = (bf16[192,512]{1,0:T(8,128)(2,1)S(1)}, bf16[192,512]{1,0:T(8,128)(2,1)S(1)}, u32[]{:S(2)}, u32[]{:S(2)}) collective-permute-start(bf16[192,512]{1,0:T(8,128)(2,1)S(1)} %keys_values.1.refs_0_), channel_id=1, source_target_pairs={{0,8},{2,10},{4,12},{6,14},{8,16},{10,18},{12,20},{14,22},{16,24},... | collective-permute-start | bytes 589832 | tf_op jit(solution)/shard_map/ppermute | solution.py:202
  152.9 12.0 %collective-permute-start.45 = (bf16[192,512]{1,0:T(8,128)(2,1)S(1)}, bf16[192,512]{1,0:T(8,128)(2,1)S(1)}, u32[]{:S(2)}, u32[]{:S(2)}) collective-permute-start(bf16[192,512]{1,0:T(8,128)(2,1)S(1)} %keys_values.1.refs_0_), channel_id=1, source_target_pairs={{0,24},{2,26},{4,28},{6,30},{8,0},{10,2},{12,4},{14,6},{16,8},{18,... | collective-permute-start | bytes 589832 | tf_op jit(solution)/shard_map/ppermute | solution.py:202
  162.8 8.6 %collective-permute-start.48 = (bf16[192,512]{1,0:T(8,128)(2,1)S(1)}, bf16[192,512]{1,0:T(8,128)(2,1)S(1)}, u32[]{:S(2)}, u32[]{:S(2)}) collective-permute-start(bf16[192,512]{1,0:T(8,128)(2,1)S(1)} %collective-permute-done.44.refs_0_), channel_id=1, source_target_pairs={{0,8},{2,10},{4,12},{6,14},{8,16},{10,18},{12,20},{14,22},{16,24},... | collective-permute-start | bytes 589832 | tf_op jit(solution)/shard_map/ppermute | solution.py:202
  169.0 9.5 %collective-permute-start.47 = (bf16[3,192,512]{2,1,0:T(8,128)(2,1)S(1)}, bf16[3,192,512]{2,1,0:T(8,128)(2,1)S(1)}, u32[]{:S(2)}, u32[]{:S(2)}) collective-permute-start(bf16[3,192,512]{2,1,0:T(8,128)(2,1)S(1)} %stack.20.refs_2_), channel_id=1, source_target_pairs={{0,2},{2,0},{4,6},{6,4},{8,10},{10,8},{12,14},{14,12},{16,18},{18,... | collective-permute-start | bytes 1769480 | tf_op jit(solution)/shard_map/ppermute | solution.py:210
  169.1 7.9 %collective-permute-start.43 = (bf16[2,192,512]{2,1,0:T(8,128)(2,1)S(1)}, bf16[2,192,512]{2,1,0:T(8,128)(2,1)S(1)}, u32[]{:S(2)}, u32[]{:S(2)}) collective-permute-start(bf16[2,192,512]{2,1,0:T(8,128)(2,1)S(1)} %stack.19.refs_0_), channel_id=1, source_target_pairs={{0,2},{2,0},{4,6},{6,4},{8,10},{10,8},{12,14},{14,12},{16,18},{18,... | collective-permute-start | bytes 1179656 | tf_op jit(solution)/shard_map/ppermute | solution.py:210
  (34 other events, 237.9 us)
